TPU v7x, 512 devices: a whole 4x4x16 slice. The times are simulated.
512 devices in a mesh: kp: 32 (over x, y, core), ka: 16 (over z).
Axes of the slice: x: 4, y: 4, z: 16, core: 2. Of those that a mesh axis runs over, the one named last changes fastest.
Arguments:
- band_form: bfloat16 [64, 24, 2048], P('ka'), may hold values from -0.71875 to 0.71875
- interp_coef: bfloat16 [64, 128, 128], P('ka'), may hold values from -0.5 to 0.5
- screen: bfloat16 [64, 2048, 32], P('ka', 'kp'), may hold values from -0.3984375 to 0.3984375
- coulomb: float32 [2048], replicated, may hold values from 0.3 to 3
- shift_map: int32 [64, 2048], replicated, may hold values from 0 to 2047, each once within a row
- grid_order: int32 [64], replicated, may hold values from 0 to 63, each once
- energies: float32 [8192], P('ka'), may hold values from 0.18101934 to 0.543058
- initial: float32 [8192, 64], P('ka'), may hold values from -6 to 6
Outputs:
- kernel: bfloat16 [8192, 8192], P('ka', 'kp')
- subspace: float32 [8192, 64], P('ka')
All inputs are finite; a program needn't handle non-finite values.
Results may differ from a plain program's by a relative error of at most 0.02.
Values may be sent and summed in bfloat16 or wider, within the bound.
No kernel may reach another device: no remote copies, remote signals or barrier semaphores. Data moves between devices by JAX's collectives and lax.ppermute only.
A program may use at most 64 MiB of HBM per device.

v0:
```python
import jax
import jax.numpy as jnp
from jax import lax
from jax.sharding import PartitionSpec as P

NV = 8
NC = 16
STEPS = 2
GRID_Y = 8


def broadcast(block, axis, source):
    block = jnp.where(lax.axis_index(axis) == source, block, jnp.zeros_like(block))
    return lax.psum(block, axis)


def pair_block(near_form, mapped, near_coef, far_coef, screen_cols, coulomb):
    valence = (
        (near_form[:NV, None, :].astype(jnp.float32) * mapped[None, :NV, :].astype(jnp.float32))
        .reshape(NV * NV, -1)
        .astype(jnp.bfloat16)
    )
    conduction = (
        (near_form[NV:, None, :].astype(jnp.float32) * mapped[None, NV:, :].astype(jnp.float32))
        .reshape(NC * NC, -1)
        .astype(jnp.bfloat16)
    )
    scaled = (coulomb[None, :] * valence.astype(jnp.float32)).astype(jnp.bfloat16)
    direct = jnp.dot(conduction, scaled.T, preferred_element_type=jnp.float32)
    left = jnp.dot(conduction, screen_cols, preferred_element_type=jnp.float32)
    right = jnp.dot(valence, screen_cols, preferred_element_type=jnp.float32)
    direct = direct + jnp.dot(
        left, right.T, precision=lax.Precision.HIGHEST, preferred_element_type=jnp.float32
    )
    block = (
        direct.reshape(NC, NC, NV, NV)
        .transpose(2, 0, 3, 1)
        .reshape(NV * NC, NV * NC)
        .astype(jnp.bfloat16)
    )
    half = jnp.dot(block, far_coef, preferred_element_type=jnp.float32).astype(jnp.bfloat16)
    return jnp.dot(near_coef.T, half, preferred_element_type=jnp.float32).astype(jnp.bfloat16)


def transfer_table(near_cells, far_cells, grid_x):
    step_x = (near_cells[:, None] // GRID_Y - far_cells[None, :] // GRID_Y) % grid_x
    step_y = (near_cells[:, None] % GRID_Y - far_cells[None, :] % GRID_Y) % GRID_Y
    return (step_x * GRID_Y + step_y).reshape(-1)


def on_device(band_form, interp_coef, screen, coulomb, shift_map, grid_order, energies, initial):
    size_ka = lax.axis_size("ka")
    size_kp = lax.axis_size("kp")
    tile_row = lax.axis_index("ka")
    tile_col = lax.axis_index("kp")
    near_count = band_form.shape[0]
    total_points = near_count * size_ka
    far_count = total_points // size_kp
    pairs = interp_coef.shape[1]
    grid_x = total_points // GRID_Y
    source_row = tile_col * far_count // near_count
    far_offset = tile_col * far_count % near_count
    far_form, far_coef = (
        broadcast(band_form, "ka", source_row),
        broadcast(interp_coef, "ka", source_row),
    )
    far_form = lax.dynamic_slice_in_dim(far_form, far_offset, far_count, 0)
    far_coef = lax.dynamic_slice_in_dim(far_coef, far_offset, far_count, 0)
    near_ids = tile_row * near_count + jnp.arange(near_count, dtype=jnp.int32)
    far_ids = tile_col * far_count + jnp.arange(far_count, dtype=jnp.int32)
    near_cells = jnp.take(grid_order, near_ids)
    far_cells = jnp.take(grid_order, far_ids)
    transfers = transfer_table(near_cells, far_cells, grid_x)
    full_screen = lax.all_gather(screen, "kp", axis=1, tiled=True)
    shard_piece = lax.all_gather(full_screen, "ka", axis=0, tiled=True)
    piece_rows = shard_piece.shape[0]
    matches = (transfers[:, None] == jnp.arange(piece_rows, dtype=jnp.int32)[None, :]).astype(
        jnp.bfloat16
    )
    picked = jnp.einsum("pn,nge->pge", matches, shard_piece, preferred_element_type=jnp.float32)
    pair_screen = picked.astype(jnp.bfloat16)
    near_slots = jnp.repeat(jnp.arange(near_count, dtype=jnp.int32), far_count)
    far_slots = jnp.tile(jnp.arange(far_count, dtype=jnp.int32), near_count)

    def one_pair(item):
        near_slot, far_slot, transfer, screen_cols = item
        mapping = shift_map[transfer]
        mapped = jnp.take(far_form[far_slot], mapping, axis=1)
        return pair_block(
            band_form[near_slot],
            mapped,
            interp_coef[near_slot],
            far_coef[far_slot],
            screen_cols,
            coulomb,
        )

    blocks = lax.map(one_pair, (near_slots, far_slots, transfers, pair_screen))
    kernel = (
        blocks.reshape(near_count, far_count, pairs, pairs)
        .transpose(0, 2, 1, 3)
        .reshape(near_count * pairs, far_count * pairs)
    )
    vectors = initial
    for repeat in range(STEPS):
        source_vectors = broadcast(vectors.astype(jnp.bfloat16), "ka", source_row)
        far_vectors = lax.dynamic_slice_in_dim(
            source_vectors, far_offset * pairs, far_count * pairs, 0
        )
        product = jnp.dot(kernel, far_vectors, preferred_element_type=jnp.float32)
        images = energies[:, None] * vectors + lax.psum(product, "kp")
        local_correlation = jnp.dot(
            images.T, images, precision=lax.Precision.HIGHEST, preferred_element_type=jnp.float32
        )
        correlation = lax.psum(local_correlation, "ka") / (total_points * pairs)
        factor = jnp.linalg.cholesky(correlation)
        vectors = jax.scipy.linalg.solve_triangular(factor, images.T, lower=True).T
    return (kernel, vectors)


def solution(mesh):
    return jax.shard_map(
        on_device,
        mesh=mesh,
        in_specs=(
            P("ka", None, None),
            P("ka", None, None),
            P("ka", "kp", None),
            P(),
            P(),
            P(),
            P("ka"),
            P("ka", None),
        ),
        out_specs=(P("ka", "kp"), P("ka", None)),
        check_vma=False,
    )
```

profile of v0, /device:TPU:6, one launch (start us, length us, event | category | flops | bytes accessed | tf_op | source)
XLA Modules:
  0.0 1005.5 jit_solution(15382052530630806148)
XLA Ops:
  7.2 1.5 convert_select_fusion
  9.5 1.9 copy.46
  11.4 1.4 broadcast_select_fusion
  13.7 29.5 %all_gather.6 = bf16[4,2048,32]{2,0,1:T(4,128)(2,1)S(1)} all-gather(bf16[4,64,32]{2,0,1:T(4,128)(2,1)S(1)} %copy.47), channel_id=1, replica_groups=mesh['kp'=32,'ka'=16] {'kp'}, dimensions={1}, use_global_device_ids=true | all-gather | bytes 540672 | tf_op jit(solution)/shard_map/all_gather | solution.py:74
  43.2 2.2 copy.48
  49.3 114.2 %all-reduce.12.cloned.1.call-done = (bf16[4,24,2048]{1,2,0:T(8,128)(2,1)}, bf16[4,128,128]{2,1,0:T(8,128)(2,1)}, bf16[512,64]{0,1:T(8,128)(2,1)}) async-done(((bf16[4,24,2048]{1,2,0:T(8,128)(2,1)}, bf16[4,128,128]{2,1,0:T(8,128)(2,1)}, bf16[512,64]{0,1:T(8,128)(2,1)}), (bf16[4,24,2048]{1,2,0:T(8,128)(2,1)}, bf16[4,128,128]{2,1,0:T(8,128)(2,1)}, bf16[512,64]{0,1:T(8,128)(2,1)})) %all-reduce.12.cloned.1.call-update) | async-done | bytes 589840 | tf_op jit(solution)/shard_map/psum | solution.py:14
  164.3 1.3 constant_dynamic-slice_fusion.3
  165.6 101.9 %all-gather.2.cloned.1.call-done = bf16[64,2048,32]{1,2,0:T(8,128)(2,1)} async-done(((bf16[4,2048,32]{1,2,0:T(8,128)(2,1)}), bf16[64,2048,32]{1,2,0:T(8,128)(2,1)}) %all-gather.2.cloned.1.call-update) | async-done | bytes 8388624 | tf_op jit(solution)/shard_map/all_gather | solution.py:75
  267.5 12.2 %fusion.29 = bf16[8,2048,32]{1,0,2:T(8,128)(2,1)S(1)} fusion(bf16[64,2048,32]{1,2,0:T(8,128)(2,1)} %all-gather.2.cloned.1.call-done, s32[8]{0:T(128)} %fusion.54), kind=kOutput, calls=%fused_computation.46 | convolution fusion | flops 67633664 | bytes 9437216 | tf_op jit(solution)/shard_map/pn,nge->pge/dot_general | solution.py:80
  279.7 178.9 %while.10 = (s32[]{:T(128)}, bf16[8,128,128]{2,1,0:T(8,128)(2,1)S(1)}, s32[8]{0:T(128)}, bf16[4,128,128]{2,1,0:T(8,128)(2,1)}, bf16[4,24,2048]{2,1,0:T(8,128)(2,...) while((s32[]{:T(128)}, ...), condition=%wide.region_3.4_spmd, body=%wide.region_2.3_spmd.sunk | while | flops 125931528 | bytes 14897595 | solution.py:98
  279.9 1.2 dynamic_slice.77
  286.2 1.3 dynamic_slice.75
  292.6 6.2 gather_fusion
  302.2 1.2 dynamic_slice.77
  308.5 1.3 dynamic_slice.75
  314.9 6.2 gather_fusion
  324.6 1.2 dynamic_slice.77
  330.9 1.3 dynamic_slice.75
  337.3 6.2 gather_fusion
  346.9 1.2 dynamic_slice.77
  353.2 1.3 dynamic_slice.75
  359.6 6.2 gather_fusion
  369.2 1.2 dynamic_slice.77
  375.5 1.3 dynamic_slice.75
  381.9 6.2 gather_fusion
  391.6 1.2 dynamic_slice.77
  397.9 1.3 dynamic_slice.75
  404.3 6.2 gather_fusion
  413.9 1.2 dynamic_slice.77
  420.2 1.3 dynamic_slice.75
  426.6 6.2 gather_fusion
  442.6 1.3 dynamic_slice.75
  448.9 6.2 gather_fusion
  458.9 1.7 fusion.47
  460.7 130.7 %all-reduce.6.cloned.1.call-done = f32[512,64]{0,1:T(8,128)} async-done(((f32[512,64]{0,1:T(8,128)}), f32[512,64]{0,1:T(8,128)}) %all-reduce.6.cloned.1.call-update) | async-done | bytes 131088 | tf_op jit(solution)/shard_map/psum | solution.py:111
  591.3 1.2 fusion.35
  592.6 56.9 %psum.60 = f32[64,64]{0,1:T(8,128)S(1)} all-reduce(f32[64,64]{0,1:T(8,128)S(1)} %fusion.35), channel_id=1, replica_groups=mesh['kp'=32,'ka'=16] {'ka'}, use_global_device_ids=true, to_apply=%region_6.7 | all-reduce | flops 4096 | bytes 32768 | tf_op jit(solution)/shard_map/psum | solution.py:115
  649.6 5.8 cholesky.44
  656.8 4.9 custom-call.6
  661.7 1.2 fusion.33
  663.6 131.0 %all-reduce.8.cloned.1.call-done = bf16[512,64]{0,1:T(8,128)(2,1)} async-done(((bf16[512,64]{0,1:T(8,128)(2,1)}), bf16[512,64]{0,1:T(8,128)(2,1)}) %all-reduce.8.cloned.1.call-update) | async-done | bytes 65552 | tf_op jit(solution)/shard_map/psum | solution.py:14
  794.6 1.6 fusion.45
  796.3 130.4 %all-reduce.10.cloned.1.call-done = f32[512,64]{0,1:T(8,128)} async-done(((f32[512,64]{0,1:T(8,128)}), f32[512,64]{0,1:T(8,128)}) %all-reduce.10.cloned.1.call-update) | async-done | bytes 131088 | tf_op jit(solution)/shard_map/psum | solution.py:111
  926.7 1.2 fusion.36
  928.0 56.9 %psum.63 = f32[64,64]{0,1:T(8,128)S(1)} all-reduce(f32[64,64]{0,1:T(8,128)S(1)} %fusion.36), channel_id=1, replica_groups=mesh['kp'=32,'ka'=16] {'ka'}, use_global_device_ids=true, to_apply=%region_11.14 | all-reduce | flops 4096 | bytes 32768 | tf_op jit(solution)/shard_map/psum | solution.py:115
  984.9 5.8 cholesky.55
  992.1 4.9 custom-call.7
  997.0 1.9 convolution_bitcast_fusion
  (283 shorter events, 72.8 us)
Async XLA Ops:
  7.2 39.9 %copy-start = (s32[64]{0:T(128)S(1)}, s32[64]{0:T(128)}, u32[]{:S(2)}) copy-start(s32[64]{0:T(128)} %param.18) | copy-start | bytes 772
  7.2 156.3 %all-reduce.12.cloned.1.call-start = ((), (), s32[]{:S(2)}) async-start(), calls=%async_computation.4 | async-start | bytes 4587520 | tf_op jit(solution)/shard_map/psum | solution.py:14
  12.8 0.8 copy-start.7
  12.8 254.6 %all-gather.2.cloned.1.call-start = ((), (), s32[]{:S(2)}) async-start(), calls=%async_computation | async-start | bytes 8912896 | tf_op jit(solution)/shard_map/all_gather | solution.py:75
  45.5 545.9 %all-reduce.6.cloned.1.call-start = ((), (), s32[]{:S(2)}) async-start(), calls=%async_computation.1 | async-start | bytes 262144 | tf_op jit(solution)/shard_map/psum | solution.py:111
  279.7 311.6 %copy-start.4 = (f32[512,64]{0,1:T(8,128)S(1)}, f32[512,64]{0,1:T(8,128)}, u32[]{:S(2)}) copy-start(f32[512,64]{0,1:T(8,128)} %param.20) | copy-start | bytes 393220
  279.9 12.3 %copy-start.1 = (bf16[8,2048,32]{1,0,2:T(8,128)(2,1)}, bf16[8,2048,32]{1,0,2:T(8,128)(2,1)S(1)}, u32[]{:S(2)}) copy-start(bf16[8,2048,32]{1,0,2:T(8,128)(2,1)S(1)} %get-tuple-element.271) | copy-start | bytes 3145732 | tf_op jit(solution)/shard_map/while
  299.0 1.0 copy-start.5
  299.5 2.7 copy-start.2
  302.2 12.3 %copy-start.1 = (bf16[8,2048,32]{1,0,2:T(8,128)(2,1)}, bf16[8,2048,32]{1,0,2:T(8,128)(2,1)S(1)}, u32[]{:S(2)}) copy-start(bf16[8,2048,32]{1,0,2:T(8,128)(2,1)S(1)} %get-tuple-element.271) | copy-start | bytes 3145732 | tf_op jit(solution)/shard_map/while
  321.3 1.0 copy-start.5
  321.8 2.7 copy-start.2
  324.6 12.3 %copy-start.1 = (bf16[8,2048,32]{1,0,2:T(8,128)(2,1)}, bf16[8,2048,32]{1,0,2:T(8,128)(2,1)S(1)}, u32[]{:S(2)}) copy-start(bf16[8,2048,32]{1,0,2:T(8,128)(2,1)S(1)} %get-tuple-element.271) | copy-start | bytes 3145732 | tf_op jit(solution)/shard_map/while
  343.6 1.0 copy-start.5
  344.2 2.7 copy-start.2
  346.9 12.3 %copy-start.1 = (bf16[8,2048,32]{1,0,2:T(8,128)(2,1)}, bf16[8,2048,32]{1,0,2:T(8,128)(2,1)S(1)}, u32[]{:S(2)}) copy-start(bf16[8,2048,32]{1,0,2:T(8,128)(2,1)S(1)} %get-tuple-element.271) | copy-start | bytes 3145732 | tf_op jit(solution)/shard_map/while
  366.0 1.0 copy-start.5
  366.5 2.7 copy-start.2
  369.2 12.3 %copy-start.1 = (bf16[8,2048,32]{1,0,2:T(8,128)(2,1)}, bf16[8,2048,32]{1,0,2:T(8,128)(2,1)S(1)}, u32[]{:S(2)}) copy-start(bf16[8,2048,32]{1,0,2:T(8,128)(2,1)S(1)} %get-tuple-element.271) | copy-start | bytes 3145732 | tf_op jit(solution)/shard_map/while
  388.3 1.0 copy-start.5
  388.8 2.7 copy-start.2
  391.6 12.3 %copy-start.1 = (bf16[8,2048,32]{1,0,2:T(8,128)(2,1)}, bf16[8,2048,32]{1,0,2:T(8,128)(2,1)S(1)}, u32[]{:S(2)}) copy-start(bf16[8,2048,32]{1,0,2:T(8,128)(2,1)S(1)} %get-tuple-element.271) | copy-start | bytes 3145732 | tf_op jit(solution)/shard_map/while
  410.7 1.0 copy-start.5
  411.2 2.7 copy-start.2
  413.9 12.3 %copy-start.1 = (bf16[8,2048,32]{1,0,2:T(8,128)(2,1)}, bf16[8,2048,32]{1,0,2:T(8,128)(2,1)S(1)}, u32[]{:S(2)}) copy-start(bf16[8,2048,32]{1,0,2:T(8,128)(2,1)S(1)} %get-tuple-element.271) | copy-start | bytes 3145732 | tf_op jit(solution)/shard_map/while
  433.0 1.0 copy-start.5
  433.5 2.7 copy-start.2
  436.2 12.3 %copy-start.1 = (bf16[8,2048,32]{1,0,2:T(8,128)(2,1)}, bf16[8,2048,32]{1,0,2:T(8,128)(2,1)S(1)}, u32[]{:S(2)}) copy-start(bf16[8,2048,32]{1,0,2:T(8,128)(2,1)S(1)} %get-tuple-element.271) | copy-start | bytes 3145732 | tf_op jit(solution)/shard_map/while
  455.3 1.0 copy-start.5
  455.9 2.7 copy-start.2
  458.6 203.1 %copy-start.6 = (f32[512]{0:T(512)S(1)}, f32[512]{0:T(512)}, u32[]{:S(2)}) copy-start(f32[512]{0:T(512)} %param.19) | copy-start | bytes 6148
  458.9 540.0 %copy-start.3 = (bf16[64,8,2,128]{3,1,2,0:T(8,128)(2,1)}, bf16[64,8,2,128]{3,1,2,0:T(8,128)(2,1)S(1)}, u32[]{:S(2)}) copy-start(bf16[64,8,2,128]{3,1,2,0:T(8,128)(2,1)S(1)} %copy.67) | copy-start | bytes 786436
  460.6 334.0 %all-reduce.8.cloned.1.call-start = ((), (), s32[]{:S(2)}) async-start(), calls=%async_computation.2 | async-start | bytes 131072 | tf_op jit(solution)/shard_map/psum | solution.py:14
  663.6 263.1 %all-reduce.10.cloned.1.call-start = ((), (), s32[]{:S(2)}) async-start(), calls=%async_computation.3 | async-start | bytes 262144 | tf_op jit(solution)/shard_map/psum | solution.py:111
Sparse Core Ops, SparseCore 0:
  13.0 150.4 all-reduce.11
  165.6 101.8 all-gather.1
  460.8 130.5 all-reduce.5
  663.7 130.8 all-reduce.7
  798.3 128.4 all-reduce.9
where the time goes:
time: 1010 us
  waiting for transfers between devices  608 us (60%)
  blocking collectives  143 us (14%)
  local copies, waits for them, and re-layouts  99.7 us (10%)
  other arithmetic  50.7 us (5%)
  loops' own time  48.2 us (5%)
  matrix products  40.9 us (4%)
  between operations  14 us (1%)
    psum x2, waiting for transfers between devices, on_device(): images = energies[:, None] * vectors + lax.psum(product, 'kp')  261 us
    psum x2, waiting for transfers between devices, broadcast(): return lax.psum(block, axis)  245 us
    psum x2, blocking collectives, on_device(): correlation = lax.psum(local_correlation, 'ka') / (total_points * pairs)  114 us
    all_gather x1, waiting for transfers between devices, on_device(): shard_piece = lax.all_gather(full_screen, 'ka', axis=0, tiled=True)  102 us
    gather x16, local copies, waits for them, and re-layouts, one_pair(): mapped = jnp.take(far_form[far_slot], mapping, axis=1)  51 us
    another operation x1, loops' own time, on_device(): blocks = lax.map(one_pair, (near_slots, far_slots, transfers, pair_screen))  48.2 us
    dynamic_slice x40, local copies, waits for them, and re-layouts, on_device(): blocks = lax.map(one_pair, (near_slots, far_slots, transfers, pair_screen))  34.1 us
    all_gather x1, blocking collectives, on_device(): full_screen = lax.all_gather(screen, 'kp', axis=1, tiled=True)  29.5 us
  transfers between devices with their start and end apart: 5, of which 5 were waited for; matrix products, arithmetic and copies ran while one was open for 1% of the time, Pallas kernels for 0%

commit v1 on v0

v1 whole, which is shorter than its diff:
```python
import jax
import jax.numpy as jnp
from jax import lax
from jax.experimental import pallas as pl
from jax.experimental.pallas import tpu as pltpu
from jax.sharding import PartitionSpec as P

NV, NC = 8, 16
GRID_Y = 8
GRID_X = 8
BF, F32 = jnp.bfloat16, jnp.float32
HIGH = lax.Precision.HIGHEST
VM = pl.BlockSpec(memory_space=pltpu.VMEM)
SM = pl.BlockSpec(memory_space=pltpu.SMEM)


def pick_kernel(t_ref, g_ref, o_ref, rolled):
    def roll_one(h, _):
        x = g_ref[h, 0:64, :].astype(F32)
        rolled[0, h] = x.astype(BF)
        for s in range(1, 4):
            rolled[s, h] = pltpu.roll(x, 32 * s, 1).astype(BF)
        return 0

    lax.fori_loop(0, 16, roll_one, 0)
    lane_block = lax.broadcasted_iota(jnp.int32, (64, 128), 1) // 32

    def dest(d, _):
        for j in range(2):
            acc = None
            for i in range(4):
                q = t_ref[(2 * d + j) * 4 + i]
                tile = rolled[(i - q) & 3, q >> 2].astype(F32)
                acc = tile if acc is None else jnp.where(lane_block == i, tile, acc)
            o_ref[d, 64 * j : 64 * j + 64, :] = acc.astype(BF)
        half = d & 1
        plane = d >> 1
        o_ref[d, 128:152, :] = g_ref[plane, pl.ds(pl.multiple_of(64 + 24 * half, 8), 24), :]
        o_ref[d, 152:160, :] = g_ref[plane, pl.ds(pl.multiple_of(112 + 8 * half, 8), 8), :]
        o_ref[d, 160:168, :] = g_ref[plane, 128:136, :]
        return 0

    lax.fori_loop(0, 32, dest, 0)


def pick(gathered, table):
    return pl.pallas_call(
        pick_kernel,
        out_shape=jax.ShapeDtypeStruct((32, 168, 128), BF),
        in_specs=[pl.BlockSpec(memory_space=pltpu.SMEM), pl.BlockSpec(memory_space=pltpu.VMEM)],
        out_specs=pl.BlockSpec(memory_space=pltpu.VMEM),
        scratch_shapes=[pltpu.VMEM((4, 16, 64, 128), BF)],
        name="pick",
    )(table, gathered)


def pair_kernel(t_ref, r_ref, near_ref, coef_ref, coul_ref, map_ref, o_ref, y_ref, far, farc, cond, val, scaled, expand):
    step = pl.program_id(0)
    j = step // 4
    i = step % 4

    @pl.when(step == 0)
    def _():
        lane = lax.broadcasted_iota(jnp.int32, (24, 128), 1)
        for m in range(16):
            lo = r_ref[2 * m, 128:152, :].astype(F32)
            hi = r_ref[2 * m + 1, 128:152, :].astype(F32)
            far[0, m] = jnp.where(lane < 64, lo, pltpu.roll(hi, 64, 1))
            far[1, m] = jnp.where(lane < 64, pltpu.roll(lo, 64, 1), hi)
        rows = r_ref[:, 152:160, :].reshape(256, 128)
        out_row = lax.broadcasted_iota(jnp.int32, (128, 256), 0)
        in_row = lax.broadcasted_iota(jnp.int32, (128, 256), 1)
        for k in range(2):
            sel = (in_row == (out_row // 4) * 8 + k * 4 + out_row % 4).astype(F32).astype(BF)
            farc[k] = jnp.dot(sel, rows, preferred_element_type=F32).astype(BF)
        row = lax.broadcasted_iota(jnp.int32, (64, 1024), 0)
        col = lax.broadcasted_iota(jnp.int32, (64, 1024), 1)
        expand[...] = (row == col // 16).astype(F32).astype(BF)

    def gather_chunk(m, _):
        idx = map_ref[0, pl.ds(m, 1), :]
        low = jnp.broadcast_to(idx & 127, (24, 128))
        high = jnp.broadcast_to(idx >> 7, (24, 128))
        acc = jnp.take_along_axis(far[j, 0], low, axis=1)
        for s in range(1, 16):
            acc = jnp.where(high == s, jnp.take_along_axis(far[j, s], low, axis=1), acc)
        cs = pl.ds(pl.multiple_of(m * 128, 128), 128)
        a = near_ref[i, :, cs].astype(F32)
        coul = coul_ref[pl.ds(m, 1), :]
        for c in range(NC):
            cond[c * 16 : c * 16 + 16, cs] = (a[8 + c : 9 + c, :] * acc[8:24, :]).astype(BF)
        for v in range(0, NV, 2):
            x = jnp.concatenate([a[v : v + 1, :] * acc[0:8, :], a[v + 1 : v + 2, :] * acc[0:8, :]], axis=0).astype(BF)
            val[v * 8 : v * 8 + 16, cs] = x
            scaled[v * 8 : v * 8 + 16, cs] = (coul * x.astype(F32)).astype(BF)
        return 0

    lax.fori_loop(0, 16, gather_chunk, 0)
    nt = (((1,), (1,)), ((), ()))
    cols = r_ref[:, pl.ds(pl.multiple_of(64 * j, 64), 64), :].reshape(2048, 128)
    left = jnp.dot(cond[...], cols, preferred_element_type=F32)
    right = jnp.dot(val[...], cols, preferred_element_type=F32)
    left = jnp.where(lax.broadcasted_iota(jnp.int32, (256, 128), 1) // 32 == i, left, 0.0)
    direct = lax.dot_general(cond[...], scaled[...], nt, preferred_element_type=F32)
    direct += lax.dot_general(left, right, nt, precision=lax.Precision.HIGHEST, preferred_element_type=F32)
    spread = jnp.dot(direct.astype(BF), expand[...], preferred_element_type=F32)
    r16 = lax.broadcasted_iota(jnp.int32, (256, 1024), 0) % 16
    c16 = lax.broadcasted_iota(jnp.int32, (256, 1024), 1) % 16
    spread = jnp.where(r16 == c16, spread, 0.0).astype(BF)
    group = (lax.broadcasted_iota(jnp.int32, (16, 256), 0) == lax.broadcasted_iota(jnp.int32, (16, 256), 1) // 16).astype(F32).astype(BF)
    wide = jnp.dot(group, spread, preferred_element_type=F32).astype(BF)
    block = jnp.concatenate([wide[:, v * 128 : v * 128 + 128] for v in range(NV)], axis=0)
    half = jnp.dot(block, farc[j], preferred_element_type=F32).astype(BF)
    tn = (((0,), (0,)), ((), ()))
    out = lax.dot_general(coef_ref[i], half, tn, preferred_element_type=F32).astype(BF)
    o_ref[pl.ds(pl.multiple_of(i * 128, 128), 128), pl.ds(pl.multiple_of(j * 128, 128), 128)] = out

    @pl.when(step == 7)
    def _():
        odd = t_ref[8] == 1
        both = r_ref[:, 160:168, :].reshape(256, 128).astype(F32)
        lane = lax.broadcasted_iota(jnp.int32, (256, 128), 1)
        other = pltpu.roll(both, 64, 1)
        first = jnp.where(lane < 64, jnp.where(odd, other, both), 0.0).astype(BF)
        second = jnp.where(lane < 64, 0.0, jnp.where(odd, both, other)).astype(BF)
        y = jnp.dot(o_ref[0:256, :], first, preferred_element_type=F32)
        y_ref[...] = y + jnp.dot(o_ref[256:512, :], second, preferred_element_type=F32)


def pair_blocks(table, received, near, coef, coulomb, shift_map):
    grid_spec = pltpu.PrefetchScalarGridSpec(
        num_scalar_prefetch=1,
        grid=(8,),
        in_specs=[
            pl.BlockSpec((32, 168, 128), lambda p, t: (0, 0, 0)),
            pl.BlockSpec((4, 24, 2048), lambda p, t: (0, 0, 0)),
            pl.BlockSpec((4, 128, 128), lambda p, t: (0, 0, 0)),
            pl.BlockSpec((16, 128), lambda p, t: (0, 0)),
            pl.BlockSpec((1, 16, 128), lambda p, t: (t[p], 0, 0)),
        ],
        out_specs=(pl.BlockSpec((512, 256), lambda p, t: (0, 0)), pl.BlockSpec((256, 128), lambda p, t: (0, 0))),
        scratch_shapes=[
            pltpu.VMEM((2, 16, 24, 128), F32),
            pltpu.VMEM((2, 128, 128), BF),
            pltpu.VMEM((256, 2048), BF),
            pltpu.VMEM((64, 2048), BF),
            pltpu.VMEM((64, 2048), BF),
            pltpu.VMEM((64, 1024), BF),
        ],
    )
    return pl.pallas_call(
        pair_kernel,
        grid_spec=grid_spec,
        out_shape=(jax.ShapeDtypeStruct((512, 256), BF), jax.ShapeDtypeStruct((256, 128), F32)),
        name="pairs",
    )(table, received, near, coef, coulomb, shift_map)


def split_kernel(x_ref, o_ref):
    lane = lax.broadcasted_iota(jnp.int32, (8, 128), 1)
    for m in range(16):
        x = x_ref[m]
        high = x.astype(BF).astype(F32)
        low = x - high
        o_ref[2 * m] = jnp.where(lane < 64, high, pltpu.roll(low, 64, 1)).astype(BF)
        o_ref[2 * m + 1] = jnp.where(lane < 64, pltpu.roll(high, 64, 1), low).astype(BF)


def split_parts(x):
    return pl.pallas_call(
        split_kernel,
        out_shape=jax.ShapeDtypeStruct((32, 8, 128), BF),
        in_specs=[VM],
        out_specs=VM,
        name="split",
    )(x)


TN = (((0,), (0,)), ((), ()))
NT = (((1,), (1,)), ((), ()))


def fold_rows(square):
    lane = lax.broadcasted_iota(jnp.int32, (32, 128), 1)
    return jnp.where(lane < 64, square[0:32], pltpu.roll(square[32:64], 64, 1))


def second_kernel(k_ref, x_ref, o_ref):
    x = x_ref[...].reshape(256, 128)
    lane = lax.broadcasted_iota(jnp.int32, (256, 128), 1)
    low = jnp.dot(k_ref[0:256, :], x, preferred_element_type=F32)
    high = jnp.dot(k_ref[256:512, :], x, preferred_element_type=F32)
    low = low + pltpu.roll(low, 64, 1)
    high = high + pltpu.roll(high, 64, 1)
    y = jnp.where(lane < 64, low, high)
    corr = lax.dot_general(x, x, TN, preferred_element_type=F32)
    corr = corr + pltpu.roll(corr, 64, 1)
    corr = fold_rows(corr[0:64] + corr[64:128])
    o_ref[:, 0:8, :] = y.reshape(32, 8, 128)
    o_ref[:, 8:9, :] = corr.reshape(32, 1, 128)


def second_product(kernel, x):
    return pl.pallas_call(
        second_kernel,
        out_shape=jax.ShapeDtypeStruct((32, 9, 128), F32),
        in_specs=[VM, VM],
        out_specs=VM,
        name="second",
    )(kernel, x)


def inverse_factor(packed, scale):
    lane = lax.broadcasted_iota(jnp.int32, (64, 128), 1)
    row = lax.broadcasted_iota(jnp.int32, (64, 128), 0)
    full = jnp.concatenate([packed, pltpu.roll(packed, 64, 1)], axis=0) * scale
    work = jnp.where(lane < 64, full, (lane - 64 == row).astype(F32))
    done = []
    tiles = [work[8 * t : 8 * t + 8] for t in range(8)]
    for j in range(64):
        t0 = j // 8
        top = jnp.broadcast_to(tiles[t0][:, j : j + 1], (8, 128))
        pivot = top[j % 8 : j % 8 + 1, :]
        r = lax.rsqrt(pivot)
        r = r * (1.5 - 0.5 * pivot * r * r)
        line = tiles[t0][j % 8 : j % 8 + 1, :] * r
        done.append(line)
        scaled = line * r
        for t in range(t0, 8):
            column = top if t == t0 else jnp.broadcast_to(tiles[t][:, j : j + 1], (8, 128))
            tiles[t] = tiles[t] - column * scaled
    return jnp.concatenate(done, axis=0)


def apply_inverse(x, inv):
    lane = lax.broadcasted_iota(jnp.int32, (64, 128), 1)
    upper = jnp.where(lane < 64, pltpu.roll(inv, 64, 1), 0.0)
    lower = jnp.where(lane < 64, 0.0, inv)
    both = jnp.concatenate([upper, lower], axis=0)
    return lax.dot_general(x, both, NT, precision=HIGH, preferred_element_type=F32)


def middle_kernel(g_ref, image_ref, corr_ref, *, scale):
    packed = g_ref[:, 8:9, :].reshape(32, 128)
    inv = inverse_factor(packed, scale)
    image = apply_inverse(g_ref[:, 0:8, :].reshape(256, 128), inv)
    image_ref[...] = image
    corr = lax.dot_general(image, image, TN, precision=HIGH, preferred_element_type=F32)
    corr = corr[0:64] + pltpu.roll(corr[64:128], 64, 1)
    corr_ref[...] = fold_rows(corr)


def middle(g, scale):
    return pl.pallas_call(
        lambda *refs: middle_kernel(*refs, scale=scale),
        out_shape=(jax.ShapeDtypeStruct((256, 128), F32), jax.ShapeDtypeStruct((32, 128), F32)),
        in_specs=[VM],
        out_specs=(VM, VM),
        name="middle",
    )(g)


def last_kernel(image_ref, corr_ref, o_ref, *, scale):
    packed = corr_ref[0]
    for m in range(1, 16):
        packed = packed + corr_ref[m]
    inv = inverse_factor(packed, scale)
    vectors = apply_inverse(image_ref[...], inv)
    o_ref[0:256, :] = vectors[:, 0:64]
    o_ref[256:512, :] = pltpu.roll(vectors, 64, 1)[:, 0:64]


def last(image, corr, scale):
    return pl.pallas_call(
        lambda *refs: last_kernel(*refs, scale=scale),
        out_shape=jax.ShapeDtypeStruct((512, 64), F32),
        in_specs=[VM, VM],
        out_specs=VM,
        name="last",
    )(image, corr)


def halves_in_lanes(rows, start):
    low = lax.dynamic_slice_in_dim(rows, start, 8, 0)
    high = lax.dynamic_slice_in_dim(rows, start + 256, 8, 0)
    return jnp.concatenate([low, high], axis=1)


def on_device(band_form, interp_coef, screen, coulomb, shift_map, grid_order, energies, initial):
    plane = lax.axis_index("ka")
    col = lax.axis_index("kp")
    cells_x, cells_y = grid_order // GRID_Y, grid_order % GRID_Y
    near_x = lax.dynamic_slice_in_dim(cells_x, 4 * plane, 4)
    near_y = lax.dynamic_slice_in_dim(cells_y, 4 * plane, 4)
    table = (near_x[None, :] - cells_x[:, None]) % GRID_X * GRID_Y + (near_y[None, :] - cells_y[:, None]) % GRID_Y
    table = table.reshape(256)

    columns = screen.transpose(1, 0, 2).reshape(64, 128)
    forms = lax.dynamic_slice_in_dim(band_form, 64 * col, 64, 2).reshape(2, 2, 24, 64).transpose(0, 2, 1, 3).reshape(48, 128)
    coefs = lax.dynamic_slice_in_dim(interp_coef, 4 * col, 4, 1).reshape(16, 128)
    starts = halves_in_lanes(initial, 8 * col)
    diagonal = halves_in_lanes(jnp.broadcast_to(energies[:, None], (512, 64)), 8 * col)
    piece = jnp.concatenate([columns, forms, coefs, starts.astype(BF)], axis=0)
    gathered = lax.all_gather(piece, "ka", axis=0, tiled=False)
    received = lax.all_to_all(pick(gathered, table), "kp", 0, 0, tiled=True)

    own = lax.dynamic_slice_in_dim(table, 8 * col, 8)
    scalars = jnp.concatenate([own, jnp.broadcast_to(col % 2, (8,)).astype(jnp.int32)])
    kernel, product = pair_blocks(
        scalars, received, band_form, interp_coef, coulomb.reshape(16, 128), shift_map.reshape(64, 16, 128)
    )
    product = lax.all_to_all(product.reshape(32, 8, 128), "kp", 0, 0, tiled=True)
    image = jnp.sum(product, axis=0) + diagonal * starts
    far = lax.all_to_all(split_parts(lax.all_gather(image, "ka", axis=0, tiled=False)), "kp", 0, 0, tiled=True)

    sums = jnp.sum(lax.all_to_all(second_product(kernel, far), "kp", 0, 0, tiled=True), axis=0)
    sums = sums + jnp.concatenate([diagonal * image, jnp.zeros((1, 128), F32)], axis=0)
    everyone = lax.all_to_all(jnp.broadcast_to(sums[None], (32, 9, 128)), "kp", 0, 0, tiled=True)
    scale = 1.0 / 8192
    image, corr = middle(everyone, scale)
    vectors = last(image, lax.all_gather(corr, "ka", axis=0, tiled=False), scale)
    return (kernel, vectors)


def solution(mesh):
    return jax.shard_map(
        on_device,
        mesh=mesh,
        in_specs=(
            P("ka", None, None),
            P("ka", None, None),
            P("ka", "kp", None),
            P(),
            P(),
            P(),
            P("ka"),
            P("ka", None),
        ),
        out_specs=(P("ka", "kp"), P("ka", None)),
        check_vma=False,
    )
```

time: 1010 us -> 248 us (0.25)
  waiting for transfers between devices: 608 us -> 29.8 us
  local copies, waits for them, and re-layouts: 99.7 us -> 8.56 us
  Pallas kernels: 0 us -> 60 us
  other arithmetic: 50.7 us -> 1.64 us
  loops' own time: 48.2 us -> 0 us
  matrix products: 40.9 us -> 0 us
  starting transfers between devices: 0.39 us -> 19.2 us
  blocking collectives: 143 us -> 126 us
  between operations: 14 us -> 0.74 us
    psum x4 -> x0, waiting for transfers between devices: 506 us -> none  [the longest x2 261 us: on_device(): images = energies[:, None] * vectors + lax.psum(product, 'kp')]
    psum x2 -> x0, blocking collectives: 114 us -> none  [on_device(): correlation = lax.psum(local_correlation, 'ka') / (total_points * pairs)]
    all_gather x1 -> x0, waiting for transfers between devices: 102 us -> none  [on_device(): shard_piece = lax.all_gather(full_screen, 'ka', axis=0, tiled=True)]
    all_gather x1 -> x3, blocking collectives: 29.5 us -> 101 us  [the longest x1 40.7 us: on_device(): gathered = lax.all_gather(piece, 'ka', axis=0, tiled=False)]
    pallas_call x0 -> x6, Pallas kernels: none -> 60 us  [the longest x1 35.6 us: pair_blocks(): pl.pallas_call(pair_kernel, grid_spec=grid_spec, out_shape=(jax.ShapeDtyp...]
    gather x18 -> x0, local copies, waits for them, and re-layouts: 52.3 us -> none  [the longest x16 51 us: one_pair(): mapped = jnp.take(far_form[far_slot], mapping, axis=1)]
    another operation x1 -> x0, loops' own time: 48.2 us -> none  [on_device(): blocks = lax.map(one_pair, (near_slots, far_slots, transfers, pair_screen))]
    dot_general x45 -> x0, matrix products: 37.8 us -> none  [the longest x1 12.2 us: on_device(): jnp.einsum('pn,nge->pge', matches, shard_piece, preferred_element_type=jn...]
  transfers between devices with their start and end apart: 5 -> 3, of which waited for: 5 -> 3; matrix products, arithmetic and copies ran while one was open for 1% -> 1% of each run, Pallas kernels for 0% -> 0%
where the time goes in v1:
time: 248 us; the launch traced here: 246 us
  blocking collectives  126 us (51%)
  Pallas kernels  60 us (24%)
  waiting for transfers between devices  29.8 us (12%)
  starting transfers between devices  19.2 us (8%)
  local copies, waits for them, and re-layouts  8.56 us (3%)
    all_gather x1, blocking collectives, on_device(): gathered = lax.all_gather(piece, 'ka', axis=0, tiled=False)  40.7 us
    pallas_call x1, Pallas kernels, pair_blocks(): pl.pallas_call(pair_kernel, grid_spec=grid_spec, out_shape=(jax.ShapeDtyp...  35.6 us
    all_gather x1, blocking collectives, on_device(): lax.all_gather(corr, 'ka', axis=0, tiled=False)  32 us
    all_gather x1, blocking collectives, on_device(): lax.all_gather(image, 'ka', axis=0, tiled=False)  28.6 us
    all_to_all x1, waiting for transfers between devices, on_device(): received = lax.all_to_all(pick(gathered, table), 'kp', 0, 0, tiled=True)  17.3 us
    all_to_all x1, blocking collectives, on_device(): lax.all_to_all(jnp.broadcast_to(sums[None], (32, 9, 128)), 'kp', 0, 0, ti...  12.6 us
    all_to_all x1, blocking collectives, on_device(): lax.all_to_all(split_parts(lax.all_gather(image, 'ka', axis=0, tiled=Fals...  12.1 us
    pallas_call x1, Pallas kernels, middle(): pl.pallas_call(lambda *refs: middle_kernel(*refs, scale=scale), out_shape...  8.33 us
  transfers between devices with their start and end apart: 3, of which 3 were waited for; matrix products, arithmetic and copies ran while one was open for 1% of the time, Pallas kernels for 0%

profile of v1, /device:TPU:6, one launch (start us, length us, event | category | flops | bytes accessed | tf_op | source)
XLA Modules:
  0.0 245.8 jit_solution(9681262454798475931)
XLA Ops:
  0.6 0.7 and_select_fusion.1
  1.3 0.1 dynamic_slice.28
  1.4 0.1 dynamic_slice.27
  1.4 0.1 broadcast_subtract_fusion
  1.5 0.1 sub.44
  1.6 0.1 sub.48
  1.8 0.9 constant_dynamic-slice_fusion.1
  2.6 0.1 copy.29
  2.7 0.1 copy.28
  2.7 0.9 constant_dynamic-slice_fusion.3
  3.6 0.1 reshape.108
  3.7 0.8 copy.26
  4.6 0.1 fusion.4
  4.6 0.7 constant_dynamic-slice_fusion.2
  5.3 40.7 %all-gather = bf16[2176,128]{1,0:T(8,128)(2,1)} all-gather(bf16[136,128]{1,0:T(8,128)(2,1)S(1)} %pad_maximum_fusion), channel_id=2, replica_groups=mesh['kp'=32,'ka'=16] {'ka'}, dimensions={0}, use_global_device_ids=true | all-gather | bytes 591872 | tf_op jit(solution)/shard_map/all_gather | solution.py:304
  46.0 0.6 fusion.5.t_ref
  46.6 4.5 %pick.1 = bf16[32,168,128]{2,1,0:T(8,128)(2,1)} custom-call(s32[256]{0:T(256)} %fusion.5.t_ref, bf16[16,136,128]{2,1,0:T(8,128)(2,1)} %bitcast.17), custom_call_target="tpu_custom_call" | custom-call | tf_op jit(solution)/shard_map/pick/pallas_call | solution.py:47
  51.1 0.0 copy-start.2
  51.1 7.7 %all-to-all-start = ((bf16[32,168,128]{2,1,0:T(8,128)(2,1)}), bf16[32,168,128]{2,1,0:T(8,128)(2,1)S(1)}, u32[]{:S(2)}, u32[]{:S(2)}) async-start(bf16[32,168,128]{2,1,0:T(8,128)(2,1)} %pick.1), calls=%async_computation | async-start | bytes 2752512 | tf_op jit(solution)/shard_map/all_to_all | solution.py:305
  58.8 0.0 copy-done.2
  58.9 0.1 dynamic_slice.29
  58.9 0.0 copy-done.1
  58.9 0.9 copy.30
  59.9 0.5 concatenate.37.t_ref
  60.4 17.3 %all-to-all-done.r_ref = bf16[32,168,128]{2,1,0:T(8,128)(2,1)S(1)} async-done(((bf16[32,168,128]{2,1,0:T(8,128)(2,1)}), bf16[32,168,128]{2,1,0:T(8,128)(2,1)S(1)}, u32[]{:S(2)}, u32[]{:S(2)}) %all-to-all-start) | async-done | bytes 1376288 | tf_op jit(solution)/shard_map/all_to_all | solution.py:305
  77.7 1.1 copy-done
  78.7 35.6 %pairs.1 = (bf16[512,256]{1,0:T(8,128)(2,1)}, f32[256,128]{1,0:T(8,128)}) custom-call(s32[16]{0:T(128)} %concatenate.37.t_ref, bf16[32,168,128]{2,1,0:T(8,128)(2,1)} %copy-done, bf16[4,24,2048]{2,1,0:T(8,128)(2,1)} %near_ref.1, bf16[4,128,128]{2,1,0:T(8,128)(2,1)} %coef_ref.1, f32[16,128]{1,0:T(8,128)} %bitcast.27, s32[64,16,128]{2,1,0:T(8,128)} %bitcast.18), custom_call_target="tpu_custom_call" | custom-call | tf_op jit(solution)/shard_map/pairs/pallas_call | solution.py:151
  114.3 5.6 %all-to-all-start.1 = ((f32[32,8,128]{2,1,0:T(8,128)}), f32[32,8,128]{2,1,0:T(8,128)S(1)}, u32[]{:S(2)}, u32[]{:S(2)}) async-start(f32[32,8,128]{2,1,0:T(8,128)} %bitcast.21), calls=%async_computation.1 | async-start | bytes 262144 | tf_op jit(solution)/shard_map/all_to_all | solution.py:312
  120.0 0.0 copy-done.3
  120.0 0.1 fusion.9
  120.1 5.8 %all-to-all-done.1 = f32[32,8,128]{2,1,0:T(8,128)S(1)} async-done(((f32[32,8,128]{2,1,0:T(8,128)}), f32[32,8,128]{2,1,0:T(8,128)S(1)}, u32[]{:S(2)}, u32[]{:S(2)}) %all-to-all-start.1) | async-done | bytes 131104 | tf_op jit(solution)/shard_map/all_to_all | solution.py:312
  125.9 0.1 broadcast_in_dim.11
  125.9 0.1 broadcast_in_dim.10
  126.0 0.1 fusion
  126.1 28.6 %all_gather.18.x_ref = f32[16,8,128]{2,1,0:T(8,128)} all-gather(f32[1,8,128]{2,1,0:T(8,128)S(1)} %fusion), channel_id=1, replica_groups=mesh['kp'=32,'ka'=16] {'ka'}, dimensions={0}, use_global_device_ids=true | all-gather | bytes 69632 | tf_op jit(solution)/shard_map/all_gather | solution.py:314
  154.7 1.6 split.1
  156.3 12.1 %all_to_all.25.x_ref = bf16[32,8,128]{2,1,0:T(8,128)(2,1)} all-to-all(bf16[32,8,128]{2,1,0:T(8,128)(2,1)} %split.1), channel_id=1, replica_groups=mesh['kp'=32,'ka'=16] {'kp'}, dimensions={0} | all-to-all | bytes 131072 | tf_op jit(solution)/shard_map/all_to_all | solution.py:314
  168.4 2.0 second.1
  170.4 5.8 %all-to-all-start.3 = ((f32[32,9,128]{2,1,0:T(8,128)}), f32[32,9,128]{2,1,0:T(8,128)S(1)}, u32[]{:S(2)}, u32[]{:S(2)}) async-start(f32[32,9,128]{2,1,0:T(8,128)} %second.1), calls=%async_computation.3 | async-start | bytes 524288 | tf_op jit(solution)/shard_map/all_to_all | solution.py:316
  176.2 0.1 broadcast_in_dim.13
  176.3 0.1 broadcast_in_dim.12
  176.4 0.1 fusion.1
  176.4 6.7 %all-to-all-done.3 = f32[32,9,128]{2,1,0:T(8,128)S(1)} async-done(((f32[32,9,128]{2,1,0:T(8,128)}), f32[32,9,128]{2,1,0:T(8,128)S(1)}, u32[]{:S(2)}, u32[]{:S(2)}) %all-to-all-start.3) | async-done | bytes 147488 | tf_op jit(solution)/shard_map/all_to_all | solution.py:316
  183.2 12.6 %all_to_all.26.refs_0_ = f32[32,9,128]{2,1,0:T(8,128)} all-to-all(f32[32,9,128]{2,1,0:T(8,128)S(1)} %broadcast_in_dim.28), channel_id=1, replica_groups=mesh['kp'=32,'ka'=16] {'kp'}, dimensions={0} | all-to-all | bytes 294912 | tf_op jit(solution)/shard_map/all_to_all | solution.py:318
  195.8 8.3 %middle.1 = (f32[256,128]{1,0:T(8,128)}, f32[32,128]{1,0:T(8,128)}) custom-call(f32[32,9,128]{2,1,0:T(8,128)} %all_to_all.26.refs_0_), custom_call_target="tpu_custom_call" | custom-call | tf_op jit(solution)/shard_map/middle/pallas_call | solution.py:254
  204.1 32.0 %all-gather.1 = f32[512,128]{1,0:T(8,128)} all-gather(f32[32,128]{1,0:T(8,128)} %get-tuple-element.9), channel_id=3, replica_groups=mesh['kp'=32,'ka'=16] {'ka'}, dimensions={0}, use_global_device_ids=true | all-gather | bytes 278528 | tf_op jit(solution)/shard_map/all_gather | solution.py:321
  236.1 8.0 %last.1 = f32[512,64]{1,0:T(8,128)} custom-call(f32[256,128]{1,0:T(8,128)} %get-tuple-element.8.refs_0_, f32[16,32,128]{2,1,0:T(8,128)} %bitcast.19), custom_call_target="tpu_custom_call" | custom-call | tf_op jit(solution)/shard_map/last/pallas_call | solution.py:274
  244.1 1.7 copy.27
  (9 shorter events, 0.1 us)
Async XLA Ops:
  51.1 7.7 %copy-start.2 = (s32[256]{0:T(256)S(1)}, s32[256]{0:T(256)}, u32[]{:S(2)}) copy-start(s32[256]{0:T(256)} %fusion.5.t_ref) | copy-start | bytes 3076
  51.1 7.8 %copy-start.1 = (s32[64,2048]{1,0:T(8,128)S(1)}, s32[64,2048]{1,0:T(8,128)}, u32[]{:S(2)}) copy-start(s32[64,2048]{1,0:T(8,128)} %param.12) | copy-start | bytes 1572868
  51.1 26.5 %all-to-all-start = ((bf16[32,168,128]{2,1,0:T(8,128)(2,1)}), bf16[32,168,128]{2,1,0:T(8,128)(2,1)S(1)}, u32[]{:S(2)}, u32[]{:S(2)}) async-start(bf16[32,168,128]{2,1,0:T(8,128)(2,1)} %pick.1), calls=%async_computation | async-start | bytes 2752512 | tf_op jit(solution)/shard_map/all_to_all | solution.py:305
  59.9 60.1 %copy-start.3 = (f32[512]{0:T(512)S(1)}, f32[512]{0:T(512)}, u32[]{:S(2)}) copy-start(f32[512]{0:T(512)} %param.14) | copy-start | bytes 6148
  77.6 1.1 copy-start
  114.3 11.5 %all-to-all-start.1 = ((f32[32,8,128]{2,1,0:T(8,128)}), f32[32,8,128]{2,1,0:T(8,128)S(1)}, u32[]{:S(2)}, u32[]{:S(2)}) async-start(f32[32,8,128]{2,1,0:T(8,128)} %bitcast.21), calls=%async_computation.1 | async-start | bytes 262144 | tf_op jit(solution)/shard_map/all_to_all | solution.py:312
  170.4 12.8 %all-to-all-start.3 = ((f32[32,9,128]{2,1,0:T(8,128)}), f32[32,9,128]{2,1,0:T(8,128)S(1)}, u32[]{:S(2)}, u32[]{:S(2)}) async-start(f32[32,9,128]{2,1,0:T(8,128)} %second.1), calls=%async_computation.3 | async-start | bytes 524288 | tf_op jit(solution)/shard_map/all_to_all | solution.py:316

commit v2 on v1

--- a/solution.py
+++ b/solution.py
@@ -95,7 +95,7 @@
             scaled[v * 8 : v * 8 + 16, cs] = (coul * x.astype(F32)).astype(BF)
         return 0
 
-    lax.fori_loop(0, 16, gather_chunk, 0)
+    lax.fori_loop(0, 16, gather_chunk, 0, unroll=4)
     nt = (((1,), (1,)), ((), ()))
     cols = r_ref[:, pl.ds(pl.multiple_of(64 * j, 64), 64), :].reshape(2048, 128)
     left = jnp.dot(cond[...], cols, preferred_element_type=F32)
@@ -132,10 +132,10 @@
         num_scalar_prefetch=1,
         grid=(8,),
         in_specs=[
-            pl.BlockSpec((32, 168, 128), lambda p, t: (0, 0, 0)),
-            pl.BlockSpec((4, 24, 2048), lambda p, t: (0, 0, 0)),
-            pl.BlockSpec((4, 128, 128), lambda p, t: (0, 0, 0)),
-            pl.BlockSpec((16, 128), lambda p, t: (0, 0)),
+            VM,
+            VM,
+            VM,
+            VM,
             pl.BlockSpec((1, 16, 128), lambda p, t: (t[p], 0, 0)),
         ],
         out_specs=(pl.BlockSpec((512, 256), lambda p, t: (0, 0)), pl.BlockSpec((256, 128), lambda p, t: (0, 0))),
@@ -232,11 +232,13 @@
     return jnp.concatenate(done, axis=0)
 
 
+def lane_halves(inv):
+    lane = lax.broadcasted_iota(jnp.int32, (64, 128), 1)
+    return jnp.where(lane < 64, pltpu.roll(inv, 64, 1), 0.0), jnp.where(lane < 64, 0.0, inv)
+
+
 def apply_inverse(x, inv):
-    lane = lax.broadcasted_iota(jnp.int32, (64, 128), 1)
-    upper = jnp.where(lane < 64, pltpu.roll(inv, 64, 1), 0.0)
-    lower = jnp.where(lane < 64, 0.0, inv)
-    both = jnp.concatenate([upper, lower], axis=0)
+    both = jnp.concatenate(lane_halves(inv), axis=0)
     return lax.dot_general(x, both, NT, precision=HIGH, preferred_element_type=F32)
 
 
@@ -265,19 +267,25 @@
     for m in range(1, 16):
         packed = packed + corr_ref[m]
     inv = inverse_factor(packed, scale)
-    vectors = apply_inverse(image_ref[...], inv)
-    o_ref[0:256, :] = vectors[:, 0:64]
-    o_ref[256:512, :] = pltpu.roll(vectors, 64, 1)[:, 0:64]
+    upper, lower = lane_halves(inv)
+    image = image_ref[...]
+    o_ref[:, 0:256] = lax.dot_general(upper, image, NT, precision=HIGH, preferred_element_type=F32)
+    o_ref[:, 256:512] = lax.dot_general(lower, image, NT, precision=HIGH, preferred_element_type=F32)
 
 
 def last(image, corr, scale):
     return pl.pallas_call(
         lambda *refs: last_kernel(*refs, scale=scale),
-        out_shape=jax.ShapeDtypeStruct((512, 64), F32),
+        out_shape=jax.ShapeDtypeStruct((64, 512), F32),
         in_specs=[VM, VM],
         out_specs=VM,
         name="last",
-    )(image, corr)
+    )(image, corr).T
+
+
+def to_all(x, axis):
+    size = lax.axis_size(axis)
+    return lax.all_to_all(jnp.broadcast_to(x[None], (size, *x.shape)), axis, 0, 0, tiled=True)
 
 
 def halves_in_lanes(rows, start):
@@ -311,14 +319,14 @@
     )
     product = lax.all_to_all(product.reshape(32, 8, 128), "kp", 0, 0, tiled=True)
     image = jnp.sum(product, axis=0) + diagonal * starts
-    far = lax.all_to_all(split_parts(lax.all_gather(image, "ka", axis=0, tiled=False)), "kp", 0, 0, tiled=True)
+    far = lax.all_to_all(split_parts(to_all(image, "ka")), "kp", 0, 0, tiled=True)
 
     sums = jnp.sum(lax.all_to_all(second_product(kernel, far), "kp", 0, 0, tiled=True), axis=0)
     sums = sums + jnp.concatenate([diagonal * image, jnp.zeros((1, 128), F32)], axis=0)
-    everyone = lax.all_to_all(jnp.broadcast_to(sums[None], (32, 9, 128)), "kp", 0, 0, tiled=True)
+    everyone = to_all(sums, "kp")
     scale = 1.0 / 8192
     image, corr = middle(everyone, scale)
-    vectors = last(image, lax.all_gather(corr, "ka", axis=0, tiled=False), scale)
+    vectors = last(image, to_all(corr, "ka"), scale)
     return (kernel, vectors)
 
 

time: 248 us -> 221 us (0.89)
  Pallas kernels: 60 us -> 52.3 us
  waiting for transfers between devices: 29.8 us -> 23 us
  blocking collectives: 126 us -> 120 us
  starting transfers between devices: 19.2 us -> 13.4 us
    all_gather x2 -> x0, blocking collectives: 60.6 us -> none  [the longest x1 32 us: on_device(): lax.all_gather(corr, 'ka', axis=0, tiled=False)]
    all_to_all x2 -> x5, blocking collectives: 24.6 us -> 79.6 us  [the longest x3 54.8 us: to_all(): lax.all_to_all(jnp.broadcast_to(x[None], (size, *x.shape)), axis, 0, 0, t...]
    pallas_call x1, Pallas kernels: 35.6 us -> 27.9 us  [pair_blocks(): pl.pallas_call(pair_kernel, grid_spec=grid_spec, out_shape=(jax.ShapeDtyp...]
    all_to_all x1 -> x0, waiting for transfers between devices: 6.72 us -> none  [on_device(): lax.all_to_all(second_product(kernel, far), 'kp', 0, 0, tiled=True)]
    all_to_all x1 -> x0, starting transfers between devices: 5.82 us -> none  [on_device(): lax.all_to_all(second_product(kernel, far), 'kp', 0, 0, tiled=True)]
  transfers between devices with their start and end apart: 3 -> 2, of which waited for: 3 -> 2; matrix products, arithmetic and copies ran while one was open for 1% -> 1% of each run, Pallas kernels for 0% -> 0%
where the time goes in v2:
time: 221 us; the launch traced here: 219 us
  blocking collectives  120 us (54%)
  Pallas kernels  52.3 us (24%)
  waiting for transfers between devices  23 us (10%)
  starting transfers between devices  13.4 us (6%)
  local copies, waits for them, and re-layouts  7.52 us (3%)
    all_to_all x3, blocking collectives, to_all(): lax.all_to_all(jnp.broadcast_to(x[None], (size, *x.shape)), axis, 0, 0, t...  54.8 us
    all_gather x1, blocking collectives, on_device(): gathered = lax.all_gather(piece, 'ka', axis=0, tiled=False)  40.7 us
    pallas_call x1, Pallas kernels, pair_blocks(): pl.pallas_call(pair_kernel, grid_spec=grid_spec, out_shape=(jax.ShapeDtyp...  27.9 us
    all_to_all x1, waiting for transfers between devices, on_device(): received = lax.all_to_all(pick(gathered, table), 'kp', 0, 0, tiled=True)  17.2 us
    all_to_all x1, blocking collectives, on_device(): lax.all_to_all(second_product(kernel, far), 'kp', 0, 0, tiled=True)  12.8 us
    all_to_all x1, blocking collectives, on_device(): lax.all_to_all(split_parts(to_all(image, 'ka')), 'kp', 0, 0, tiled=True)  12.1 us
    pallas_call x1, Pallas kernels, middle(): pl.pallas_call(lambda *refs: middle_kernel(*refs, scale=scale), out_shape...  8.34 us
    pallas_call x1, Pallas kernels, last(): pl.pallas_call(lambda *refs: last_kernel(*refs, scale=scale), out_shape=j...  7.93 us
  transfers between devices with their start and end apart: 2, of which 2 were waited for; matrix products, arithmetic and copies ran while one was open for 1% of the time, Pallas kernels for 0%

profile of v2, /device:TPU:6, one launch (start us, length us, event | category | flops | bytes accessed | tf_op | source)
XLA Modules:
  0.0 218.7 jit_solution(18151765203118140119)
XLA Ops:
  0.6 0.7 and_select_fusion.1
  1.3 0.1 dynamic_slice.28
  1.4 0.1 dynamic_slice.27
  1.4 0.1 broadcast_subtract_fusion
  1.5 0.1 sub.44
  1.6 0.1 sub.48
  1.8 0.9 constant_dynamic-slice_fusion.1
  2.6 0.1 copy.28
  2.7 0.1 copy.27
  2.7 0.9 constant_dynamic-slice_fusion.3
  3.6 0.1 reshape.77
  3.7 0.8 copy.26
  4.6 0.1 fusion.3
  4.6 0.7 constant_dynamic-slice_fusion.2
  5.3 40.7 %all-gather = bf16[2176,128]{1,0:T(8,128)(2,1)} all-gather(bf16[136,128]{1,0:T(8,128)(2,1)S(1)} %pad_maximum_fusion), channel_id=2, replica_groups=mesh['kp'=32,'ka'=16] {'ka'}, dimensions={0}, use_global_device_ids=true | all-gather | bytes 591872 | tf_op jit(solution)/shard_map/all_gather | solution.py:312
  46.0 0.6 fusion.4.t_ref
  46.6 4.5 %pick.1 = bf16[32,168,128]{2,1,0:T(8,128)(2,1)} custom-call(s32[256]{0:T(256)} %fusion.4.t_ref, bf16[16,136,128]{2,1,0:T(8,128)(2,1)} %bitcast.13), custom_call_target="tpu_custom_call" | custom-call | tf_op jit(solution)/shard_map/pick/pallas_call | solution.py:47
  51.1 0.0 copy-start.2
  51.1 0.0 copy-start.1
  51.1 7.7 %all-to-all-start = ((bf16[32,168,128]{2,1,0:T(8,128)(2,1)}), bf16[32,168,128]{2,1,0:T(8,128)(2,1)S(1)}, u32[]{:S(2)}, u32[]{:S(2)}) async-start(bf16[32,168,128]{2,1,0:T(8,128)(2,1)} %pick.1), calls=%async_computation | async-start | bytes 2752512 | tf_op jit(solution)/shard_map/all_to_all | solution.py:313
  58.9 0.0 copy-done.2
  58.9 0.1 dynamic_slice.29
  58.9 0.0 copy-done.1
  58.9 0.9 copy.29
  59.8 0.0 copy-start.3
  59.8 0.6 concatenate.27.t_ref
  60.4 17.2 %all-to-all-done.r_ref = bf16[32,168,128]{2,1,0:T(8,128)(2,1)S(1)} async-done(((bf16[32,168,128]{2,1,0:T(8,128)(2,1)}), bf16[32,168,128]{2,1,0:T(8,128)(2,1)S(1)}, u32[]{:S(2)}, u32[]{:S(2)}) %all-to-all-start) | async-done | bytes 1376288 | tf_op jit(solution)/shard_map/all_to_all | solution.py:313
  77.7 0.0 copy-start
  77.7 1.1 copy-done
  78.8 27.9 %pairs.1 = (bf16[512,256]{1,0:T(8,128)(2,1)}, f32[256,128]{1,0:T(8,128)}) custom-call(s32[16]{0:T(128)} %concatenate.27.t_ref, bf16[32,168,128]{2,1,0:T(8,128)(2,1)} %copy-done, bf16[4,24,2048]{2,1,0:T(8,128)(2,1)} %near_ref.1, bf16[4,128,128]{2,1,0:T(8,128)(2,1)} %coef_ref.1, f32[16,128]{1,0:T(8,128)} %bitcast.21, s32[64,16,128]{2,1,0:T(8,128)} %bitcast.14), custom_call_target="tpu_custom_call" | custom-call | tf_op jit(solution)/shard_map/pairs/pallas_call | solution.py:151
  106.7 5.6 %all-to-all-start.1 = ((f32[32,8,128]{2,1,0:T(8,128)}), f32[32,8,128]{2,1,0:T(8,128)S(1)}, u32[]{:S(2)}, u32[]{:S(2)}) async-start(f32[32,8,128]{2,1,0:T(8,128)} %bitcast.16), calls=%async_computation.1 | async-start | bytes 262144 | tf_op jit(solution)/shard_map/all_to_all | solution.py:320
  112.3 0.0 copy-done.3
  112.3 0.1 fusion.9
  112.4 5.8 %all-to-all-done.1 = f32[32,8,128]{2,1,0:T(8,128)S(1)} async-done(((f32[32,8,128]{2,1,0:T(8,128)}), f32[32,8,128]{2,1,0:T(8,128)S(1)}, u32[]{:S(2)}, u32[]{:S(2)}) %all-to-all-start.1) | async-done | bytes 131104 | tf_op jit(solution)/shard_map/all_to_all | solution.py:320
  118.2 0.1 concatenate.31
  118.3 0.1 concatenate.30
  118.3 0.1 fusion
  118.4 20.0 %all_to_all.35.x_ref = f32[16,8,128]{2,1,0:T(8,128)} all-to-all(f32[16,8,128]{2,1,0:T(8,128)S(1)} %broadcast_in_dim.6), channel_id=1, replica_groups=mesh['kp'=32,'ka'=16] {'ka'}, dimensions={0} | all-to-all | bytes 131072 | tf_op jit(solution)/shard_map/all_to_all | solution.py:288
  138.4 1.6 split.1
  140.0 12.1 %all_to_all.36.x_ref = bf16[32,8,128]{2,1,0:T(8,128)(2,1)} all-to-all(bf16[32,8,128]{2,1,0:T(8,128)(2,1)} %split.1), channel_id=1, replica_groups=mesh['kp'=32,'ka'=16] {'kp'}, dimensions={0} | all-to-all | bytes 131072 | tf_op jit(solution)/shard_map/all_to_all | solution.py:322
  152.1 2.0 second.1
  154.1 12.8 %all_to_all.37 = f32[32,9,128]{2,1,0:T(8,128)S(1)} all-to-all(f32[32,9,128]{2,1,0:T(8,128)} %second.1), channel_id=1, replica_groups=mesh['kp'=32,'ka'=16] {'kp'}, dimensions={0} | all-to-all | bytes 294912 | tf_op jit(solution)/shard_map/all_to_all | solution.py:324
  166.9 12.6 %all_to_all.38.refs_0_ = f32[32,9,128]{2,1,0:T(8,128)} all-to-all(f32[32,9,128]{2,1,0:T(8,128)S(1)} %broadcast_in_dim.7), channel_id=1, replica_groups=mesh['kp'=32,'ka'=16] {'kp'}, dimensions={0} | all-to-all | bytes 294912 | tf_op jit(solution)/shard_map/all_to_all | solution.py:288
  179.5 8.3 %middle.1 = (f32[256,128]{1,0:T(8,128)}, f32[32,128]{1,0:T(8,128)}) custom-call(f32[32,9,128]{2,1,0:T(8,128)} %all_to_all.38.refs_0_), custom_call_target="tpu_custom_call" | custom-call | tf_op jit(solution)/shard_map/middle/pallas_call | solution.py:256
  187.9 0.7 broadcast_in_dim.8
  188.6 22.2 %all_to_all.39.refs_1_ = f32[16,32,128]{2,1,0:T(8,128)} all-to-all(f32[16,32,128]{2,1,0:T(8,128)S(1)} %broadcast_in_dim.8), channel_id=1, replica_groups=mesh['kp'=32,'ka'=16] {'ka'}, dimensions={0} | all-to-all | bytes 524288 | tf_op jit(solution)/shard_map/all_to_all | solution.py:288
  210.8 7.9 %last.1 = f32[64,512]{1,0:T(8,128)} custom-call(f32[256,128]{1,0:T(8,128)} %get-tuple-element.8.refs_0_, f32[16,32,128]{2,1,0:T(8,128)} %all_to_all.39.refs_1_), custom_call_target="tpu_custom_call" | custom-call | tf_op jit(solution)/shard_map/last/pallas_call | solution.py:277
  (7 shorter events, 0.1 us)
Async XLA Ops:
  51.1 7.7 %copy-start.2 = (s32[256]{0:T(256)S(1)}, s32[256]{0:T(256)}, u32[]{:S(2)}) copy-start(s32[256]{0:T(256)} %fusion.4.t_ref) | copy-start | bytes 3076
  51.1 7.8 %copy-start.1 = (s32[64,2048]{1,0:T(8,128)S(1)}, s32[64,2048]{1,0:T(8,128)}, u32[]{:S(2)}) copy-start(s32[64,2048]{1,0:T(8,128)} %param.12) | copy-start | bytes 1572868
  51.1 26.5 %all-to-all-start = ((bf16[32,168,128]{2,1,0:T(8,128)(2,1)}), bf16[32,168,128]{2,1,0:T(8,128)(2,1)S(1)}, u32[]{:S(2)}, u32[]{:S(2)}) async-start(bf16[32,168,128]{2,1,0:T(8,128)(2,1)} %pick.1), calls=%async_computation | async-start | bytes 2752512 | tf_op jit(solution)/shard_map/all_to_all | solution.py:313
  59.8 52.5 %copy-start.3 = (f32[512]{0:T(512)S(1)}, f32[512]{0:T(512)}, u32[]{:S(2)}) copy-start(f32[512]{0:T(512)} %param.14) | copy-start | bytes 6148
  77.7 1.1 copy-start
  106.7 11.5 %all-to-all-start.1 = ((f32[32,8,128]{2,1,0:T(8,128)}), f32[32,8,128]{2,1,0:T(8,128)S(1)}, u32[]{:S(2)}, u32[]{:S(2)}) async-start(f32[32,8,128]{2,1,0:T(8,128)} %bitcast.16), calls=%async_computation.1 | async-start | bytes 262144 | tf_op jit(solution)/shard_map/all_to_all | solution.py:320

commit v3 on v2

v3 whole, which is shorter than its diff:
```python
import jax
import jax.numpy as jnp
from jax import lax
from jax.experimental import pallas as pl
from jax.experimental.pallas import tpu as pltpu
from jax.sharding import PartitionSpec as P

NV, NC = 8, 16
GRID_Y = 8
GRID_X = 8
BF, F32 = jnp.bfloat16, jnp.float32
HIGH = lax.Precision.HIGHEST
VM = pl.BlockSpec(memory_space=pltpu.VMEM)
SM = pl.BlockSpec(memory_space=pltpu.SMEM)


def pick_kernel(t_ref, g_ref, o_ref, rolled):
    def roll_one(h, _):
        x = g_ref[h, 0:64, :].astype(F32)
        rolled[0, h] = x.astype(BF)
        for s in range(1, 4):
            rolled[s, h] = pltpu.roll(x, 32 * s, 1).astype(BF)
        return 0

    lax.fori_loop(0, 16, roll_one, 0)
    lane_block = lax.broadcasted_iota(jnp.int32, (64, 128), 1) // 32

    def dest(d, _):
        for j in range(2):
            acc = None
            for i in range(4):
                q = t_ref[(2 * d + j) * 4 + i]
                tile = rolled[(i - q) & 3, q >> 2].astype(F32)
                acc = tile if acc is None else jnp.where(lane_block == i, tile, acc)
            o_ref[d, 64 * j : 64 * j + 64, :] = acc.astype(BF)
        half = d & 1
        plane = d >> 1
        o_ref[d, 128:152, :] = g_ref[plane, pl.ds(pl.multiple_of(64 + 24 * half, 8), 24), :]
        o_ref[d, 152:160, :] = g_ref[plane, pl.ds(pl.multiple_of(112 + 8 * half, 8), 8), :]
        o_ref[d, 160:168, :] = g_ref[plane, 128:136, :]
        return 0

    lax.fori_loop(0, 32, dest, 0)


def pick(gathered, table):
    return pl.pallas_call(
        pick_kernel,
        out_shape=jax.ShapeDtypeStruct((32, 168, 128), BF),
        in_specs=[pl.BlockSpec(memory_space=pltpu.SMEM), pl.BlockSpec(memory_space=pltpu.VMEM)],
        out_specs=pl.BlockSpec(memory_space=pltpu.VMEM),
        scratch_shapes=[pltpu.VMEM((4, 16, 64, 128), BF)],
        name="pick",
    )(table, gathered)


NT = (((1,), (1,)), ((), ()))
TN = (((0,), (0,)), ((), ()))


def prepare_kernel(form_ref, o_ref):
    for c in range(NC):
        o_ref[0, c] = jnp.broadcast_to(form_ref[0, 8 + c : 9 + c, :].astype(F32), (16, 2048)).astype(BF)


def prepare(near):
    return pl.pallas_call(
        prepare_kernel,
        grid=(4,),
        in_specs=[pl.BlockSpec((1, 24, 2048), lambda i: (i, 0, 0))],
        out_specs=pl.BlockSpec((1, 16, 16, 2048), lambda i: (i, 0, 0, 0)),
        out_shape=jax.ShapeDtypeStruct((4, 16, 16, 2048), BF),
        name="prepare",
    )(near)


def pair_kernel(t_ref, r_ref, near_ref, wide_ref, coef_ref, coul_ref, map_ref, o_ref, send_ref, far, farc, nearc, cols, cond, val, scaled, acc, right, kt):
    lane24 = lax.broadcasted_iota(jnp.int32, (24, 128), 1)
    for m in range(16):
        lo = r_ref[2 * m, 128:152, :].astype(F32)
        hi = r_ref[2 * m + 1, 128:152, :].astype(F32)
        at = (slice(24 * (m // 2), 24 * (m // 2) + 24), slice(128 * (m % 2), 128 * (m % 2) + 128))
        far[(0, *at)] = jnp.where(lane24 < 64, lo, pltpu.roll(hi, 64, 1)).astype(BF)
        far[(1, *at)] = jnp.where(lane24 < 64, pltpu.roll(lo, 64, 1), hi).astype(BF)
    rows = r_ref[:, 152:160, :].reshape(256, 128)
    out_row = lax.broadcasted_iota(jnp.int32, (128, 256), 0)
    in_row = lax.broadcasted_iota(jnp.int32, (128, 256), 1)
    for k in range(2):
        sel = (in_row == (out_row // 4) * 8 + k * 4 + out_row % 4).astype(F32).astype(BF)
        farc[k] = jnp.dot(sel, rows, preferred_element_type=F32).astype(BF)
        cols[k] = r_ref[:, 64 * k : 64 * k + 64, :].reshape(2048, 128).astype(F32).T.astype(BF)
    old = lax.broadcasted_iota(jnp.int32, (128, 128), 1)
    new = lax.broadcasted_iota(jnp.int32, (128, 128), 0)
    order = (old == (new % 8) * 16 + new // 8).astype(F32).astype(BF)
    for i in range(4):
        nearc[i] = lax.dot_general(coef_ref[i], order, (((0,), (1,)), ((), ())), preferred_element_type=F32).astype(BF)

    place = lax.broadcasted_iota(jnp.int32, (256, 128), 0).astype(F32).astype(BF)
    one, zero = jnp.ones((), BF), jnp.zeros((), BF)
    granule = lax.broadcasted_iota(jnp.int32, (8, 128), 1) // 16

    def finish(p):
        j = p // 4
        i = p % 4
        r_hi = right[...].astype(BF)
        r_lo = (right[...] - r_hi.astype(F32)).astype(BF)
        left = acc[64:96, :]
        l_hi = left.astype(BF)
        l_lo = (left - l_hi.astype(F32)).astype(BF)
        low = jnp.dot(r_lo, l_hi, preferred_element_type=F32) + jnp.dot(r_hi, l_lo, preferred_element_type=F32)
        direct = acc[0:64, :] + (jnp.dot(r_hi, l_hi, preferred_element_type=F32) + low)
        tiles = []
        for half in range(2):
            t = [direct[8 * v : 8 * v + 8, 128 * half : 128 * half + 128] for v in range(8)]
            for s in (1, 2, 4):
                upper = (granule & s) != 0
                n = list(t)
                for v in range(8):
                    if not v & s:
                        a, b = t[v], t[v | s]
                        n[v] = jnp.where(upper, pltpu.roll(b, 16 * s, 1), a)
                        n[v | s] = jnp.where(upper, b, pltpu.roll(a, 128 - 16 * s, 1))
                t = n
            tiles += t
        block = jnp.concatenate(tiles, axis=0).astype(BF)
        half = jnp.dot(block, farc[j], preferred_element_type=F32).astype(BF)
        out = jnp.dot(nearc[i], half, preferred_element_type=F32)
        at_i = pl.ds(pl.multiple_of(i * 128, 128), 128)
        at_j = pl.ds(pl.multiple_of(j * 128, 128), 128)
        o_ref[at_i, at_j] = out.astype(BF)
        kt[at_j, at_i] = out.T.astype(BF)

    def pair(p, _):
        finish(jnp.maximum(p - 1, 0))
        j = p // 4
        i = p % 4
        index = map_ref[t_ref[p]]
        for m in range(16):
            cs = slice(128 * m, 128 * m + 128)
            if m % 2 == 0:
                pick_low = [
                    jnp.where(place == (index[n : n + 1, :] & 255).astype(F32).astype(BF), one, zero) for n in (m, m + 1)
                ]
                both = jnp.dot(far[j], jnp.concatenate(pick_low, axis=1), preferred_element_type=F32)
            high = jnp.broadcast_to(index[m : m + 1, :] >> 8, (24, 128))
            ls = slice(128 * (m % 2), 128 * (m % 2) + 128)
            got = both[0:24, ls]
            for s in range(1, 8):
                got = jnp.where(high == s, both[24 * s : 24 * s + 24, ls], got)
            a = near_ref[i, :, cs].astype(F32)
            m_c = got[8:24, :].astype(BF)
            for c in range(NC):
                cond[16 * c : 16 * c + 16, cs] = wide_ref[i, c, :, cs] * m_c
            a_v = a[0:8, :]
            coul = coul_ref[m : m + 1, :]
            for v in range(0, NV, 2):
                x = jnp.concatenate([a_v * got[v : v + 1, :], a_v * got[v + 1 : v + 2, :]], axis=0).astype(BF)
                val[8 * v : 8 * v + 16, cs] = x
                scaled[8 * v : 8 * v + 16, cs] = (coul * x.astype(F32)).astype(BF)
        own = cols[j, pl.ds(pl.multiple_of(32 * i, 32), 32), :]
        acc[0:64, :] = lax.dot_general(scaled[...], cond[...], NT, preferred_element_type=F32)
        acc[64:96, :] = lax.dot_general(own, cond[...], NT, preferred_element_type=F32)
        right[...] = lax.dot_general(val[...], own, NT, preferred_element_type=F32)
        return 0

    lax.fori_loop(0, 8, pair, 0)
    finish(7)

    odd = t_ref[8] == 1
    both = r_ref[:, 160:168, :].reshape(256, 128).astype(F32)
    lane = lax.broadcasted_iota(jnp.int32, (256, 128), 1)
    other = pltpu.roll(both, 64, 1)
    first = jnp.where(lane < 64, jnp.where(odd, other, both), 0.0).astype(BF)
    second = jnp.where(lane < 64, 0.0, jnp.where(odd, both, other)).astype(BF)
    y = jnp.dot(o_ref[0:256, :], first, preferred_element_type=F32)
    y = y + jnp.dot(o_ref[256:512, :], second, preferred_element_type=F32)
    y_hi = y.astype(BF)
    send_ref[:, 0:8, :] = y_hi.reshape(32, 8, 128)
    send_ref[:, 8:16, :] = (y - y_hi.astype(F32)).astype(BF).reshape(32, 8, 128)
    for b in range(4):
        send_ref[:, 16 + 8 * b : 24 + 8 * b, :] = kt[:, 128 * b : 128 * b + 128].reshape(32, 8, 128)


def pair_blocks(table, received, near, wide, coef, coulomb, shift_map):
    return pl.pallas_call(
        pair_kernel,
        in_specs=[SM, VM, VM, VM, VM, VM, VM],
        out_specs=(VM, VM),
        out_shape=(jax.ShapeDtypeStruct((512, 256), BF), jax.ShapeDtypeStruct((32, 48, 128), BF)),
        scratch_shapes=[
            pltpu.VMEM((2, 192, 256), BF),
            pltpu.VMEM((2, 128, 128), BF),
            pltpu.VMEM((4, 128, 128), BF),
            pltpu.VMEM((2, 128, 2048), BF),
            pltpu.VMEM((256, 2048), BF),
            pltpu.VMEM((64, 2048), BF),
            pltpu.VMEM((64, 2048), BF),
            pltpu.VMEM((96, 256), F32),
            pltpu.VMEM((64, 32), F32),
            pltpu.VMEM((256, 512), BF),
        ],
        name="pairs",
    )(table, received, near, wide, coef, coulomb, shift_map)


def fold_rows(square):
    lane = lax.broadcasted_iota(jnp.int32, (32, 128), 1)
    return jnp.where(lane < 64, square[0:32], pltpu.roll(square[32:64], 64, 1))


def second_kernel(r_ref, x_ref, o_ref):
    lane = lax.broadcasted_iota(jnp.int32, (8, 128), 1)
    parts = []
    for m in range(16):
        x = x_ref[m]
        high = x.astype(BF).astype(F32)
        low = x - high
        parts.append(jnp.where(lane < 64, high, pltpu.roll(low, 64, 1)))
        parts.append(jnp.where(lane < 64, pltpu.roll(high, 64, 1), low))
    x = jnp.concatenate(parts, axis=0)
    xt = x.T.astype(BF)
    sums = []
    for b in range(4):
        g = jnp.dot(xt, r_ref[:, 16 + 8 * b : 24 + 8 * b, :].reshape(256, 128), preferred_element_type=F32)
        sums.append(g[0:64] + g[64:128])
    for b in range(2):
        y = jnp.concatenate([sums[b], sums[b + 2]], axis=0).T
        o_ref[16 * b : 16 * b + 16, 0:8, :] = y.reshape(16, 8, 128)
    corr = jnp.dot(xt, x.astype(BF), preferred_element_type=F32)
    corr = corr + pltpu.roll(corr, 64, 1)
    corr = fold_rows(corr[0:64] + corr[64:128])
    o_ref[:, 8:9, :] = corr.reshape(32, 1, 128)


def second_product(received, x):
    return pl.pallas_call(
        second_kernel,
        out_shape=jax.ShapeDtypeStruct((32, 9, 128), F32),
        in_specs=[VM, VM],
        out_specs=VM,
        name="second",
    )(received, x)


def inverse_factor(packed, scale):
    lane = lax.broadcasted_iota(jnp.int32, (64, 128), 1)
    row = lax.broadcasted_iota(jnp.int32, (64, 128), 0)
    full = jnp.concatenate([packed, pltpu.roll(packed, 64, 1)], axis=0) * scale
    work = jnp.where(lane < 64, full, (lane - 64 == row).astype(F32))
    done = []
    tiles = [work[8 * t : 8 * t + 8] for t in range(8)]
    for j in range(64):
        t0 = j // 8
        top = jnp.broadcast_to(tiles[t0][:, j : j + 1], (8, 128))
        pivot = top[j % 8 : j % 8 + 1, :]
        r = lax.rsqrt(pivot)
        r = r * (1.5 - 0.5 * pivot * r * r)
        line = tiles[t0][j % 8 : j % 8 + 1, :] * r
        done.append(line)
        scaled = line * r
        for t in range(t0, 8):
            column = top if t == t0 else jnp.broadcast_to(tiles[t][:, j : j + 1], (8, 128))
            tiles[t] = tiles[t] - column * scaled
    return jnp.concatenate(done, axis=0)


def lane_halves(inv):
    lane = lax.broadcasted_iota(jnp.int32, (64, 128), 1)
    return jnp.where(lane < 64, pltpu.roll(inv, 64, 1), 0.0), jnp.where(lane < 64, 0.0, inv)


def apply_inverse(x, inv):
    both = jnp.concatenate(lane_halves(inv), axis=0)
    return lax.dot_general(x, both, NT, precision=HIGH, preferred_element_type=F32)


def middle_kernel(g_ref, image_ref, corr_ref, *, scale):
    packed = g_ref[:, 8:9, :].reshape(32, 128)
    inv = inverse_factor(packed, scale)
    image = apply_inverse(g_ref[:, 0:8, :].reshape(256, 128), inv)
    image_ref[...] = image
    corr = lax.dot_general(image, image, TN, precision=HIGH, preferred_element_type=F32)
    corr = corr[0:64] + pltpu.roll(corr[64:128], 64, 1)
    corr = fold_rows(corr)
    for m in range(16):
        corr_ref[m] = corr


def middle(g, scale):
    return pl.pallas_call(
        lambda *refs: middle_kernel(*refs, scale=scale),
        out_shape=(jax.ShapeDtypeStruct((256, 128), F32), jax.ShapeDtypeStruct((16, 32, 128), F32)),
        in_specs=[VM],
        out_specs=(VM, VM),
        name="middle",
    )(g)


def last_kernel(image_ref, corr_ref, o_ref, *, scale):
    packed = corr_ref[0]
    for m in range(1, 16):
        packed = packed + corr_ref[m]
    inv = inverse_factor(packed, scale)
    upper, lower = lane_halves(inv)
    image = image_ref[...]
    o_ref[:, 0:256] = lax.dot_general(upper, image, NT, precision=HIGH, preferred_element_type=F32)
    o_ref[:, 256:512] = lax.dot_general(lower, image, NT, precision=HIGH, preferred_element_type=F32)


def last(image, corr, scale):
    return pl.pallas_call(
        lambda *refs: last_kernel(*refs, scale=scale),
        out_shape=jax.ShapeDtypeStruct((64, 512), F32),
        in_specs=[VM, VM],
        out_specs=VM,
        name="last",
    )(image, corr).T


def to_all(x, axis):
    size = lax.axis_size(axis)
    return lax.all_to_all(jnp.broadcast_to(x[None], (size, *x.shape)), axis, 0, 0, tiled=True)


def halves_in_lanes(rows, start):
    low = lax.dynamic_slice_in_dim(rows, start, 8, 0)
    high = lax.dynamic_slice_in_dim(rows, start + 256, 8, 0)
    return jnp.concatenate([low, high], axis=1)


def on_device(band_form, interp_coef, screen, coulomb, shift_map, grid_order, energies, initial):
    plane = lax.axis_index("ka")
    col = lax.axis_index("kp")
    cells_x, cells_y = grid_order // GRID_Y, grid_order % GRID_Y
    near_x = lax.dynamic_slice_in_dim(cells_x, 4 * plane, 4)
    near_y = lax.dynamic_slice_in_dim(cells_y, 4 * plane, 4)
    table = (near_x[None, :] - cells_x[:, None]) % GRID_X * GRID_Y + (near_y[None, :] - cells_y[:, None]) % GRID_Y
    table = table.reshape(256)

    columns = screen.transpose(1, 0, 2).reshape(64, 128)
    forms = lax.dynamic_slice_in_dim(band_form, 64 * col, 64, 2).reshape(2, 2, 24, 64).transpose(0, 2, 1, 3).reshape(48, 128)
    coefs = lax.dynamic_slice_in_dim(interp_coef, 4 * col, 4, 1).reshape(16, 128)
    starts = halves_in_lanes(initial, 8 * col)
    diagonal = halves_in_lanes(jnp.broadcast_to(energies[:, None], (512, 64)), 8 * col)
    piece = jnp.concatenate([columns, forms, coefs, starts.astype(BF)], axis=0)
    gathered = lax.all_gather(piece, "ka", axis=0, tiled=False)
    received = lax.all_to_all(pick(gathered, table), "kp", 0, 0, tiled=True)

    own = lax.dynamic_slice_in_dim(table, 8 * col, 8)
    scalars = jnp.concatenate([own, jnp.broadcast_to(col % 2, (8,)).astype(jnp.int32)])
    kernel, sent = pair_blocks(scalars, received, band_form, prepare(band_form), interp_coef, coulomb.reshape(16, 128), shift_map.reshape(64, 16, 128))
    sent = lax.all_to_all(sent, "kp", 0, 0, tiled=True)
    image = jnp.sum(sent[:, 0:16, :].astype(F32).reshape(64, 8, 128), axis=0) + diagonal * starts

    sums = jnp.sum(lax.all_to_all(second_product(sent, to_all(image, "ka")), "kp", 0, 0, tiled=True), axis=0)
    sums = sums + jnp.concatenate([diagonal * image, jnp.zeros((1, 128), F32)], axis=0)
    everyone = to_all(sums, "kp")
    scale = 1.0 / 8192
    image, corr = middle(everyone, scale)
    vectors = last(image, lax.all_to_all(corr, "ka", 0, 0, tiled=True), scale)
    return (kernel, vectors)


def solution(mesh):
    return jax.shard_map(
        on_device,
        mesh=mesh,
        in_specs=(
            P("ka", None, None),
            P("ka", None, None),
            P("ka", "kp", None),
            P(),
            P(),
            P(),
            P("ka"),
            P("ka", None),
        ),
        out_specs=(P("ka", "kp"), P("ka", None)),
        check_vma=False,
    )
```

time: 221 us -> 200 us (0.905)
  blocking collectives: 120 us -> 109 us
  Pallas kernels: 52.3 us -> 45 us
    all_to_all x3 -> x2, blocking collectives: 54.8 us -> 32.8 us  [to_all(): lax.all_to_all(jnp.broadcast_to(x[None], (size, *x.shape)), axis, 0, 0, t...]
    all_to_all x2, blocking collectives: 24.8 us -> 35.8 us  [the longest x1 23.1 us: on_device(): vectors = last(image, lax.all_to_all(corr, 'ka', 0, 0, tiled=True), scale)]
    pallas_call x2, Pallas kernels: 29.5 us -> 21.9 us  [the longest x1 17.9 us: pair_blocks(): pl.pallas_call(pair_kernel, in_specs=[SM, VM, VM, VM, VM, VM, VM], out_sp...]
    all_to_all x1, waiting for transfers between devices: 17.2 us -> 13.3 us  [on_device(): received = lax.all_to_all(pick(gathered, table), 'kp', 0, 0, tiled=True)]
    all_to_all x1, waiting for transfers between devices: 5.77 us -> 8 us  [on_device(): sent = lax.all_to_all(sent, 'kp', 0, 0, tiled=True)]
  transfers between devices with their start and end apart: 2 -> 2, of which waited for: 2 -> 2; matrix products, arithmetic and copies ran while one was open for 1% -> 1% of each run, Pallas kernels for 0% -> 2%
where the time goes in v3:
time: 200 us; the launch traced here: 198 us
  blocking collectives  109 us (54%)
  Pallas kernels  45 us (22%)
  waiting for transfers between devices  21.3 us (11%)
  starting transfers between devices  13.3 us (7%)
  local copies, waits for them, and re-layouts  6.7 us (3%)
    all_gather x1, blocking collectives, on_device(): gathered = lax.all_gather(piece, 'ka', axis=0, tiled=False)  40.7 us
    all_to_all x2, blocking collectives, to_all(): lax.all_to_all(jnp.broadcast_to(x[None], (size, *x.shape)), axis, 0, 0, t...  32.8 us
    all_to_all x1, blocking collectives, on_device(): vectors = last(image, lax.all_to_all(corr, 'ka', 0, 0, tiled=True), scale)  23.1 us
    pallas_call x1, Pallas kernels, pair_blocks(): pl.pallas_call(pair_kernel, in_specs=[SM, VM, VM, VM, VM, VM, VM], out_sp...  17.9 us
    all_to_all x1, waiting for transfers between devices, on_device(): received = lax.all_to_all(pick(gathered, table), 'kp', 0, 0, tiled=True)  13.3 us
    all_to_all x1, blocking collectives, on_device(): lax.all_to_all(second_product(sent, to_all(image, 'ka')), 'kp', 0, 0, til...  12.7 us
    pallas_call x1, Pallas kernels, middle(): pl.pallas_call(lambda *refs: middle_kernel(*refs, scale=scale), out_shape...  8.47 us
    all_to_all x1, waiting for transfers between devices, on_device(): sent = lax.all_to_all(sent, 'kp', 0, 0, tiled=True)  8 us
  transfers between devices with their start and end apart: 2, of which 2 were waited for; matrix products, arithmetic and copies ran while one was open for 1% of the time, Pallas kernels for 2%

profile of v3, /device:TPU:6, one launch (start us, length us, event | category | flops | bytes accessed | tf_op | source)
XLA Modules:
  0.0 197.9 jit_solution(10971738129632868942)
XLA Ops:
  0.6 0.9 constant_dynamic-slice_fusion.1
  1.5 0.1 copy.27
  1.6 0.1 copy.28
  1.6 0.8 constant_dynamic-slice_fusion.3
  2.5 0.1 reshape.79
  2.6 0.8 copy.26
  3.4 0.1 fusion.3
  3.5 0.7 constant_dynamic-slice_fusion.2
  4.2 40.7 %all-gather = bf16[2176,128]{1,0:T(8,128)(2,1)} all-gather(bf16[136,128]{1,0:T(8,128)(2,1)S(1)} %pad_maximum_fusion), channel_id=2, replica_groups=mesh['kp'=32,'ka'=16] {'ka'}, dimensions={0}, use_global_device_ids=true | all-gather | bytes 591872 | tf_op jit(solution)/shard_map/all_gather | solution.py:346
  44.9 0.7 and_select_fusion.1
  45.6 0.1 dynamic_slice.27
  45.7 0.1 dynamic_slice.28
  45.7 0.1 broadcast_subtract_fusion
  45.8 0.1 sub.44
  45.9 0.1 sub.48
  46.0 0.6 fusion.4.t_ref
  46.6 4.5 %pick.1 = bf16[32,168,128]{2,1,0:T(8,128)(2,1)} custom-call(s32[256]{0:T(256)} %fusion.4.t_ref, bf16[16,136,128]{2,1,0:T(8,128)(2,1)} %bitcast.14), custom_call_target="tpu_custom_call" | custom-call | tf_op jit(solution)/shard_map/pick/pallas_call | solution.py:47
  51.1 7.6 %all-to-all-start = ((bf16[32,168,128]{2,1,0:T(8,128)(2,1)}), bf16[32,168,128]{2,1,0:T(8,128)(2,1)S(1)}, u32[]{:S(2)}, u32[]{:S(2)}) async-start(bf16[32,168,128]{2,1,0:T(8,128)(2,1)} %pick.1), calls=%async_computation | async-start | bytes 2752512 | tf_op jit(solution)/shard_map/all_to_all | solution.py:347
  58.7 0.0 copy-start.3
  58.7 0.0 copy-start.2
  58.7 4.0 %prepare.1.wide_ref = bf16[4,16,16,2048]{3,2,1,0:T(8,128)(2,1)} custom-call(bf16[4,24,2048]{2,1,0:T(8,128)(2,1)} %near_ref.1), custom_call_target="tpu_custom_call" | custom-call | tf_op jit(solution)/shard_map/prepare/pallas_call | solution.py:67
  62.7 0.0 copy-done.3
  62.7 0.1 dynamic_slice.29
  62.8 0.0 copy-done.2
  62.8 0.9 copy.29
  63.7 0.5 concatenate.27.t_ref
  64.2 13.3 %all-to-all-done.r_ref = bf16[32,168,128]{2,1,0:T(8,128)(2,1)S(1)} async-done(((bf16[32,168,128]{2,1,0:T(8,128)(2,1)}), bf16[32,168,128]{2,1,0:T(8,128)(2,1)S(1)}, u32[]{:S(2)}, u32[]{:S(2)}) %all-to-all-start) | async-done | bytes 1376288 | tf_op jit(solution)/shard_map/all_to_all | solution.py:347
  77.5 0.0 copy-start
  77.5 1.1 copy-done
  78.6 0.0 copy-start.4
  78.6 17.9 %pairs.1 = (bf16[512,256]{1,0:T(8,128)(2,1)}, bf16[32,48,128]{2,1,0:T(8,128)(2,1)}) custom-call(s32[16]{0:T(128)} %concatenate.27.t_ref, bf16[32,168,128]{2,1,0:T(8,128)(2,1)} %copy-done, bf16[4,24,2048]{2,1,0:T(8,128)(2,1)} %near_ref.1, bf16[4,16,16,2048]{3,2,1,0:T(8,128)(2,1)} %prepare.1.wide_ref, bf16[4,128,128]{2,1,0:T(8,128)(2,1)} %coef_ref.1, ...), custom_call_target="tpu_custom_call" | custom-call | tf_op jit(solution)/shard_map/pairs/pallas_call | solution.py:185
  96.5 5.6 %all-to-all-start.1 = ((bf16[32,48,128]{2,1,0:T(8,128)(2,1)}), bf16[32,48,128]{2,1,0:T(8,128)(2,1)S(1)}, u32[]{:S(2)}, u32[]{:S(2)}) async-start(bf16[32,48,128]{2,1,0:T(8,128)(2,1)} %get-tuple-element.7), calls=%async_computation.1 | async-start | bytes 786432 | tf_op jit(solution)/shard_map/all_to_all | solution.py:352
  102.2 0.0 copy-done.4
  102.2 0.1 fusion.9
  102.3 8.0 %all-to-all-done.1.r_ref = bf16[32,48,128]{2,1,0:T(8,128)(2,1)S(1)} async-done(((bf16[32,48,128]{2,1,0:T(8,128)(2,1)}), bf16[32,48,128]{2,1,0:T(8,128)(2,1)S(1)}, u32[]{:S(2)}, u32[]{:S(2)}) %all-to-all-start.1) | async-done | bytes 393248 | tf_op jit(solution)/shard_map/all_to_all | solution.py:352
  110.3 0.0 copy-start.1
  110.3 0.1 convert_reduce_fusion
  110.3 0.1 concatenate.30
  110.4 0.1 concatenate.31
  110.5 0.1 fusion
  110.6 20.2 %all_to_all.30.x_ref = f32[16,8,128]{2,1,0:T(8,128)} all-to-all(f32[16,8,128]{2,1,0:T(8,128)S(1)} %broadcast_in_dim.4), channel_id=1, replica_groups=mesh['kp'=32,'ka'=16] {'ka'}, dimensions={0} | all-to-all | bytes 131072 | tf_op jit(solution)/shard_map/all_to_all | solution.py:322
  130.8 0.0 copy-done.1
  130.8 2.2 %second.1 = f32[32,9,128]{2,1,0:T(8,128)} custom-call(bf16[32,48,128]{2,1,0:T(8,128)(2,1)} %copy-done.1, f32[16,8,128]{2,1,0:T(8,128)} %all_to_all.30.x_ref), custom_call_target="tpu_custom_call" | custom-call | tf_op jit(solution)/shard_map/second/pallas_call | solution.py:236
  133.1 12.7 %all_to_all.31 = f32[32,9,128]{2,1,0:T(8,128)S(1)} all-to-all(f32[32,9,128]{2,1,0:T(8,128)} %second.1), channel_id=1, replica_groups=mesh['kp'=32,'ka'=16] {'kp'}, dimensions={0} | all-to-all | bytes 294912 | tf_op jit(solution)/shard_map/all_to_all | solution.py:355
  145.9 12.6 %all_to_all.32.refs_0_ = f32[32,9,128]{2,1,0:T(8,128)} all-to-all(f32[32,9,128]{2,1,0:T(8,128)S(1)} %broadcast_in_dim.5), channel_id=1, replica_groups=mesh['kp'=32,'ka'=16] {'kp'}, dimensions={0} | all-to-all | bytes 294912 | tf_op jit(solution)/shard_map/all_to_all | solution.py:322
  158.4 8.5 %middle.1 = (f32[256,128]{1,0:T(8,128)}, f32[16,32,128]{2,1,0:T(8,128)}) custom-call(f32[32,9,128]{2,1,0:T(8,128)} %all_to_all.32.refs_0_), custom_call_target="tpu_custom_call" | custom-call | tf_op jit(solution)/shard_map/middle/pallas_call | solution.py:290
  166.9 23.1 %all_to_all.33.refs_1_ = f32[16,32,128]{2,1,0:T(8,128)} all-to-all(f32[16,32,128]{2,1,0:T(8,128)} %get-tuple-element.9), channel_id=1, replica_groups=mesh['kp'=32,'ka'=16] {'ka'}, dimensions={0} | all-to-all | bytes 524288 | tf_op jit(solution)/shard_map/all_to_all | solution.py:360
  190.0 7.9 %last.1 = f32[64,512]{1,0:T(8,128)} custom-call(f32[256,128]{1,0:T(8,128)} %get-tuple-element.8.refs_0_, f32[16,32,128]{2,1,0:T(8,128)} %all_to_all.33.refs_1_), custom_call_target="tpu_custom_call" | custom-call | tf_op jit(solution)/shard_map/last/pallas_call | solution.py:311
  (7 shorter events, 0.1 us)
Async XLA Ops:
  51.1 26.4 %all-to-all-start = ((bf16[32,168,128]{2,1,0:T(8,128)(2,1)}), bf16[32,168,128]{2,1,0:T(8,128)(2,1)S(1)}, u32[]{:S(2)}, u32[]{:S(2)}) async-start(bf16[32,168,128]{2,1,0:T(8,128)(2,1)} %pick.1), calls=%async_computation | async-start | bytes 2752512 | tf_op jit(solution)/shard_map/all_to_all | solution.py:347
  58.7 4.0 %copy-start.3 = (s32[256]{0:T(256)S(1)}, s32[256]{0:T(256)}, u32[]{:S(2)}) copy-start(s32[256]{0:T(256)} %fusion.4.t_ref) | copy-start | bytes 3076
  58.7 4.1 %copy-start.2 = (s32[64,2048]{1,0:T(8,128)S(1)}, s32[64,2048]{1,0:T(8,128)}, u32[]{:S(2)}) copy-start(s32[64,2048]{1,0:T(8,128)} %param.12) | copy-start | bytes 1572868
  77.5 1.1 copy-start
  78.6 23.5 %copy-start.4 = (f32[512]{0:T(512)S(1)}, f32[512]{0:T(512)}, u32[]{:S(2)}) copy-start(f32[512]{0:T(512)} %param.14) | copy-start | bytes 6148
  96.5 13.7 %all-to-all-start.1 = ((bf16[32,48,128]{2,1,0:T(8,128)(2,1)}), bf16[32,48,128]{2,1,0:T(8,128)(2,1)S(1)}, u32[]{:S(2)}, u32[]{:S(2)}) async-start(bf16[32,48,128]{2,1,0:T(8,128)(2,1)} %get-tuple-element.7), calls=%async_computation.1 | async-start | bytes 786432 | tf_op jit(solution)/shard_map/all_to_all | solution.py:352
  110.3 20.6 %copy-start.1 = (bf16[32,48,128]{2,1,0:T(8,128)(2,1)}, bf16[32,48,128]{2,1,0:T(8,128)(2,1)S(1)}, u32[]{:S(2)}) copy-start(bf16[32,48,128]{2,1,0:T(8,128)(2,1)S(1)} %all-to-all-done.1.r_ref) | copy-start | bytes 1179652

commit v4 on v3

--- a/solution.py
+++ b/solution.py
@@ -22,7 +22,7 @@
             rolled[s, h] = pltpu.roll(x, 32 * s, 1).astype(BF)
         return 0
 
-    lax.fori_loop(0, 16, roll_one, 0)
+    lax.fori_loop(0, 16, roll_one, 0, unroll=4)
     lane_block = lax.broadcasted_iota(jnp.int32, (64, 128), 1) // 32
 
     def dest(d, _):
@@ -40,7 +40,7 @@
         o_ref[d, 160:168, :] = g_ref[plane, 128:136, :]
         return 0
 
-    lax.fori_loop(0, 32, dest, 0)
+    lax.fori_loop(0, 32, dest, 0, unroll=4)
 
 
 def pick(gathered, table):
@@ -135,6 +135,7 @@
         j = p // 4
         i = p % 4
         index = map_ref[t_ref[p]]
+        scaled[64:96, :] = cols[j, pl.ds(pl.multiple_of(32 * i, 32), 32), :]
         for m in range(16):
             cs = slice(128 * m, 128 * m + 128)
             if m % 2 == 0:
@@ -157,10 +158,12 @@
                 x = jnp.concatenate([a_v * got[v : v + 1, :], a_v * got[v + 1 : v + 2, :]], axis=0).astype(BF)
                 val[8 * v : 8 * v + 16, cs] = x
                 scaled[8 * v : 8 * v + 16, cs] = (coul * x.astype(F32)).astype(BF)
-        own = cols[j, pl.ds(pl.multiple_of(32 * i, 32), 32), :]
-        acc[0:64, :] = lax.dot_general(scaled[...], cond[...], NT, preferred_element_type=F32)
-        acc[64:96, :] = lax.dot_general(own, cond[...], NT, preferred_element_type=F32)
-        right[...] = lax.dot_general(val[...], own, NT, preferred_element_type=F32)
+            if m % 2:
+                ks = slice(128 * m - 128, 128 * m + 128)
+                part = lax.dot_general(scaled[:, ks], cond[:, ks], NT, preferred_element_type=F32)
+                total = part if m == 1 else total + part
+        acc[...] = total
+        right[...] = lax.dot_general(val[...], scaled[64:96, :], NT, preferred_element_type=F32)
         return 0
 
     lax.fori_loop(0, 8, pair, 0)
@@ -194,7 +197,7 @@
             pltpu.VMEM((2, 128, 2048), BF),
             pltpu.VMEM((256, 2048), BF),
             pltpu.VMEM((64, 2048), BF),
-            pltpu.VMEM((64, 2048), BF),
+            pltpu.VMEM((96, 2048), BF),
             pltpu.VMEM((96, 256), F32),
             pltpu.VMEM((64, 32), F32),
             pltpu.VMEM((256, 512), BF),
@@ -249,18 +252,23 @@
     work = jnp.where(lane < 64, full, (lane - 64 == row).astype(F32))
     done = []
     tiles = [work[8 * t : 8 * t + 8] for t in range(8)]
-    for j in range(64):
-        t0 = j // 8
-        top = jnp.broadcast_to(tiles[t0][:, j : j + 1], (8, 128))
-        pivot = top[j % 8 : j % 8 + 1, :]
-        r = lax.rsqrt(pivot)
-        r = r * (1.5 - 0.5 * pivot * r * r)
-        line = tiles[t0][j % 8 : j % 8 + 1, :] * r
-        done.append(line)
-        scaled = line * r
-        for t in range(t0, 8):
-            column = top if t == t0 else jnp.broadcast_to(tiles[t][:, j : j + 1], (8, 128))
-            tiles[t] = tiles[t] - column * scaled
+    for t in range(8):
+        column = {u: [jnp.broadcast_to(tiles[u][:, 8 * t + k : 8 * t + k + 1], (8, 128)) for k in range(8)] for u in range(t, 8)}
+        for k in range(8):
+            pivot = column[t][k][k : k + 1, :]
+            y = lax.rsqrt(pivot)
+            square = y * y
+            near_one = pivot * square
+            inverse = square * (2.0 - near_one)
+            line = tiles[t][k : k + 1, :]
+            done.append(line * (y * (1.5 - 0.5 * near_one)))
+            line = line * inverse
+            ahead = {m: column[t][m][k : k + 1, :] * inverse for m in range(k + 1, 8)}
+            for u in range(t, 8):
+                factor = column[u][k]
+                for m in range(k + 1, 8):
+                    column[u][m] = column[u][m] - factor * ahead[m]
+                tiles[u] = tiles[u] - factor * line
     return jnp.concatenate(done, axis=0)
 
 
@@ -346,6 +354,7 @@
     gathered = lax.all_gather(piece, "ka", axis=0, tiled=False)
     received = lax.all_to_all(pick(gathered, table), "kp", 0, 0, tiled=True)
 
+    received = pltpu.with_memory_space_constraint(received, pltpu.VMEM)
     own = lax.dynamic_slice_in_dim(table, 8 * col, 8)
     scalars = jnp.concatenate([own, jnp.broadcast_to(col % 2, (8,)).astype(jnp.int32)])
     kernel, sent = pair_blocks(scalars, received, band_form, prepare(band_form), interp_coef, coulomb.reshape(16, 128), shift_map.reshape(64, 16, 128))

time: 200 us -> 188 us (0.940)
  Pallas kernels: 45 us -> 33.8 us
    pallas_call x1, Pallas kernels: 8.47 us -> 4.48 us  [middle(): pl.pallas_call(lambda *refs: middle_kernel(*refs, scale=scale), out_shape...]
    pallas_call x1, Pallas kernels: 7.93 us -> 3.95 us  [last(): pl.pallas_call(lambda *refs: last_kernel(*refs, scale=scale), out_shape=j...]
    pallas_call x1, Pallas kernels: 17.9 us -> 15.6 us  [pair_blocks(): pl.pallas_call(pair_kernel, in_specs=[SM, VM, VM, VM, VM, VM, VM], out_sp...]
where the time goes in v4:
time: 188 us; the launch traced here: 186 us
  blocking collectives  109 us (58%)
  Pallas kernels  33.8 us (18%)
  waiting for transfers between devices  21.3 us (11%)
  starting transfers between devices  13.3 us (7%)
  local copies, waits for them, and re-layouts  5.6 us (3%)
    all_gather x1, blocking collectives, on_device(): gathered = lax.all_gather(piece, 'ka', axis=0, tiled=False)  40.7 us
    all_to_all x2, blocking collectives, to_all(): lax.all_to_all(jnp.broadcast_to(x[None], (size, *x.shape)), axis, 0, 0, t...  32.8 us
    all_to_all x1, blocking collectives, on_device(): vectors = last(image, lax.all_to_all(corr, 'ka', 0, 0, tiled=True), scale)  23.1 us
    pallas_call x1, Pallas kernels, pair_blocks(): pl.pallas_call(pair_kernel, in_specs=[SM, VM, VM, VM, VM, VM, VM], out_sp...  15.6 us
    all_to_all x1, waiting for transfers between devices, on_device(): received = lax.all_to_all(pick(gathered, table), 'kp', 0, 0, tiled=True)  13.3 us
    all_to_all x1, blocking collectives, on_device(): lax.all_to_all(second_product(sent, to_all(image, 'ka')), 'kp', 0, 0, til...  12.7 us
    all_to_all x1, waiting for transfers between devices, on_device(): sent = lax.all_to_all(sent, 'kp', 0, 0, tiled=True)  8 us
    all_to_all x1, starting transfers between devices, on_device(): received = lax.all_to_all(pick(gathered, table), 'kp', 0, 0, tiled=True)  7.61 us
  transfers between devices with their start and end apart: 2, of which 2 were waited for; matrix products, arithmetic and copies ran while one was open for 1% of the time, Pallas kernels for 2%

profile of v4, /device:TPU:6, one launch (start us, length us, event | category | flops | bytes accessed | tf_op | source)
XLA Modules:
  0.0 185.6 jit_solution(17275088696710346699)
XLA Ops:
  0.6 0.9 constant_dynamic-slice_fusion.1
  1.5 0.1 copy.27
  1.6 0.1 copy.28
  1.6 0.8 constant_dynamic-slice_fusion.3
  2.5 0.1 reshape.79
  2.6 0.8 copy.26
  3.4 0.1 fusion.3
  3.5 0.7 constant_dynamic-slice_fusion.2
  4.2 40.7 %all-gather = bf16[2176,128]{1,0:T(8,128)(2,1)} all-gather(bf16[136,128]{1,0:T(8,128)(2,1)S(1)} %pad_maximum_fusion), channel_id=2, replica_groups=mesh['kp'=32,'ka'=16] {'ka'}, dimensions={0}, use_global_device_ids=true | all-gather | bytes 591872 | tf_op jit(solution)/shard_map/all_gather | solution.py:354
  44.9 0.7 and_select_fusion.1
  45.6 0.1 dynamic_slice.27
  45.7 0.1 dynamic_slice.28
  45.7 0.1 broadcast_subtract_fusion
  45.8 0.1 sub.44
  45.9 0.1 sub.48
  46.0 0.6 fusion.4.t_ref
  46.6 3.5 %pick.1 = bf16[32,168,128]{2,1,0:T(8,128)(2,1)} custom-call(s32[256]{0:T(256)} %fusion.4.t_ref, bf16[16,136,128]{2,1,0:T(8,128)(2,1)} %bitcast.14), custom_call_target="tpu_custom_call" | custom-call | tf_op jit(solution)/shard_map/pick/pallas_call | solution.py:47
  50.1 7.6 %all-to-all-start = ((bf16[32,168,128]{2,1,0:T(8,128)(2,1)}), bf16[32,168,128]{2,1,0:T(8,128)(2,1)S(1)}, u32[]{:S(2)}, u32[]{:S(2)}) async-start(bf16[32,168,128]{2,1,0:T(8,128)(2,1)} %pick.1), calls=%async_computation | async-start | bytes 2752512 | tf_op jit(solution)/shard_map/all_to_all | solution.py:355
  57.8 0.0 copy-start.2
  57.8 0.0 copy-start.1
  57.8 4.0 %prepare.1.wide_ref = bf16[4,16,16,2048]{3,2,1,0:T(8,128)(2,1)} custom-call(bf16[4,24,2048]{2,1,0:T(8,128)(2,1)} %near_ref.1), custom_call_target="tpu_custom_call" | custom-call | tf_op jit(solution)/shard_map/prepare/pallas_call | solution.py:67
  61.8 0.0 copy-done.2
  61.8 0.1 dynamic_slice.29
  61.8 0.0 copy-done.1
  61.8 0.9 copy.29
  62.7 0.5 concatenate.27.t_ref
  63.2 13.3 %all-to-all-done.r_ref = bf16[32,168,128]{2,1,0:T(8,128)(2,1)S(1)} async-done(((bf16[32,168,128]{2,1,0:T(8,128)(2,1)}), bf16[32,168,128]{2,1,0:T(8,128)(2,1)S(1)}, u32[]{:S(2)}, u32[]{:S(2)}) %all-to-all-start) | async-done | bytes 1376288 | tf_op jit(solution)/shard_map/all_to_all | solution.py:355
  76.6 0.0 copy-start.3
  76.6 15.6 %pairs.1 = (bf16[512,256]{1,0:T(8,128)(2,1)}, bf16[32,48,128]{2,1,0:T(8,128)(2,1)}) custom-call(s32[16]{0:T(128)} %concatenate.27.t_ref, bf16[32,168,128]{2,1,0:T(8,128)(2,1)S(1)} %all-to-all-done.r_ref, bf16[4,24,2048]{2,1,0:T(8,128)(2,1)} %near_ref.1, bf16[4,16,16,2048]{3,2,1,0:T(8,128)(2,1)} %prepare.1.wide_ref, bf16[4,128,128]{2,1,0:T(8,128)(2,1)} %coef_ref.1, ...), custom_call_target="tpu_custom_call" | custom-call | tf_op jit(solution)/shard_map/pairs/pallas_call | solution.py:188
  92.1 5.7 %all-to-all-start.1 = ((bf16[32,48,128]{2,1,0:T(8,128)(2,1)}), bf16[32,48,128]{2,1,0:T(8,128)(2,1)S(1)}, u32[]{:S(2)}, u32[]{:S(2)}) async-start(bf16[32,48,128]{2,1,0:T(8,128)(2,1)} %get-tuple-element.7), calls=%async_computation.1 | async-start | bytes 786432 | tf_op jit(solution)/shard_map/all_to_all | solution.py:361
  97.8 0.0 copy-done.3
  97.8 0.1 fusion.9
  97.9 8.0 %all-to-all-done.1.r_ref = bf16[32,48,128]{2,1,0:T(8,128)(2,1)S(1)} async-done(((bf16[32,48,128]{2,1,0:T(8,128)(2,1)}), bf16[32,48,128]{2,1,0:T(8,128)(2,1)S(1)}, u32[]{:S(2)}, u32[]{:S(2)}) %all-to-all-start.1) | async-done | bytes 393248 | tf_op jit(solution)/shard_map/all_to_all | solution.py:361
  105.9 0.0 copy-start
  105.9 0.1 convert_reduce_fusion
  106.0 0.1 concatenate.30
  106.1 0.1 concatenate.31
  106.1 0.1 fusion
  106.2 20.2 %all_to_all.30.x_ref = f32[16,8,128]{2,1,0:T(8,128)} all-to-all(f32[16,8,128]{2,1,0:T(8,128)S(1)} %broadcast_in_dim.4), channel_id=1, replica_groups=mesh['kp'=32,'ka'=16] {'ka'}, dimensions={0} | all-to-all | bytes 131072 | tf_op jit(solution)/shard_map/all_to_all | solution.py:330
  126.5 0.0 copy-done
  126.5 2.2 %second.1 = f32[32,9,128]{2,1,0:T(8,128)} custom-call(bf16[32,48,128]{2,1,0:T(8,128)(2,1)} %copy-done, f32[16,8,128]{2,1,0:T(8,128)} %all_to_all.30.x_ref), custom_call_target="tpu_custom_call" | custom-call | tf_op jit(solution)/shard_map/second/pallas_call | solution.py:239
  128.7 12.7 %all_to_all.31 = f32[32,9,128]{2,1,0:T(8,128)S(1)} all-to-all(f32[32,9,128]{2,1,0:T(8,128)} %second.1), channel_id=1, replica_groups=mesh['kp'=32,'ka'=16] {'kp'}, dimensions={0} | all-to-all | bytes 294912 | tf_op jit(solution)/shard_map/all_to_all | solution.py:364
  141.5 12.6 %all_to_all.32.refs_0_ = f32[32,9,128]{2,1,0:T(8,128)} all-to-all(f32[32,9,128]{2,1,0:T(8,128)S(1)} %broadcast_in_dim.5), channel_id=1, replica_groups=mesh['kp'=32,'ka'=16] {'kp'}, dimensions={0} | all-to-all | bytes 294912 | tf_op jit(solution)/shard_map/all_to_all | solution.py:330
  154.1 4.5 %middle.1 = (f32[256,128]{1,0:T(8,128)}, f32[16,32,128]{2,1,0:T(8,128)}) custom-call(f32[32,9,128]{2,1,0:T(8,128)} %all_to_all.32.refs_0_), custom_call_target="tpu_custom_call" | custom-call | tf_op jit(solution)/shard_map/middle/pallas_call | solution.py:298
  158.5 23.1 %all_to_all.33.refs_1_ = f32[16,32,128]{2,1,0:T(8,128)} all-to-all(f32[16,32,128]{2,1,0:T(8,128)} %get-tuple-element.9), channel_id=1, replica_groups=mesh['kp'=32,'ka'=16] {'ka'}, dimensions={0} | all-to-all | bytes 524288 | tf_op jit(solution)/shard_map/all_to_all | solution.py:369
  181.7 4.0 %last.1 = f32[64,512]{1,0:T(8,128)} custom-call(f32[256,128]{1,0:T(8,128)} %get-tuple-element.8.refs_0_, f32[16,32,128]{2,1,0:T(8,128)} %all_to_all.33.refs_1_), custom_call_target="tpu_custom_call" | custom-call | tf_op jit(solution)/shard_map/last/pallas_call | solution.py:319
  (7 shorter events, 0.1 us)
Async XLA Ops:
  50.1 26.4 %all-to-all-start = ((bf16[32,168,128]{2,1,0:T(8,128)(2,1)}), bf16[32,168,128]{2,1,0:T(8,128)(2,1)S(1)}, u32[]{:S(2)}, u32[]{:S(2)}) async-start(bf16[32,168,128]{2,1,0:T(8,128)(2,1)} %pick.1), calls=%async_computation | async-start | bytes 2752512 | tf_op jit(solution)/shard_map/all_to_all | solution.py:355
  57.8 4.0 %copy-start.2 = (s32[256]{0:T(256)S(1)}, s32[256]{0:T(256)}, u32[]{:S(2)}) copy-start(s32[256]{0:T(256)} %fusion.4.t_ref) | copy-start | bytes 3076
  57.8 4.1 %copy-start.1 = (s32[64,2048]{1,0:T(8,128)S(1)}, s32[64,2048]{1,0:T(8,128)}, u32[]{:S(2)}) copy-start(s32[64,2048]{1,0:T(8,128)} %param.12) | copy-start | bytes 1572868
  76.6 21.2 %copy-start.3 = (f32[512]{0:T(512)S(1)}, f32[512]{0:T(512)}, u32[]{:S(2)}) copy-start(f32[512]{0:T(512)} %param.14) | copy-start | bytes 6148
  92.1 13.8 %all-to-all-start.1 = ((bf16[32,48,128]{2,1,0:T(8,128)(2,1)}), bf16[32,48,128]{2,1,0:T(8,128)(2,1)S(1)}, u32[]{:S(2)}, u32[]{:S(2)}) async-start(bf16[32,48,128]{2,1,0:T(8,128)(2,1)} %get-tuple-element.7), calls=%async_computation.1 | async-start | bytes 786432 | tf_op jit(solution)/shard_map/all_to_all | solution.py:361
  105.9 20.6 %copy-start = (bf16[32,48,128]{2,1,0:T(8,128)(2,1)}, bf16[32,48,128]{2,1,0:T(8,128)(2,1)S(1)}, u32[]{:S(2)}) copy-start(bf16[32,48,128]{2,1,0:T(8,128)(2,1)S(1)} %all-to-all-done.1.r_ref) | copy-start | bytes 1179652

commit v5 on v4

--- a/solution.py
+++ b/solution.py
@@ -14,6 +14,71 @@
 SM = pl.BlockSpec(memory_space=pltpu.SMEM)
 
 
+def device_at(axis):
+    return lax.axis_index(axis)
+
+
+def vmem(x):
+    return pltpu.with_memory_space_constraint(x, pltpu.VMEM)
+
+
+def share_kernel(form_ref, coef_ref, screen_ref, start_ref, energy_ref, cell_ref, cells_ref, piece_ref, first_ref, diagonal_ref, table_ref, form, coef, sems):
+    plane, col = device_at("ka"), device_at("kp")
+    odd = (col & 1) == 1
+    copies = (
+        pltpu.make_async_copy(form_ref.at[:, :, pl.ds(pl.multiple_of(128 * (col // 2), 128), 128)], form, sems.at[0]),
+        pltpu.make_async_copy(coef_ref.at[:, pl.ds(pl.multiple_of(8 * (col // 2), 8), 8), :], coef, sems.at[1]),
+    )
+    for copy in copies:
+        copy.start()
+    x, y = cells_ref[...] >> 3, cells_ref[...] & 7
+    for i in range(4):
+        cell = cell_ref[4 * plane + i]
+        table_ref[i : i + 1, :] = (((cell >> 3) - x) & 7) * 8 + (((cell & 7) - y) & 7)
+    piece_ref[0:64, :] = jnp.concatenate([screen_ref[q].astype(F32) for q in range(4)], axis=1).astype(BF)
+    block = col // 16
+    back = (128 - 8 * (col % 16)) % 128
+
+    def rows_of(parts):
+        both = jnp.concatenate([pltpu.roll(part, back, 1) for part in parts], axis=0)
+        return both.T[0:8]
+
+    first = rows_of([start_ref[:, pl.ds(pl.multiple_of(256 * h + 128 * block, 128), 128)] for h in range(2)])
+    first_ref[...] = first
+    diagonal_ref[...] = rows_of([jnp.broadcast_to(energy_ref[pl.ds(2 * h + block, 1), :], (64, 128)) for h in range(2)])
+    piece_ref[128:136, :] = first.astype(BF)
+    lane = lax.broadcasted_iota(jnp.int32, (24, 128), 1)
+    row = lax.broadcasted_iota(jnp.int32, (8, 128), 0)
+    copies[0].wait()
+    copies[1].wait()
+    for h in range(2):
+        a, b = form[2 * h].astype(F32), form[2 * h + 1].astype(F32)
+        low = jnp.where(odd, pltpu.roll(a, 64, 1), a)
+        high = jnp.where(odd, b, pltpu.roll(b, 64, 1))
+        piece_ref[64 + 24 * h : 88 + 24 * h, :] = jnp.where(lane < 64, low, high).astype(BF)
+        a, b = coef[2 * h].astype(F32), coef[2 * h + 1].astype(F32)
+        low = jnp.where(odd, pltpu.roll(a, 4, 0), a)
+        high = jnp.where(odd, b, pltpu.roll(b, 4, 0))
+        piece_ref[112 + 8 * h : 120 + 8 * h, :] = jnp.where(row < 4, low, high).astype(BF)
+
+
+def share(forms, coefs, screen, initial, energies, cells):
+    hbm = pl.BlockSpec(memory_space=pl.ANY)
+    return pl.pallas_call(
+        share_kernel,
+        in_specs=[hbm, hbm, VM, VM, VM, SM, VM],
+        out_specs=(VM, VM, VM, VM),
+        out_shape=(
+            jax.ShapeDtypeStruct((136, 128), BF),
+            jax.ShapeDtypeStruct((8, 128), F32),
+            jax.ShapeDtypeStruct((8, 128), F32),
+            jax.ShapeDtypeStruct((4, 64), jnp.int32),
+        ),
+        scratch_shapes=[pltpu.VMEM((4, 24, 128), BF), pltpu.VMEM((4, 8, 128), BF), pltpu.SemaphoreType.DMA((2,))],
+        name="share",
+    )(forms, coefs, screen, initial.T, energies.reshape(4, 128), cells, cells.reshape(1, 64))
+
+
 def pick_kernel(t_ref, g_ref, o_ref, rolled):
     def roll_one(h, _):
         x = g_ref[h, 0:64, :].astype(F32)
@@ -29,7 +94,7 @@
         for j in range(2):
             acc = None
             for i in range(4):
-                q = t_ref[(2 * d + j) * 4 + i]
+                q = t_ref[i, 2 * d + j]
                 tile = rolled[(i - q) & 3, q >> 2].astype(F32)
                 acc = tile if acc is None else jnp.where(lane_block == i, tile, acc)
             o_ref[d, 64 * j : 64 * j + 64, :] = acc.astype(BF)
@@ -70,11 +135,13 @@
         in_specs=[pl.BlockSpec((1, 24, 2048), lambda i: (i, 0, 0))],
         out_specs=pl.BlockSpec((1, 16, 16, 2048), lambda i: (i, 0, 0, 0)),
         out_shape=jax.ShapeDtypeStruct((4, 16, 16, 2048), BF),
+        compiler_params=pltpu.CompilerParams(vmem_limit_bytes=32 << 20),
         name="prepare",
     )(near)
 
 
 def pair_kernel(t_ref, r_ref, near_ref, wide_ref, coef_ref, coul_ref, map_ref, o_ref, send_ref, far, farc, nearc, cols, cond, val, scaled, acc, right, kt):
+    col = device_at("kp")
     lane24 = lax.broadcasted_iota(jnp.int32, (24, 128), 1)
     for m in range(16):
         lo = r_ref[2 * m, 128:152, :].astype(F32)
@@ -134,7 +201,7 @@
         finish(jnp.maximum(p - 1, 0))
         j = p // 4
         i = p % 4
-        index = map_ref[t_ref[p]]
+        index = map_ref[t_ref[i, 2 * col + j]]
         scaled[64:96, :] = cols[j, pl.ds(pl.multiple_of(32 * i, 32), 32), :]
         for m in range(16):
             cs = slice(128 * m, 128 * m + 128)
@@ -169,7 +236,7 @@
     lax.fori_loop(0, 8, pair, 0)
     finish(7)
 
-    odd = t_ref[8] == 1
+    odd = (col & 1) == 1
     both = r_ref[:, 160:168, :].reshape(256, 128).astype(F32)
     lane = lax.broadcasted_iota(jnp.int32, (256, 128), 1)
     other = pltpu.roll(both, 64, 1)
@@ -202,6 +269,7 @@
             pltpu.VMEM((64, 32), F32),
             pltpu.VMEM((256, 512), BF),
         ],
+        compiler_params=pltpu.CompilerParams(vmem_limit_bytes=32 << 20),
         name="pairs",
     )(table, received, near, wide, coef, coulomb, shift_map)
 
@@ -245,11 +313,43 @@
     )(received, x)
 
 
-def inverse_factor(packed, scale):
+def pack_symmetric(square):
+    lane = lax.broadcasted_iota(jnp.int32, (32, 128), 1)
+    row = lax.broadcasted_iota(jnp.int32, (32, 128), 0)
+    corner = pltpu.roll(square[32:64], 96, 1)
+    values = jnp.where(lane < row, corner, square[0:32])
+    diagonal = jnp.sum(jnp.where(lane == row, corner, 0.0), axis=0, keepdims=True)
+    values = jnp.where(lane[0:16] < 64, values[0:16], pltpu.roll(values[16:32], 64, 1))
+    high = values.astype(BF).astype(F32)
+    tail = jnp.broadcast_to(diagonal, (8, 128))
+    tail_high = tail.astype(BF).astype(F32)
+    tail = jnp.where(row[0:8] == 0, tail_high, jnp.where(row[0:8] == 1, tail - tail_high, 0.0))
+    return jnp.concatenate([high, values - high, tail], axis=0).astype(BF)
+
+
+def unpack_symmetric(parts):
+    lane = lax.broadcasted_iota(jnp.int32, (32, 128), 1)
+    row = lax.broadcasted_iota(jnp.int32, (32, 128), 0)
+    values = parts[0:16] + parts[16:32]
+    values = jnp.concatenate([values, pltpu.roll(values, 64, 1)], axis=0)
+    diagonal = jnp.broadcast_to(pltpu.roll(parts[32:40], 32, 1)[0:1] + pltpu.roll(parts[32:40], 32, 1)[1:2], (32, 128))
+    top = jnp.where(lane < row, 0.0, jnp.where(lane == row, 0.5 * values, values))
+    top = jnp.where(lane < 64, top, 0.0)
+    low = pltpu.roll(values, 32, 1)
+    low = jnp.where(lane - 32 < row, low, jnp.where(lane - 32 == row, 0.5 * diagonal, 0.0))
+    low = jnp.where(lane < 32, 0.0, low)
+    half = jnp.concatenate([top, low, jnp.zeros((64, 128), F32)], axis=0)
+    return half[0:64] + half.T[0:64]
+
+
+def unfold_rows(packed):
+    return jnp.concatenate([packed, pltpu.roll(packed, 64, 1)], axis=0)
+
+
+def inverse_factor(full, scale):
     lane = lax.broadcasted_iota(jnp.int32, (64, 128), 1)
     row = lax.broadcasted_iota(jnp.int32, (64, 128), 0)
-    full = jnp.concatenate([packed, pltpu.roll(packed, 64, 1)], axis=0) * scale
-    work = jnp.where(lane < 64, full, (lane - 64 == row).astype(F32))
+    work = jnp.where(lane < 64, full * scale, (lane - 64 == row).astype(F32))
     done = []
     tiles = [work[8 * t : 8 * t + 8] for t in range(8)]
     for t in range(8):
@@ -284,12 +384,12 @@
 
 def middle_kernel(g_ref, image_ref, corr_ref, *, scale):
     packed = g_ref[:, 8:9, :].reshape(32, 128)
-    inv = inverse_factor(packed, scale)
+    inv = inverse_factor(unfold_rows(packed), scale)
     image = apply_inverse(g_ref[:, 0:8, :].reshape(256, 128), inv)
     image_ref[...] = image
     corr = lax.dot_general(image, image, TN, precision=HIGH, preferred_element_type=F32)
     corr = corr[0:64] + pltpu.roll(corr[64:128], 64, 1)
-    corr = fold_rows(corr)
+    corr = pack_symmetric(corr)
     for m in range(16):
         corr_ref[m] = corr
 
@@ -297,7 +397,7 @@
 def middle(g, scale):
     return pl.pallas_call(
         lambda *refs: middle_kernel(*refs, scale=scale),
-        out_shape=(jax.ShapeDtypeStruct((256, 128), F32), jax.ShapeDtypeStruct((16, 32, 128), F32)),
+        out_shape=(jax.ShapeDtypeStruct((256, 128), F32), jax.ShapeDtypeStruct((16, 40, 128), BF)),
         in_specs=[VM],
         out_specs=(VM, VM),
         name="middle",
@@ -305,10 +405,10 @@
 
 
 def last_kernel(image_ref, corr_ref, o_ref, *, scale):
-    packed = corr_ref[0]
+    parts = corr_ref[0].astype(F32)
     for m in range(1, 16):
-        packed = packed + corr_ref[m]
-    inv = inverse_factor(packed, scale)
+        parts = parts + corr_ref[m].astype(F32)
+    inv = inverse_factor(unpack_symmetric(parts), scale)
     upper, lower = lane_halves(inv)
     image = image_ref[...]
     o_ref[:, 0:256] = lax.dot_general(upper, image, NT, precision=HIGH, preferred_element_type=F32)
@@ -330,43 +430,23 @@
     return lax.all_to_all(jnp.broadcast_to(x[None], (size, *x.shape)), axis, 0, 0, tiled=True)
 
 
-def halves_in_lanes(rows, start):
-    low = lax.dynamic_slice_in_dim(rows, start, 8, 0)
-    high = lax.dynamic_slice_in_dim(rows, start + 256, 8, 0)
-    return jnp.concatenate([low, high], axis=1)
-
-
 def on_device(band_form, interp_coef, screen, coulomb, shift_map, grid_order, energies, initial):
-    plane = lax.axis_index("ka")
-    col = lax.axis_index("kp")
-    cells_x, cells_y = grid_order // GRID_Y, grid_order % GRID_Y
-    near_x = lax.dynamic_slice_in_dim(cells_x, 4 * plane, 4)
-    near_y = lax.dynamic_slice_in_dim(cells_y, 4 * plane, 4)
-    table = (near_x[None, :] - cells_x[:, None]) % GRID_X * GRID_Y + (near_y[None, :] - cells_y[:, None]) % GRID_Y
-    table = table.reshape(256)
-
-    columns = screen.transpose(1, 0, 2).reshape(64, 128)
-    forms = lax.dynamic_slice_in_dim(band_form, 64 * col, 64, 2).reshape(2, 2, 24, 64).transpose(0, 2, 1, 3).reshape(48, 128)
-    coefs = lax.dynamic_slice_in_dim(interp_coef, 4 * col, 4, 1).reshape(16, 128)
-    starts = halves_in_lanes(initial, 8 * col)
-    diagonal = halves_in_lanes(jnp.broadcast_to(energies[:, None], (512, 64)), 8 * col)
-    piece = jnp.concatenate([columns, forms, coefs, starts.astype(BF)], axis=0)
+    piece, starts, diagonal, table = share(band_form, interp_coef, screen, initial, energies, grid_order)
     gathered = lax.all_gather(piece, "ka", axis=0, tiled=False)
-    received = lax.all_to_all(pick(gathered, table), "kp", 0, 0, tiled=True)
-
-    received = pltpu.with_memory_space_constraint(received, pltpu.VMEM)
-    own = lax.dynamic_slice_in_dim(table, 8 * col, 8)
-    scalars = jnp.concatenate([own, jnp.broadcast_to(col % 2, (8,)).astype(jnp.int32)])
-    kernel, sent = pair_blocks(scalars, received, band_form, prepare(band_form), interp_coef, coulomb.reshape(16, 128), shift_map.reshape(64, 16, 128))
+    received = lax.all_to_all(pick(vmem(gathered), table), "kp", 0, 0, tiled=True)
+    wide = vmem(prepare(band_form))
+    kernel, sent = pair_blocks(
+        table, vmem(received), band_form, wide, interp_coef, coulomb.reshape(16, 128), vmem(shift_map.reshape(64, 16, 128))
+    )
     sent = lax.all_to_all(sent, "kp", 0, 0, tiled=True)
     image = jnp.sum(sent[:, 0:16, :].astype(F32).reshape(64, 8, 128), axis=0) + diagonal * starts
 
-    sums = jnp.sum(lax.all_to_all(second_product(sent, to_all(image, "ka")), "kp", 0, 0, tiled=True), axis=0)
+    sums = jnp.sum(lax.all_to_all(second_product(vmem(sent), vmem(to_all(image, "ka"))), "kp", 0, 0, tiled=True), axis=0)
     sums = sums + jnp.concatenate([diagonal * image, jnp.zeros((1, 128), F32)], axis=0)
     everyone = to_all(sums, "kp")
     scale = 1.0 / 8192
-    image, corr = middle(everyone, scale)
-    vectors = last(image, lax.all_to_all(corr, "ka", 0, 0, tiled=True), scale)
+    image, corr = middle(vmem(everyone), scale)
+    vectors = last(vmem(image), vmem(lax.all_to_all(corr, "ka", 0, 0, tiled=True)), scale)
     return (kernel, vectors)
 
 

time: 188 us -> 177 us (0.941)
  Pallas kernels: 33.8 us -> 27.4 us
  blocking collectives: 109 us -> 115 us
  starting transfers between devices: 13.3 us -> 7.74 us
  waiting for transfers between devices: 21.3 us -> 16.3 us
    all_to_all x2 -> x3, blocking collectives: 35.8 us -> 44.4 us  [the longest x1 18.2 us: on_device(): lax.all_to_all(corr, 'ka', 0, 0, tiled=True)]
    unnamed x11 -> x22, local copies, waits for them, and re-layouts: 1.04 us -> 6.63 us
    all_to_all x2 -> x1, starting transfers between devices: 13.3 us -> 7.74 us  [on_device(): lax.all_to_all(pick(vmem(gathered), table), 'kp', 0, 0, tiled=True)]
    all_to_all x2 -> x1, waiting for transfers between devices: 21.3 us -> 16.3 us  [on_device(): lax.all_to_all(pick(vmem(gathered), table), 'kp', 0, 0, tiled=True)]
    pallas_call x1, Pallas kernels: 3.97 us -> 0.39 us  [prepare(): pl.pallas_call(prepare_kernel, grid=(4,), in_specs=[pl.BlockSpec((1, 24,...]
    dynamic_slice x7 -> x0, local copies, waits for them, and re-layouts: 2.72 us -> none  [the longest x2 0.94 us: halves_in_lanes(): low = lax.dynamic_slice_in_dim(rows, start, 8, 0)]
    pallas_call x0 -> x1, Pallas kernels: none -> 2.4 us  [share(): pl.pallas_call(share_kernel, in_specs=[hbm, hbm, VM, VM, VM, SM, VM], out...]
    pallas_call x1, Pallas kernels: 15.6 us -> 13.5 us  [pair_blocks(): pl.pallas_call(pair_kernel, in_specs=[SM, VM, VM, VM, VM, VM, VM], out_sp...]
  transfers between devices with their start and end apart: 2 -> 1, of which waited for: 2 -> 1; matrix products, arithmetic and copies ran while one was open for 1% -> 0% of each run, Pallas kernels for 2% -> 0%
where the time goes in v5:
time: 177 us; the launch traced here: 174 us
  blocking collectives  115 us (65%)
  Pallas kernels  27.4 us (15%)
  waiting for transfers between devices  16.3 us (9%)
  starting transfers between devices  7.74 us (4%)
  local copies, waits for them, and re-layouts  6.67 us (4%)
    all_gather x1, blocking collectives, on_device(): gathered = lax.all_gather(piece, 'ka', axis=0, tiled=False)  39 us
    all_to_all x2, blocking collectives, to_all(): lax.all_to_all(jnp.broadcast_to(x[None], (size, *x.shape)), axis, 0, 0, t...  32 us
    all_to_all x1, blocking collectives, on_device(): lax.all_to_all(corr, 'ka', 0, 0, tiled=True)  18.2 us
    all_to_all x1, waiting for transfers between devices, on_device(): lax.all_to_all(pick(vmem(gathered), table), 'kp', 0, 0, tiled=True)  16.3 us
    pallas_call x1, Pallas kernels, pair_blocks(): pl.pallas_call(pair_kernel, in_specs=[SM, VM, VM, VM, VM, VM, VM], out_sp...  13.5 us
    all_to_all x1, blocking collectives, on_device(): sent = lax.all_to_all(sent, 'kp', 0, 0, tiled=True)  13.5 us
    all_to_all x1, blocking collectives, on_device(): lax.all_to_all(second_product(vmem(sent), vmem(to_all(image, 'ka'))), 'kp...  12.7 us
    all_to_all x1, starting transfers between devices, on_device(): lax.all_to_all(pick(vmem(gathered), table), 'kp', 0, 0, tiled=True)  7.74 us
  transfers between devices with their start and end apart: 1, of which 1 were waited for; matrix products, arithmetic and copies ran while one was open for 0% of the time, Pallas kernels for 0%

profile of v5, /device:TPU:6, one launch (start us, length us, event | category | flops | bytes accessed | tf_op | source)
XLA Modules:
  0.0 174.3 jit_solution(13183372029473099074)
XLA Ops:
  0.6 1.5 copy.10.screen_ref
  2.1 2.4 %share.1 = (bf16[136,128]{1,0:T(8,128)(2,1)}, f32[8,128]{1,0:T(8,128)}, f32[8,128]{1,0:T(8,128)}, s32[4,64]{1,0:T(4,128)}) custom-call(bf16[4,24,2048]{2,1,0:T(8,128)(2,1)} %near_ref.1, bf16[4,128,128]{2,1,0:T(8,128)(2,1)} %coef_ref.3, bf16[4,64,32]{2,1,0:T(8,128)(2,1)} %copy.10.screen_ref, f32[64,512]{1,0:T(8,128)} %bitcast.16, f32[4,128]{1,0:T(4,128)} %bitcast.17, ...), custom_call_target="tpu_custom_call" | custom-call | tf_op jit(solution)/shard_map/share/pallas_call | solution.py:67
  4.5 39.0 %all-gather = bf16[2176,128]{1,0:T(8,128)(2,1)S(1)} all-gather(bf16[136,128]{1,0:T(8,128)(2,1)} %get-tuple-element.11), channel_id=2, replica_groups=mesh['kp'=32,'ka'=16] {'ka'}, dimensions={0}, use_global_device_ids=true | all-gather | bytes 591872 | tf_op jit(solution)/shard_map/all_gather | solution.py:435
  43.5 3.2 %pick.1 = bf16[32,168,128]{2,1,0:T(8,128)(2,1)} custom-call(s32[4,64]{1,0:T(4,128)} %get-tuple-element.10.t_ref, bf16[16,136,128]{2,1,0:T(8,128)(2,1)S(1)} %bitcast.10), custom_call_target="tpu_custom_call" | custom-call | tf_op jit(solution)/shard_map/pick/pallas_call | solution.py:112
  46.8 0.0 copy-start.2
  46.8 7.7 %all-to-all-start = ((bf16[32,168,128]{2,1,0:T(8,128)(2,1)}), bf16[32,168,128]{2,1,0:T(8,128)(2,1)S(1)}, u32[]{:S(2)}, u32[]{:S(2)}) async-start(bf16[32,168,128]{2,1,0:T(8,128)(2,1)} %pick.1), calls=%async_computation | async-start | bytes 2752512 | tf_op jit(solution)/shard_map/all_to_all | solution.py:436
  54.5 0.0 copy-done.2
  54.5 0.0 copy-start.7
  54.5 0.0 copy-start.3
  54.5 0.0 copy-start.5
  54.6 0.0 copy-start.6
  54.6 0.4 prepare.1.wide_ref
  55.0 0.0 copy-start
  55.0 1.9 %copy-done = bf16[4,16,16,2048]{3,2,1,0:T(8,128)(2,1)} copy-done((bf16[4,16,16,2048]{3,2,1,0:T(8,128)(2,1)}, bf16[4,16,16,2048]{3,2,1,0:T(8,128)(2,1)S(1)}, u32[]{:S(2)}) %copy-start) | copy-done | bytes 4194328
  56.9 0.0 copy-done.7
  56.9 0.1 copy.11
  57.0 16.3 %all-to-all-done.r_ref = bf16[32,168,128]{2,1,0:T(8,128)(2,1)S(1)} async-done(((bf16[32,168,128]{2,1,0:T(8,128)(2,1)}), bf16[32,168,128]{2,1,0:T(8,128)(2,1)S(1)}, u32[]{:S(2)}, u32[]{:S(2)}) %all-to-all-start) | async-done | bytes 1376288 | tf_op jit(solution)/shard_map/all_to_all | solution.py:436
  73.3 0.0 copy-done.3
  73.3 0.0 copy-done.5
  73.3 0.0 copy-done.6
  73.3 0.0 copy-start.1
  73.3 2.2 %copy-done.1 = bf16[4,16,16,2048]{3,2,1,0:T(8,128)(2,1)S(1)} copy-done((bf16[4,16,16,2048]{3,2,1,0:T(8,128)(2,1)S(1)}, bf16[4,16,16,2048]{3,2,1,0:T(8,128)(2,1)}, u32[]{:S(2)}) %copy-start.1) | copy-done | bytes 4194328
  75.5 0.0 copy-start.8
  75.5 0.0 copy-start.9
  75.5 13.5 %pairs.1 = (bf16[512,256]{1,0:T(8,128)(2,1)}, bf16[32,48,128]{2,1,0:T(8,128)(2,1)S(1)}) custom-call(s32[4,64]{1,0:T(4,128)S(1)} %copy-done.6, bf16[32,168,128]{2,1,0:T(8,128)(2,1)S(1)} %all-to-all-done.r_ref, bf16[4,24,2048]{2,1,0:T(8,128)(2,1)S(1)} %copy-done.2, bf16[4,16,16,2048]{3,2,1,0:T(8,128)(2,1)S(1)} %copy-done.1, ...), custom_call_target="tpu_custom_call" | custom-call | tf_op jit(solution)/shard_map/pairs/pallas_call | solution.py:255
  89.0 13.5 %all_to_all.30.r_ref = bf16[32,48,128]{2,1,0:T(8,128)(2,1)S(1)} all-to-all(bf16[32,48,128]{2,1,0:T(8,128)(2,1)S(1)} %get-tuple-element.13), channel_id=1, replica_groups=mesh['kp'=32,'ka'=16] {'kp'}, dimensions={0} | all-to-all | bytes 786432 | tf_op jit(solution)/shard_map/all_to_all | solution.py:441
  102.5 0.1 convert_reduce_fusion
  102.5 0.0 copy-done.8
  102.5 0.0 copy-done.9
  102.6 19.5 %all_to_all.31.x_ref = f32[16,8,128]{2,1,0:T(8,128)S(1)} all-to-all(f32[16,8,128]{2,1,0:T(8,128)S(1)} %broadcast_in_dim.4), channel_id=1, replica_groups=mesh['kp'=32,'ka'=16] {'ka'}, dimensions={0} | all-to-all | bytes 131072 | tf_op jit(solution)/shard_map/all_to_all | solution.py:430
  122.1 1.3 second.1
  123.4 12.7 %all_to_all.32 = f32[32,9,128]{2,1,0:T(8,128)S(1)} all-to-all(f32[32,9,128]{2,1,0:T(8,128)} %second.1), channel_id=1, replica_groups=mesh['kp'=32,'ka'=16] {'kp'}, dimensions={0} | all-to-all | bytes 294912 | tf_op jit(solution)/shard_map/all_to_all | solution.py:444
  136.1 12.5 %all_to_all.33.refs_0_ = f32[32,9,128]{2,1,0:T(8,128)S(1)} all-to-all(f32[32,9,128]{2,1,0:T(8,128)S(1)} %broadcast_in_dim.5), channel_id=1, replica_groups=mesh['kp'=32,'ka'=16] {'kp'}, dimensions={0} | all-to-all | bytes 294912 | tf_op jit(solution)/shard_map/all_to_all | solution.py:430
  148.6 3.5 %middle.1 = (f32[256,128]{1,0:T(8,128)}, bf16[16,40,128]{2,1,0:T(8,128)(2,1)}) custom-call(f32[32,9,128]{2,1,0:T(8,128)S(1)} %all_to_all.33.refs_0_), custom_call_target="tpu_custom_call" | custom-call | tf_op jit(solution)/shard_map/middle/pallas_call | solution.py:398
  152.1 18.2 %all_to_all.34.refs_1_ = bf16[16,40,128]{2,1,0:T(8,128)(2,1)S(1)} all-to-all(bf16[16,40,128]{2,1,0:T(8,128)(2,1)} %get-tuple-element.17), channel_id=1, replica_groups=mesh['kp'=32,'ka'=16] {'ka'}, dimensions={0} | all-to-all | bytes 327680 | tf_op jit(solution)/shard_map/all_to_all | solution.py:449
  170.4 0.0 copy-start.4
  170.4 0.9 copy-done.4
  171.3 3.0 %last.1 = f32[64,512]{1,0:T(8,128)} custom-call(f32[256,128]{1,0:T(8,128)S(1)} %copy-done.4, bf16[16,40,128]{2,1,0:T(8,128)(2,1)S(1)} %all_to_all.34.refs_1_), custom_call_target="tpu_custom_call" | custom-call | tf_op jit(solution)/shard_map/last/pallas_call | solution.py:419
  (6 shorter events, 0.1 us)
Async XLA Ops:
  46.8 7.8 %copy-start.2 = (bf16[4,24,2048]{2,1,0:T(8,128)(2,1)S(1)}, bf16[4,24,2048]{2,1,0:T(8,128)(2,1)}, u32[]{:S(2)}) copy-start(bf16[4,24,2048]{2,1,0:T(8,128)(2,1)} %near_ref.1) | copy-start | bytes 1179652
  46.8 26.6 %all-to-all-start = ((bf16[32,168,128]{2,1,0:T(8,128)(2,1)}), bf16[32,168,128]{2,1,0:T(8,128)(2,1)S(1)}, u32[]{:S(2)}, u32[]{:S(2)}) async-start(bf16[32,168,128]{2,1,0:T(8,128)(2,1)} %pick.1), calls=%async_computation | async-start | bytes 2752512 | tf_op jit(solution)/shard_map/all_to_all | solution.py:436
  54.5 2.4 %copy-start.7 = (s32[64,2048]{1,0:T(8,128)S(1)}, s32[64,2048]{1,0:T(8,128)}, u32[]{:S(2)}) copy-start(s32[64,2048]{1,0:T(8,128)} %param.12) | copy-start | bytes 1572868
  54.5 18.8 %copy-start.3 = (bf16[4,128,128]{2,1,0:T(8,128)(2,1)S(1)}, bf16[4,128,128]{2,1,0:T(8,128)(2,1)}, u32[]{:S(2)}) copy-start(bf16[4,128,128]{2,1,0:T(8,128)(2,1)} %coef_ref.3) | copy-start | bytes 393220
  54.5 18.8 %copy-start.5 = (f32[2048]{0:T(1024)S(1)}, f32[2048]{0:T(1024)}, u32[]{:S(2)}) copy-start(f32[2048]{0:T(1024)} %param.11) | copy-start | bytes 24580
  54.6 18.8 %copy-start.6 = (s32[4,64]{1,0:T(4,128)S(1)}, s32[4,64]{1,0:T(4,128)}, u32[]{:S(2)}) copy-start(s32[4,64]{1,0:T(4,128)} %get-tuple-element.10.t_ref) | copy-start | bytes 3076
  55.0 1.9 %copy-start = (bf16[4,16,16,2048]{3,2,1,0:T(8,128)(2,1)}, bf16[4,16,16,2048]{3,2,1,0:T(8,128)(2,1)S(1)}, u32[]{:S(2)}) copy-start(bf16[4,16,16,2048]{3,2,1,0:T(8,128)(2,1)S(1)} %prepare.1.wide_ref) | copy-start | bytes 12582916
  73.3 2.2 %copy-start.1 = (bf16[4,16,16,2048]{3,2,1,0:T(8,128)(2,1)S(1)}, bf16[4,16,16,2048]{3,2,1,0:T(8,128)(2,1)}, u32[]{:S(2)}) copy-start(bf16[4,16,16,2048]{3,2,1,0:T(8,128)(2,1)} %copy-done) | copy-start | bytes 12582916
  75.5 27.0 %copy-start.8 = (f32[8,128]{1,0:T(8,128)S(1)}, f32[8,128]{1,0:T(8,128)}, u32[]{:S(2)}) copy-start(f32[8,128]{1,0:T(8,128)} %get-tuple-element.15) | copy-start | bytes 12292
  75.5 27.0 %copy-start.9 = (f32[8,128]{1,0:T(8,128)S(1)}, f32[8,128]{1,0:T(8,128)}, u32[]{:S(2)}) copy-start(f32[8,128]{1,0:T(8,128)} %get-tuple-element.14) | copy-start | bytes 12292
  170.4 0.9 copy-start.4

commit v6 on v5

--- a/solution.py
+++ b/solution.py
@@ -12,6 +12,7 @@
 HIGH = lax.Precision.HIGHEST
 VM = pl.BlockSpec(memory_space=pltpu.VMEM)
 SM = pl.BlockSpec(memory_space=pltpu.SMEM)
+SMALL = pltpu.CompilerParams(vmem_limit_bytes=16 << 20)
 
 
 def device_at(axis):
@@ -35,7 +36,7 @@
     for i in range(4):
         cell = cell_ref[4 * plane + i]
         table_ref[i : i + 1, :] = (((cell >> 3) - x) & 7) * 8 + (((cell & 7) - y) & 7)
-    piece_ref[0:64, :] = jnp.concatenate([screen_ref[q].astype(F32) for q in range(4)], axis=1).astype(BF)
+    piece_ref[0:64, :] = jnp.concatenate([screen_ref[q].astype(F32) for q in range(4)], axis=0).T.astype(BF)
     block = col // 16
     back = (128 - 8 * (col % 16)) % 128
 
@@ -75,8 +76,9 @@
             jax.ShapeDtypeStruct((4, 64), jnp.int32),
         ),
         scratch_shapes=[pltpu.VMEM((4, 24, 128), BF), pltpu.VMEM((4, 8, 128), BF), pltpu.SemaphoreType.DMA((2,))],
+        compiler_params=SMALL,
         name="share",
-    )(forms, coefs, screen, initial.T, energies.reshape(4, 128), cells, cells.reshape(1, 64))
+    )(forms, coefs, screen.transpose(0, 2, 1), initial.T, energies.reshape(4, 128), cells, cells.reshape(1, 64))
 
 
 def pick_kernel(t_ref, g_ref, o_ref, rolled):
@@ -115,6 +117,7 @@
         in_specs=[pl.BlockSpec(memory_space=pltpu.SMEM), pl.BlockSpec(memory_space=pltpu.VMEM)],
         out_specs=pl.BlockSpec(memory_space=pltpu.VMEM),
         scratch_shapes=[pltpu.VMEM((4, 16, 64, 128), BF)],
+        compiler_params=SMALL,
         name="pick",
     )(table, gathered)
 
@@ -140,7 +143,12 @@
     )(near)
 
 
-def pair_kernel(t_ref, r_ref, near_ref, wide_ref, coef_ref, coul_ref, map_ref, o_ref, send_ref, far, farc, nearc, cols, cond, val, scaled, acc, right, kt):
+def pair_kernel(t_ref, r_ref, near_ref, wide_hbm, coef_ref, coul_ref, map_ref, o_ref, send_ref, far, farc, nearc, cols, cond, val, scaled, acc, right, kt, wide_ref, sems):
+    def wide_copy(i):
+        return pltpu.make_async_copy(wide_hbm.at[i], wide_ref.at[i], sems.at[i])
+
+    for i in range(4):
+        wide_copy(i).start()
     col = device_at("kp")
     lane24 = lax.broadcasted_iota(jnp.int32, (24, 128), 1)
     for m in range(16):
@@ -198,6 +206,10 @@
         kt[at_j, at_i] = out.T.astype(BF)
 
     def pair(p, _):
+        @pl.when(p < 4)
+        def _():
+            wide_copy(p).wait()
+
         finish(jnp.maximum(p - 1, 0))
         j = p // 4
         i = p % 4
@@ -254,7 +266,7 @@
 def pair_blocks(table, received, near, wide, coef, coulomb, shift_map):
     return pl.pallas_call(
         pair_kernel,
-        in_specs=[SM, VM, VM, VM, VM, VM, VM],
+        in_specs=[SM, VM, VM, pl.BlockSpec(memory_space=pl.ANY), VM, VM, VM],
         out_specs=(VM, VM),
         out_shape=(jax.ShapeDtypeStruct((512, 256), BF), jax.ShapeDtypeStruct((32, 48, 128), BF)),
         scratch_shapes=[
@@ -268,6 +280,8 @@
             pltpu.VMEM((96, 256), F32),
             pltpu.VMEM((64, 32), F32),
             pltpu.VMEM((256, 512), BF),
+            pltpu.VMEM((4, 16, 16, 2048), BF),
+            pltpu.SemaphoreType.DMA((4,)),
         ],
         compiler_params=pltpu.CompilerParams(vmem_limit_bytes=32 << 20),
         name="pairs",
@@ -309,6 +323,7 @@
         out_shape=jax.ShapeDtypeStruct((32, 9, 128), F32),
         in_specs=[VM, VM],
         out_specs=VM,
+        compiler_params=SMALL,
         name="second",
     )(received, x)
 
@@ -400,6 +415,7 @@
         out_shape=(jax.ShapeDtypeStruct((256, 128), F32), jax.ShapeDtypeStruct((16, 40, 128), BF)),
         in_specs=[VM],
         out_specs=(VM, VM),
+        compiler_params=SMALL,
         name="middle",
     )(g)
 
@@ -421,6 +437,7 @@
         out_shape=jax.ShapeDtypeStruct((64, 512), F32),
         in_specs=[VM, VM],
         out_specs=VM,
+        compiler_params=SMALL,
         name="last",
     )(image, corr).T
 
@@ -434,7 +451,7 @@
     piece, starts, diagonal, table = share(band_form, interp_coef, screen, initial, energies, grid_order)
     gathered = lax.all_gather(piece, "ka", axis=0, tiled=False)
     received = lax.all_to_all(pick(vmem(gathered), table), "kp", 0, 0, tiled=True)
-    wide = vmem(prepare(band_form))
+    wide = pltpu.with_memory_space_constraint(prepare(band_form), pltpu.HBM)
     kernel, sent = pair_blocks(
         table, vmem(received), band_form, wide, interp_coef, coulomb.reshape(16, 128), vmem(shift_map.reshape(64, 16, 128))
     )
@@ -446,7 +463,7 @@
     everyone = to_all(sums, "kp")
     scale = 1.0 / 8192
     image, corr = middle(vmem(everyone), scale)
-    vectors = last(vmem(image), vmem(lax.all_to_all(corr, "ka", 0, 0, tiled=True)), scale)
+    vectors = last(image, vmem(lax.all_to_all(corr, "ka", 0, 0, tiled=True)), scale)
     return (kernel, vectors)
 
 

time: 177 us -> 174 us (0.983)
  Pallas kernels: 27.4 us -> 25 us
    unnamed x22 -> x23, local copies, waits for them, and re-layouts: 6.63 us -> 6.96 us
where the time goes in v6:
time: 174 us; the launch traced here: 171 us
  blocking collectives  114 us (66%)
  Pallas kernels  25 us (14%)
  waiting for transfers between devices  16.3 us (9%)
  starting transfers between devices  7.74 us (4%)
  local copies, waits for them, and re-layouts  7 us (4%)
    all_gather x1, blocking collectives, on_device(): gathered = lax.all_gather(piece, 'ka', axis=0, tiled=False)  38.7 us
    all_to_all x2, blocking collectives, to_all(): lax.all_to_all(jnp.broadcast_to(x[None], (size, *x.shape)), axis, 0, 0, t...  31.9 us
    all_to_all x1, blocking collectives, on_device(): lax.all_to_all(corr, 'ka', 0, 0, tiled=True)  17.9 us
    all_to_all x1, waiting for transfers between devices, on_device(): lax.all_to_all(pick(vmem(gathered), table), 'kp', 0, 0, tiled=True)  16.3 us
    pallas_call x1, Pallas kernels, pair_blocks(): pl.pallas_call(pair_kernel, in_specs=[SM, VM, VM, pl.BlockSpec(memory_spa...  14.2 us
    all_to_all x1, blocking collectives, on_device(): sent = lax.all_to_all(sent, 'kp', 0, 0, tiled=True)  13.5 us
    all_to_all x1, blocking collectives, on_device(): lax.all_to_all(second_product(vmem(sent), vmem(to_all(image, 'ka'))), 'kp...  12.2 us
    all_to_all x1, starting transfers between devices, on_device(): lax.all_to_all(pick(vmem(gathered), table), 'kp', 0, 0, tiled=True)  7.74 us
  transfers between devices with their start and end apart: 1, of which 1 were waited for; matrix products, arithmetic and copies ran while one was open for 0% of the time, Pallas kernels for 0%

profile of v6, /device:TPU:6, one launch (start us, length us, event | category | flops | bytes accessed | tf_op | source)
XLA Modules:
  0.0 171.1 jit_solution(12373293558838929759)
XLA Ops:
  0.6 0.0 copy-start.1
  0.6 1.0 copy-done.1
  1.6 0.0 copy-start.3
  1.6 0.9 copy-done.3
  2.5 0.0 copy-start.5
  2.5 0.9 copy-done.5
  3.4 0.0 copy-start.6
  3.4 0.8 copy-done.6
  4.2 0.0 copy-start.8
  4.2 0.7 copy-done.8
  4.9 0.0 copy-start.9
  4.9 0.7 copy-done.9
  5.5 0.8 share.1
  6.4 38.7 %all-gather = bf16[2176,128]{1,0:T(8,128)(2,1)S(1)} all-gather(bf16[136,128]{1,0:T(8,128)(2,1)S(1)} %get-tuple-element.11), channel_id=2, replica_groups=mesh['kp'=32,'ka'=16] {'ka'}, dimensions={0}, use_global_device_ids=true | all-gather | bytes 591872 | tf_op jit(solution)/shard_map/all_gather | solution.py:452
  45.1 3.1 %pick.1 = bf16[32,168,128]{2,1,0:T(8,128)(2,1)} custom-call(s32[4,64]{1,0:T(4,128)S(1)} %get-tuple-element.10.t_ref, bf16[16,136,128]{2,1,0:T(8,128)(2,1)S(1)} %bitcast.11), custom_call_target="tpu_custom_call" | custom-call | tf_op jit(solution)/shard_map/pick/pallas_call | solution.py:114
  48.2 0.0 copy-start.2
  48.2 7.7 %all-to-all-start = ((bf16[32,168,128]{2,1,0:T(8,128)(2,1)}), bf16[32,168,128]{2,1,0:T(8,128)(2,1)S(1)}, u32[]{:S(2)}, u32[]{:S(2)}) async-start(bf16[32,168,128]{2,1,0:T(8,128)(2,1)} %pick.1), calls=%async_computation | async-start | bytes 2752512 | tf_op jit(solution)/shard_map/all_to_all | solution.py:453
  56.0 0.0 copy-done.2
  56.0 0.0 copy-start.10
  56.0 0.0 copy-start.4
  56.0 0.0 copy-start.7
  56.0 0.4 prepare.1.wide_hbm
  56.4 0.0 copy-start
  56.4 1.9 %copy-done = bf16[4,16,16,2048]{3,2,1,0:T(8,128)(2,1)} copy-done((bf16[4,16,16,2048]{3,2,1,0:T(8,128)(2,1)}, bf16[4,16,16,2048]{3,2,1,0:T(8,128)(2,1)S(1)}, u32[]{:S(2)}) %copy-start) | copy-done | bytes 4194328
  58.4 0.0 copy-done.10
  58.4 0.1 copy.10
  58.5 16.3 %all-to-all-done.r_ref = bf16[32,168,128]{2,1,0:T(8,128)(2,1)S(1)} async-done(((bf16[32,168,128]{2,1,0:T(8,128)(2,1)}), bf16[32,168,128]{2,1,0:T(8,128)(2,1)S(1)}, u32[]{:S(2)}, u32[]{:S(2)}) %all-to-all-start) | async-done | bytes 1376288 | tf_op jit(solution)/shard_map/all_to_all | solution.py:453
  74.8 0.0 copy-done.4
  74.8 0.0 copy-done.7
  74.8 14.2 %pairs.1 = (bf16[512,256]{1,0:T(8,128)(2,1)}, bf16[32,48,128]{2,1,0:T(8,128)(2,1)S(1)}) custom-call(s32[4,64]{1,0:T(4,128)S(1)} %get-tuple-element.10.t_ref, bf16[32,168,128]{2,1,0:T(8,128)(2,1)S(1)} %all-to-all-done.r_ref, bf16[4,24,2048]{2,1,0:T(8,128)(2,1)S(1)} %copy-done.2, bf16[4,16,16,2048]{3,2,1,0:T(8,128)(2,1)} %copy-done, ...), custom_call_target="tpu_custom_call" | custom-call | tf_op jit(solution)/shard_map/pairs/pallas_call | solution.py:267
  89.0 13.5 %all_to_all.30.r_ref = bf16[32,48,128]{2,1,0:T(8,128)(2,1)S(1)} all-to-all(bf16[32,48,128]{2,1,0:T(8,128)(2,1)S(1)} %get-tuple-element.13), channel_id=1, replica_groups=mesh['kp'=32,'ka'=16] {'kp'}, dimensions={0} | all-to-all | bytes 786432 | tf_op jit(solution)/shard_map/all_to_all | solution.py:458
  102.5 0.1 convert_reduce_fusion
  102.5 19.5 %all_to_all.31.x_ref = f32[16,8,128]{2,1,0:T(8,128)S(1)} all-to-all(f32[16,8,128]{2,1,0:T(8,128)S(1)} %broadcast_in_dim.4), channel_id=1, replica_groups=mesh['kp'=32,'ka'=16] {'ka'}, dimensions={0} | all-to-all | bytes 131072 | tf_op jit(solution)/shard_map/all_to_all | solution.py:447
  122.1 0.5 second.1
  122.6 12.2 %all_to_all.32 = f32[32,9,128]{2,1,0:T(8,128)S(1)} all-to-all(f32[32,9,128]{2,1,0:T(8,128)S(1)} %second.1), channel_id=1, replica_groups=mesh['kp'=32,'ka'=16] {'kp'}, dimensions={0} | all-to-all | bytes 294912 | tf_op jit(solution)/shard_map/all_to_all | solution.py:461
  134.9 12.4 %all_to_all.33.refs_0_ = f32[32,9,128]{2,1,0:T(8,128)S(1)} all-to-all(f32[32,9,128]{2,1,0:T(8,128)S(1)} %broadcast_in_dim.5), channel_id=1, replica_groups=mesh['kp'=32,'ka'=16] {'kp'}, dimensions={0} | all-to-all | bytes 294912 | tf_op jit(solution)/shard_map/all_to_all | solution.py:447
  147.3 2.9 %middle.1 = (f32[256,128]{1,0:T(8,128)S(1)}, bf16[16,40,128]{2,1,0:T(8,128)(2,1)S(1)}) custom-call(f32[32,9,128]{2,1,0:T(8,128)S(1)} %all_to_all.33.refs_0_), custom_call_target="tpu_custom_call" | custom-call | tf_op jit(solution)/shard_map/middle/pallas_call | solution.py:413
  150.2 17.9 %all_to_all.34.refs_1_ = bf16[16,40,128]{2,1,0:T(8,128)(2,1)S(1)} all-to-all(bf16[16,40,128]{2,1,0:T(8,128)(2,1)S(1)} %get-tuple-element.17), channel_id=1, replica_groups=mesh['kp'=32,'ka'=16] {'ka'}, dimensions={0} | all-to-all | bytes 327680 | tf_op jit(solution)/shard_map/all_to_all | solution.py:466
  168.1 3.0 %last.1 = f32[64,512]{1,0:T(8,128)} custom-call(f32[256,128]{1,0:T(8,128)S(1)} %get-tuple-element.16.refs_0_, bf16[16,40,128]{2,1,0:T(8,128)(2,1)S(1)} %all_to_all.34.refs_1_), custom_call_target="tpu_custom_call" | custom-call | tf_op jit(solution)/shard_map/last/pallas_call | solution.py:435
  (6 shorter events, 0.1 us)
Async XLA Ops:
  0.6 1.0 copy-start.1
  1.6 0.9 copy-start.3
  2.5 0.9 copy-start.5
  3.4 0.8 copy-start.6
  4.2 0.7 copy-start.8
  4.9 0.7 copy-start.9
  48.2 7.8 %copy-start.2 = (bf16[4,24,2048]{2,1,0:T(8,128)(2,1)S(1)}, bf16[4,24,2048]{2,1,0:T(8,128)(2,1)}, u32[]{:S(2)}) copy-start(bf16[4,24,2048]{2,1,0:T(8,128)(2,1)} %near_ref.1) | copy-start | bytes 1179652
  48.2 26.6 %all-to-all-start = ((bf16[32,168,128]{2,1,0:T(8,128)(2,1)}), bf16[32,168,128]{2,1,0:T(8,128)(2,1)S(1)}, u32[]{:S(2)}, u32[]{:S(2)}) async-start(bf16[32,168,128]{2,1,0:T(8,128)(2,1)} %pick.1), calls=%async_computation | async-start | bytes 2752512 | tf_op jit(solution)/shard_map/all_to_all | solution.py:453
  56.0 2.4 %copy-start.10 = (s32[64,2048]{1,0:T(8,128)S(1)}, s32[64,2048]{1,0:T(8,128)}, u32[]{:S(2)}) copy-start(s32[64,2048]{1,0:T(8,128)} %param.12) | copy-start | bytes 1572868
  56.0 18.8 %copy-start.4 = (bf16[4,128,128]{2,1,0:T(8,128)(2,1)S(1)}, bf16[4,128,128]{2,1,0:T(8,128)(2,1)}, u32[]{:S(2)}) copy-start(bf16[4,128,128]{2,1,0:T(8,128)(2,1)} %coef_ref.3) | copy-start | bytes 393220
  56.0 18.8 %copy-start.7 = (f32[2048]{0:T(1024)S(1)}, f32[2048]{0:T(1024)}, u32[]{:S(2)}) copy-start(f32[2048]{0:T(1024)} %param.11) | copy-start | bytes 24580
  56.4 2.0 %copy-start = (bf16[4,16,16,2048]{3,2,1,0:T(8,128)(2,1)}, bf16[4,16,16,2048]{3,2,1,0:T(8,128)(2,1)S(1)}, u32[]{:S(2)}) copy-start(bf16[4,16,16,2048]{3,2,1,0:T(8,128)(2,1)S(1)} %prepare.1.wide_hbm) | copy-start | bytes 12582916

commit v7 on v6

--- a/solution.py
+++ b/solution.py
@@ -23,18 +23,26 @@
     return pltpu.with_memory_space_constraint(x, pltpu.VMEM)
 
 
-def share_kernel(form_ref, coef_ref, screen_ref, start_ref, energy_ref, cell_ref, cells_ref, piece_ref, first_ref, diagonal_ref, table_ref, form, coef, sems):
+def share_kernel(form_hbm, coef_hbm, screen_hbm, start_hbm, energy_hbm, cells_hbm, piece_ref, first_ref, diagonal_ref, table_ref, form, coef, screen_ref, start_ref, energy_ref, cells_ref, sems):
     plane, col = device_at("ka"), device_at("kp")
     odd = (col & 1) == 1
-    copies = (
-        pltpu.make_async_copy(form_ref.at[:, :, pl.ds(pl.multiple_of(128 * (col // 2), 128), 128)], form, sems.at[0]),
-        pltpu.make_async_copy(coef_ref.at[:, pl.ds(pl.multiple_of(8 * (col // 2), 8), 8), :], coef, sems.at[1]),
+    moves = (
+        (cells_hbm, cells_ref),
+        (screen_hbm, screen_ref),
+        (start_hbm, start_ref),
+        (energy_hbm, energy_ref),
+        (form_hbm.at[:, :, pl.ds(pl.multiple_of(128 * (col // 2), 128), 128)], form),
+        (coef_hbm.at[:, pl.ds(pl.multiple_of(8 * (col // 2), 8), 8), :], coef),
     )
+    copies = [pltpu.make_async_copy(src, dst, sems.at[n]) for n, (src, dst) in enumerate(moves)]
     for copy in copies:
         copy.start()
+    for copy in copies:
+        copy.wait()
     x, y = cells_ref[...] >> 3, cells_ref[...] & 7
     for i in range(4):
-        cell = cell_ref[4 * plane + i]
+        own = lax.broadcasted_iota(jnp.int32, (1, 64), 1) == 4 * plane + i
+        cell = jnp.sum(jnp.where(own, cells_ref[...], 0).astype(F32), axis=1, keepdims=True).astype(jnp.int32)
         table_ref[i : i + 1, :] = (((cell >> 3) - x) & 7) * 8 + (((cell & 7) - y) & 7)
     piece_ref[0:64, :] = jnp.concatenate([screen_ref[q].astype(F32) for q in range(4)], axis=0).T.astype(BF)
     block = col // 16
@@ -50,8 +58,6 @@
     piece_ref[128:136, :] = first.astype(BF)
     lane = lax.broadcasted_iota(jnp.int32, (24, 128), 1)
     row = lax.broadcasted_iota(jnp.int32, (8, 128), 0)
-    copies[0].wait()
-    copies[1].wait()
     for h in range(2):
         a, b = form[2 * h].astype(F32), form[2 * h + 1].astype(F32)
         low = jnp.where(odd, pltpu.roll(a, 64, 1), a)
@@ -64,10 +70,10 @@
 
 
 def share(forms, coefs, screen, initial, energies, cells):
-    hbm = pl.BlockSpec(memory_space=pl.ANY)
+    hbm = pl.BlockSpec(memory_space=pltpu.HBM)
     return pl.pallas_call(
         share_kernel,
-        in_specs=[hbm, hbm, VM, VM, VM, SM, VM],
+        in_specs=[hbm] * 6,
         out_specs=(VM, VM, VM, VM),
         out_shape=(
             jax.ShapeDtypeStruct((136, 128), BF),
@@ -75,10 +81,18 @@
             jax.ShapeDtypeStruct((8, 128), F32),
             jax.ShapeDtypeStruct((4, 64), jnp.int32),
         ),
-        scratch_shapes=[pltpu.VMEM((4, 24, 128), BF), pltpu.VMEM((4, 8, 128), BF), pltpu.SemaphoreType.DMA((2,))],
+        scratch_shapes=[
+            pltpu.VMEM((4, 24, 128), BF),
+            pltpu.VMEM((4, 8, 128), BF),
+            pltpu.VMEM((4, 32, 64), BF),
+            pltpu.VMEM((64, 512), F32),
+            pltpu.VMEM((4, 128), F32),
+            pltpu.VMEM((1, 64), jnp.int32),
+            pltpu.SemaphoreType.DMA((6,)),
+        ],
         compiler_params=SMALL,
         name="share",
-    )(forms, coefs, screen.transpose(0, 2, 1), initial.T, energies.reshape(4, 128), cells, cells.reshape(1, 64))
+    )(*(pltpu.with_memory_space_constraint(x, pltpu.HBM) for x in (forms, coefs, screen.transpose(0, 2, 1), initial.T, energies.reshape(4, 128), cells.reshape(1, 64))))
 
 
 def pick_kernel(t_ref, g_ref, o_ref, rolled):

time: 174 us -> 169 us (0.971)
  local copies, waits for them, and re-layouts: 7 us -> 2.08 us
    unnamed x23 -> x11, local copies, waits for them, and re-layouts: 6.96 us -> 2.04 us
where the time goes in v7:
time: 169 us; the launch traced here: 167 us
  blocking collectives  114 us (67%)
  Pallas kernels  25.4 us (15%)
  waiting for transfers between devices  16.3 us (10%)
  starting transfers between devices  7.74 us (5%)
  local copies, waits for them, and re-layouts  2.08 us (1%)
    all_gather x1, blocking collectives, on_device(): gathered = lax.all_gather(piece, 'ka', axis=0, tiled=False)  38.7 us
    all_to_all x2, blocking collectives, to_all(): lax.all_to_all(jnp.broadcast_to(x[None], (size, *x.shape)), axis, 0, 0, t...  31.9 us
    all_to_all x1, blocking collectives, on_device(): lax.all_to_all(corr, 'ka', 0, 0, tiled=True)  17.9 us
    all_to_all x1, waiting for transfers between devices, on_device(): lax.all_to_all(pick(vmem(gathered), table), 'kp', 0, 0, tiled=True)  16.3 us
    pallas_call x1, Pallas kernels, pair_blocks(): pl.pallas_call(pair_kernel, in_specs=[SM, VM, VM, pl.BlockSpec(memory_spa...  14.2 us
    all_to_all x1, blocking collectives, on_device(): sent = lax.all_to_all(sent, 'kp', 0, 0, tiled=True)  13.5 us
    all_to_all x1, blocking collectives, on_device(): lax.all_to_all(second_product(vmem(sent), vmem(to_all(image, 'ka'))), 'kp...  12.2 us
    all_to_all x1, starting transfers between devices, on_device(): lax.all_to_all(pick(vmem(gathered), table), 'kp', 0, 0, tiled=True)  7.74 us
  transfers between devices with their start and end apart: 1, of which 1 were waited for; matrix products, arithmetic and copies ran while one was open for 0% of the time, Pallas kernels for 0%

profile of v7, /device:TPU:6, one launch (start us, length us, event | category | flops | bytes accessed | tf_op | source)
XLA Modules:
  0.0 166.6 jit_solution(3979933016032233173)
XLA Ops:
  0.6 1.2 share.1
  1.8 38.7 %all-gather = bf16[2176,128]{1,0:T(8,128)(2,1)S(1)} all-gather(bf16[136,128]{1,0:T(8,128)(2,1)S(1)} %get-tuple-element.11), channel_id=2, replica_groups=mesh['kp'=32,'ka'=16] {'ka'}, dimensions={0}, use_global_device_ids=true | all-gather | bytes 591872 | tf_op jit(solution)/shard_map/all_gather | solution.py:466
  40.5 3.1 %pick.1 = bf16[32,168,128]{2,1,0:T(8,128)(2,1)} custom-call(s32[4,64]{1,0:T(4,128)S(1)} %get-tuple-element.10.t_ref, bf16[16,136,128]{2,1,0:T(8,128)(2,1)S(1)} %bitcast.11), custom_call_target="tpu_custom_call" | custom-call | tf_op jit(solution)/shard_map/pick/pallas_call | solution.py:128
  43.7 0.0 copy-start.1
  43.7 7.7 %all-to-all-start = ((bf16[32,168,128]{2,1,0:T(8,128)(2,1)}), bf16[32,168,128]{2,1,0:T(8,128)(2,1)S(1)}, u32[]{:S(2)}, u32[]{:S(2)}) async-start(bf16[32,168,128]{2,1,0:T(8,128)(2,1)} %pick.1), calls=%async_computation | async-start | bytes 2752512 | tf_op jit(solution)/shard_map/all_to_all | solution.py:467
  51.4 0.0 copy-done.1
  51.4 0.0 copy-start.4
  51.4 0.0 copy-start.2
  51.5 0.0 copy-start.3
  51.5 0.4 prepare.1.wide_hbm
  51.9 0.0 copy-start
  51.9 1.9 %copy-done = bf16[4,16,16,2048]{3,2,1,0:T(8,128)(2,1)} copy-done((bf16[4,16,16,2048]{3,2,1,0:T(8,128)(2,1)}, bf16[4,16,16,2048]{3,2,1,0:T(8,128)(2,1)S(1)}, u32[]{:S(2)}) %copy-start) | copy-done | bytes 4194328
  53.8 0.0 copy-done.4
  53.8 0.1 copy.10
  53.9 16.3 %all-to-all-done.r_ref = bf16[32,168,128]{2,1,0:T(8,128)(2,1)S(1)} async-done(((bf16[32,168,128]{2,1,0:T(8,128)(2,1)}), bf16[32,168,128]{2,1,0:T(8,128)(2,1)S(1)}, u32[]{:S(2)}, u32[]{:S(2)}) %all-to-all-start) | async-done | bytes 1376288 | tf_op jit(solution)/shard_map/all_to_all | solution.py:467
  70.2 0.0 copy-done.2
  70.2 0.0 copy-done.3
  70.2 14.2 %pairs.1 = (bf16[512,256]{1,0:T(8,128)(2,1)}, bf16[32,48,128]{2,1,0:T(8,128)(2,1)S(1)}) custom-call(s32[4,64]{1,0:T(4,128)S(1)} %get-tuple-element.10.t_ref, bf16[32,168,128]{2,1,0:T(8,128)(2,1)S(1)} %all-to-all-done.r_ref, bf16[4,24,2048]{2,1,0:T(8,128)(2,1)S(1)} %copy-done.1, bf16[4,16,16,2048]{3,2,1,0:T(8,128)(2,1)} %copy-done, ...), custom_call_target="tpu_custom_call" | custom-call | tf_op jit(solution)/shard_map/pairs/pallas_call | solution.py:281
  84.4 13.5 %all_to_all.30.r_ref = bf16[32,48,128]{2,1,0:T(8,128)(2,1)S(1)} all-to-all(bf16[32,48,128]{2,1,0:T(8,128)(2,1)S(1)} %get-tuple-element.13), channel_id=1, replica_groups=mesh['kp'=32,'ka'=16] {'kp'}, dimensions={0} | all-to-all | bytes 786432 | tf_op jit(solution)/shard_map/all_to_all | solution.py:472
  97.9 0.1 convert_reduce_fusion
  98.0 19.5 %all_to_all.31.x_ref = f32[16,8,128]{2,1,0:T(8,128)S(1)} all-to-all(f32[16,8,128]{2,1,0:T(8,128)S(1)} %broadcast_in_dim.4), channel_id=1, replica_groups=mesh['kp'=32,'ka'=16] {'ka'}, dimensions={0} | all-to-all | bytes 131072 | tf_op jit(solution)/shard_map/all_to_all | solution.py:461
  117.5 0.5 second.1
  118.1 12.2 %all_to_all.32 = f32[32,9,128]{2,1,0:T(8,128)S(1)} all-to-all(f32[32,9,128]{2,1,0:T(8,128)S(1)} %second.1), channel_id=1, replica_groups=mesh['kp'=32,'ka'=16] {'kp'}, dimensions={0} | all-to-all | bytes 294912 | tf_op jit(solution)/shard_map/all_to_all | solution.py:475
  130.3 12.4 %all_to_all.33.refs_0_ = f32[32,9,128]{2,1,0:T(8,128)S(1)} all-to-all(f32[32,9,128]{2,1,0:T(8,128)S(1)} %broadcast_in_dim.5), channel_id=1, replica_groups=mesh['kp'=32,'ka'=16] {'kp'}, dimensions={0} | all-to-all | bytes 294912 | tf_op jit(solution)/shard_map/all_to_all | solution.py:461
  142.8 2.9 %middle.1 = (f32[256,128]{1,0:T(8,128)S(1)}, bf16[16,40,128]{2,1,0:T(8,128)(2,1)S(1)}) custom-call(f32[32,9,128]{2,1,0:T(8,128)S(1)} %all_to_all.33.refs_0_), custom_call_target="tpu_custom_call" | custom-call | tf_op jit(solution)/shard_map/middle/pallas_call | solution.py:427
  145.7 17.9 %all_to_all.34.refs_1_ = bf16[16,40,128]{2,1,0:T(8,128)(2,1)S(1)} all-to-all(bf16[16,40,128]{2,1,0:T(8,128)(2,1)S(1)} %get-tuple-element.17), channel_id=1, replica_groups=mesh['kp'=32,'ka'=16] {'ka'}, dimensions={0} | all-to-all | bytes 327680 | tf_op jit(solution)/shard_map/all_to_all | solution.py:480
  163.5 3.0 %last.1 = f32[64,512]{1,0:T(8,128)} custom-call(f32[256,128]{1,0:T(8,128)S(1)} %get-tuple-element.16.refs_0_, bf16[16,40,128]{2,1,0:T(8,128)(2,1)S(1)} %all_to_all.34.refs_1_), custom_call_target="tpu_custom_call" | custom-call | tf_op jit(solution)/shard_map/last/pallas_call | solution.py:449
  (6 shorter events, 0.1 us)
Async XLA Ops:
  43.7 7.8 %copy-start.1 = (bf16[4,24,2048]{2,1,0:T(8,128)(2,1)S(1)}, bf16[4,24,2048]{2,1,0:T(8,128)(2,1)}, u32[]{:S(2)}) copy-start(bf16[4,24,2048]{2,1,0:T(8,128)(2,1)} %near_ref.1) | copy-start | bytes 1179652
  43.7 26.6 %all-to-all-start = ((bf16[32,168,128]{2,1,0:T(8,128)(2,1)}), bf16[32,168,128]{2,1,0:T(8,128)(2,1)S(1)}, u32[]{:S(2)}, u32[]{:S(2)}) async-start(bf16[32,168,128]{2,1,0:T(8,128)(2,1)} %pick.1), calls=%async_computation | async-start | bytes 2752512 | tf_op jit(solution)/shard_map/all_to_all | solution.py:467
  51.4 2.4 %copy-start.4 = (s32[64,2048]{1,0:T(8,128)S(1)}, s32[64,2048]{1,0:T(8,128)}, u32[]{:S(2)}) copy-start(s32[64,2048]{1,0:T(8,128)} %param.12) | copy-start | bytes 1572868
  51.4 18.8 %copy-start.2 = (bf16[4,128,128]{2,1,0:T(8,128)(2,1)S(1)}, bf16[4,128,128]{2,1,0:T(8,128)(2,1)}, u32[]{:S(2)}) copy-start(bf16[4,128,128]{2,1,0:T(8,128)(2,1)} %coef_ref.1) | copy-start | bytes 393220
  51.5 18.8 %copy-start.3 = (f32[2048]{0:T(1024)S(1)}, f32[2048]{0:T(1024)}, u32[]{:S(2)}) copy-start(f32[2048]{0:T(1024)} %param.11) | copy-start | bytes 24580
  51.9 1.9 %copy-start = (bf16[4,16,16,2048]{3,2,1,0:T(8,128)(2,1)}, bf16[4,16,16,2048]{3,2,1,0:T(8,128)(2,1)S(1)}, u32[]{:S(2)}) copy-start(bf16[4,16,16,2048]{3,2,1,0:T(8,128)(2,1)S(1)} %prepare.1.wide_hbm) | copy-start | bytes 12582916

commit v8 on v7

--- a/solution.py
+++ b/solution.py
@@ -95,9 +95,13 @@
     )(*(pltpu.with_memory_space_constraint(x, pltpu.HBM) for x in (forms, coefs, screen.transpose(0, 2, 1), initial.T, energies.reshape(4, 128), cells.reshape(1, 64))))
 
 
+def slot_of(plane):
+    return (plane & 3) * 4 + (plane >> 2)
+
+
 def pick_kernel(t_ref, g_ref, o_ref, rolled):
     def roll_one(h, _):
-        x = g_ref[h, 0:64, :].astype(F32)
+        x = g_ref[slot_of(h), 0:64, :].astype(F32)
         rolled[0, h] = x.astype(BF)
         for s in range(1, 4):
             rolled[s, h] = pltpu.roll(x, 32 * s, 1).astype(BF)
@@ -115,7 +119,7 @@
                 acc = tile if acc is None else jnp.where(lane_block == i, tile, acc)
             o_ref[d, 64 * j : 64 * j + 64, :] = acc.astype(BF)
         half = d & 1
-        plane = d >> 1
+        plane = slot_of(d >> 1)
         o_ref[d, 128:152, :] = g_ref[plane, pl.ds(pl.multiple_of(64 + 24 * half, 8), 24), :]
         o_ref[d, 152:160, :] = g_ref[plane, pl.ds(pl.multiple_of(112 + 8 * half, 8), 8), :]
         o_ref[d, 160:168, :] = g_ref[plane, 128:136, :]
@@ -461,9 +465,16 @@
     return lax.all_to_all(jnp.broadcast_to(x[None], (size, *x.shape)), axis, 0, 0, tiled=True)
 
 
+def gather_planes(x):
+    for groups in ([[i + 4 * j for j in range(4)] for i in range(4)], [[4 * i + j for j in range(4)] for i in range(4)]):
+        x = jnp.broadcast_to(x[None], (4, *x.shape)).reshape(-1, 136, 128)
+        x = lax.all_to_all(x, "ka", 0, 0, tiled=True, axis_index_groups=groups)
+    return x
+
+
 def on_device(band_form, interp_coef, screen, coulomb, shift_map, grid_order, energies, initial):
     piece, starts, diagonal, table = share(band_form, interp_coef, screen, initial, energies, grid_order)
-    gathered = lax.all_gather(piece, "ka", axis=0, tiled=False)
+    gathered = gather_planes(piece)
     received = lax.all_to_all(pick(vmem(gathered), table), "kp", 0, 0, tiled=True)
     wide = pltpu.with_memory_space_constraint(prepare(band_form), pltpu.HBM)
     kernel, sent = pair_blocks(

time: 169 us -> 176 us (1.041)
  blocking collectives: 114 us -> 121 us
    all_to_all x0 -> x2, blocking collectives: none -> 46.7 us  [gather_planes(): x = lax.all_to_all(x, 'ka', 0, 0, tiled=True, axis_index_groups=groups)]
    all_gather x1 -> x0, blocking collectives: 38.7 us -> none  [on_device(): gathered = lax.all_gather(piece, 'ka', axis=0, tiled=False)]
where the time goes in v8:
time: 176 us; the launch traced here: 173 us
  blocking collectives  121 us (69%)
  Pallas kernels  25.4 us (14%)
  waiting for transfers between devices  16.3 us (9%)
  starting transfers between devices  7.74 us (4%)
  local copies, waits for them, and re-layouts  2.17 us (1%)
    all_to_all x2, blocking collectives, gather_planes(): x = lax.all_to_all(x, 'ka', 0, 0, tiled=True, axis_index_groups=groups)  46.7 us
    all_to_all x2, blocking collectives, to_all(): lax.all_to_all(jnp.broadcast_to(x[None], (size, *x.shape)), axis, 0, 0, t...  30.5 us
    all_to_all x1, blocking collectives, on_device(): lax.all_to_all(corr, 'ka', 0, 0, tiled=True)  17.9 us
    all_to_all x1, waiting for transfers between devices, on_device(): lax.all_to_all(pick(vmem(gathered), table), 'kp', 0, 0, tiled=True)  16.3 us
    pallas_call x1, Pallas kernels, pair_blocks(): pl.pallas_call(pair_kernel, in_specs=[SM, VM, VM, pl.BlockSpec(memory_spa...  14.2 us
    all_to_all x1, blocking collectives, on_device(): sent = lax.all_to_all(sent, 'kp', 0, 0, tiled=True)  13.5 us
    all_to_all x1, blocking collectives, on_device(): lax.all_to_all(second_product(vmem(sent), vmem(to_all(image, 'ka'))), 'kp...  12.2 us
    all_to_all x1, starting transfers between devices, on_device(): lax.all_to_all(pick(vmem(gathered), table), 'kp', 0, 0, tiled=True)  7.74 us
  transfers between devices with their start and end apart: 1, of which 1 were waited for; matrix products, arithmetic and copies ran while one was open for 0% of the time, Pallas kernels for 0%

profile of v8, /device:TPU:6, one launch (start us, length us, event | category | flops | bytes accessed | tf_op | source)
XLA Modules:
  0.0 173.3 jit_solution(2471603180511906955)
XLA Ops:
  0.6 1.2 share.1
  1.9 29.9 %all_to_all.40 = bf16[4,136,128]{2,1,0:T(8,128)(2,1)S(1)} all-to-all(bf16[4,136,128]{2,1,0:T(8,128)(2,1)S(1)} %broadcast_in_dim.8), channel_id=1, replica_groups={{0,4,8,12},{1,5,9,13},{2,6,10,14},{3,7,11,15},{16,20,24,28},{17,21,25,2..., dimensions={0} | all-to-all | bytes 278528 | tf_op jit(solution)/shard_map/all_to_all | solution.py:471
  31.8 0.1 broadcast_in_dim.9
  31.9 16.8 %all_to_all.41.g_ref = bf16[16,136,128]{2,1,0:T(8,128)(2,1)S(1)} all-to-all(bf16[16,136,128]{2,1,0:T(8,128)(2,1)S(1)} %bitcast.13), channel_id=1, replica_groups={{0,1,2,3},{4,5,6,7},{8,9,10,11},{12,13,14,15},{16,17,18,19},{20,21,22,2..., dimensions={0} | all-to-all | bytes 1114112 | tf_op jit(solution)/shard_map/all_to_all | solution.py:471
  48.7 3.2 %pick.1 = bf16[32,168,128]{2,1,0:T(8,128)(2,1)} custom-call(s32[4,64]{1,0:T(4,128)S(1)} %get-tuple-element.10.t_ref, bf16[16,136,128]{2,1,0:T(8,128)(2,1)S(1)} %all_to_all.41.g_ref), custom_call_target="tpu_custom_call" | custom-call | tf_op jit(solution)/shard_map/pick/pallas_call | solution.py:132
  51.8 0.0 copy-start.1
  51.8 7.7 %all-to-all-start.2 = ((bf16[32,168,128]{2,1,0:T(8,128)(2,1)}), bf16[32,168,128]{2,1,0:T(8,128)(2,1)S(1)}, u32[]{:S(2)}, u32[]{:S(2)}) async-start(bf16[32,168,128]{2,1,0:T(8,128)(2,1)} %pick.1), calls=%async_computation.2 | async-start | bytes 2752512 | tf_op jit(solution)/shard_map/all_to_all | solution.py:478
  59.6 0.0 copy-done.1
  59.6 0.0 copy-start.4
  59.6 0.0 copy-start.2
  59.6 0.0 copy-start.3
  59.6 0.4 prepare.1.wide_hbm
  60.0 0.0 copy-start
  60.0 1.9 %copy-done = bf16[4,16,16,2048]{3,2,1,0:T(8,128)(2,1)} copy-done((bf16[4,16,16,2048]{3,2,1,0:T(8,128)(2,1)}, bf16[4,16,16,2048]{3,2,1,0:T(8,128)(2,1)S(1)}, u32[]{:S(2)}) %copy-start) | copy-done | bytes 4194328
  61.9 0.0 copy-done.4
  62.0 0.1 copy.10
  62.0 16.3 %all-to-all-done.2.r_ref = bf16[32,168,128]{2,1,0:T(8,128)(2,1)S(1)} async-done(((bf16[32,168,128]{2,1,0:T(8,128)(2,1)}), bf16[32,168,128]{2,1,0:T(8,128)(2,1)S(1)}, u32[]{:S(2)}, u32[]{:S(2)}) %all-to-all-start.2) | async-done | bytes 1376288 | tf_op jit(solution)/shard_map/all_to_all | solution.py:478
  78.4 0.0 copy-done.2
  78.4 0.0 copy-done.3
  78.4 14.2 %pairs.1 = (bf16[512,256]{1,0:T(8,128)(2,1)}, bf16[32,48,128]{2,1,0:T(8,128)(2,1)S(1)}) custom-call(s32[4,64]{1,0:T(4,128)S(1)} %get-tuple-element.10.t_ref, bf16[32,168,128]{2,1,0:T(8,128)(2,1)S(1)} %all-to-all-done.2.r_ref, bf16[4,24,2048]{2,1,0:T(8,128)(2,1)S(1)} %copy-done.1, bf16[4,16,16,2048]{3,2,1,0:T(8,128)(2,1)} %copy-done, ...), custom_call_target="tpu_custom_call" | custom-call | tf_op jit(solution)/shard_map/pairs/pallas_call | solution.py:285
  92.6 13.5 %all_to_all.42.r_ref = bf16[32,48,128]{2,1,0:T(8,128)(2,1)S(1)} all-to-all(bf16[32,48,128]{2,1,0:T(8,128)(2,1)S(1)} %get-tuple-element.13), channel_id=1, replica_groups=mesh['kp'=32,'ka'=16] {'kp'}, dimensions={0} | all-to-all | bytes 786432 | tf_op jit(solution)/shard_map/all_to_all | solution.py:483
  106.1 0.1 convert_reduce_fusion
  106.2 18.1 %all_to_all.43.x_ref = f32[16,8,128]{2,1,0:T(8,128)S(1)} all-to-all(f32[16,8,128]{2,1,0:T(8,128)S(1)} %broadcast_in_dim.10), channel_id=1, replica_groups=mesh['kp'=32,'ka'=16] {'ka'}, dimensions={0} | all-to-all | bytes 131072 | tf_op jit(solution)/shard_map/all_to_all | solution.py:465
  124.2 0.5 second.1
  124.8 12.2 %all_to_all.44 = f32[32,9,128]{2,1,0:T(8,128)S(1)} all-to-all(f32[32,9,128]{2,1,0:T(8,128)S(1)} %second.1), channel_id=1, replica_groups=mesh['kp'=32,'ka'=16] {'kp'}, dimensions={0} | all-to-all | bytes 294912 | tf_op jit(solution)/shard_map/all_to_all | solution.py:486
  137.0 12.4 %all_to_all.45.refs_0_ = f32[32,9,128]{2,1,0:T(8,128)S(1)} all-to-all(f32[32,9,128]{2,1,0:T(8,128)S(1)} %broadcast_in_dim.11), channel_id=1, replica_groups=mesh['kp'=32,'ka'=16] {'kp'}, dimensions={0} | all-to-all | bytes 294912 | tf_op jit(solution)/shard_map/all_to_all | solution.py:465
  149.5 2.9 %middle.1 = (f32[256,128]{1,0:T(8,128)S(1)}, bf16[16,40,128]{2,1,0:T(8,128)(2,1)S(1)}) custom-call(f32[32,9,128]{2,1,0:T(8,128)S(1)} %all_to_all.45.refs_0_), custom_call_target="tpu_custom_call" | custom-call | tf_op jit(solution)/shard_map/middle/pallas_call | solution.py:431
  152.4 17.9 %all_to_all.46.refs_1_ = bf16[16,40,128]{2,1,0:T(8,128)(2,1)S(1)} all-to-all(bf16[16,40,128]{2,1,0:T(8,128)(2,1)S(1)} %get-tuple-element.17), channel_id=1, replica_groups=mesh['kp'=32,'ka'=16] {'ka'}, dimensions={0} | all-to-all | bytes 327680 | tf_op jit(solution)/shard_map/all_to_all | solution.py:491
  170.2 3.0 %last.1 = f32[64,512]{1,0:T(8,128)} custom-call(f32[256,128]{1,0:T(8,128)S(1)} %get-tuple-element.16.refs_0_, bf16[16,40,128]{2,1,0:T(8,128)(2,1)S(1)} %all_to_all.46.refs_1_), custom_call_target="tpu_custom_call" | custom-call | tf_op jit(solution)/shard_map/last/pallas_call | solution.py:453
  (7 shorter events, 0.1 us)
Async XLA Ops:
  51.8 7.7 %copy-start.1 = (bf16[4,24,2048]{2,1,0:T(8,128)(2,1)S(1)}, bf16[4,24,2048]{2,1,0:T(8,128)(2,1)}, u32[]{:S(2)}) copy-start(bf16[4,24,2048]{2,1,0:T(8,128)(2,1)} %near_ref.1) | copy-start | bytes 1179652
  51.8 26.6 %all-to-all-start.2 = ((bf16[32,168,128]{2,1,0:T(8,128)(2,1)}), bf16[32,168,128]{2,1,0:T(8,128)(2,1)S(1)}, u32[]{:S(2)}, u32[]{:S(2)}) async-start(bf16[32,168,128]{2,1,0:T(8,128)(2,1)} %pick.1), calls=%async_computation.2 | async-start | bytes 2752512 | tf_op jit(solution)/shard_map/all_to_all | solution.py:478
  59.6 2.4 %copy-start.4 = (s32[64,2048]{1,0:T(8,128)S(1)}, s32[64,2048]{1,0:T(8,128)}, u32[]{:S(2)}) copy-start(s32[64,2048]{1,0:T(8,128)} %param.12) | copy-start | bytes 1572868
  59.6 18.8 %copy-start.2 = (bf16[4,128,128]{2,1,0:T(8,128)(2,1)S(1)}, bf16[4,128,128]{2,1,0:T(8,128)(2,1)}, u32[]{:S(2)}) copy-start(bf16[4,128,128]{2,1,0:T(8,128)(2,1)} %coef_ref.1) | copy-start | bytes 393220
  59.6 18.8 %copy-start.3 = (f32[2048]{0:T(1024)S(1)}, f32[2048]{0:T(1024)}, u32[]{:S(2)}) copy-start(f32[2048]{0:T(1024)} %param.11) | copy-start | bytes 24580
  60.0 1.9 %copy-start = (bf16[4,16,16,2048]{3,2,1,0:T(8,128)(2,1)}, bf16[4,16,16,2048]{3,2,1,0:T(8,128)(2,1)S(1)}, u32[]{:S(2)}) copy-start(bf16[4,16,16,2048]{3,2,1,0:T(8,128)(2,1)S(1)} %prepare.1.wide_hbm) | copy-start | bytes 12582916

commit v9 on v7

--- a/solution.py
+++ b/solution.py
@@ -103,7 +103,7 @@
             rolled[s, h] = pltpu.roll(x, 32 * s, 1).astype(BF)
         return 0
 
-    lax.fori_loop(0, 16, roll_one, 0, unroll=4)
+    lax.fori_loop(0, 16, roll_one, 0, unroll=8)
     lane_block = lax.broadcasted_iota(jnp.int32, (64, 128), 1) // 32
 
     def dest(d, _):
@@ -121,7 +121,7 @@
         o_ref[d, 160:168, :] = g_ref[plane, 128:136, :]
         return 0
 
-    lax.fori_loop(0, 32, dest, 0, unroll=4)
+    lax.fori_loop(0, 32, dest, 0, unroll=8)
 
 
 def pick(gathered, table):

time: 169 us -> 169 us (level)
  no operation moved by 1% of the time
where the time goes in v9:
time: 169 us; the launch traced here: 166 us
  blocking collectives  114 us (67%)
  Pallas kernels  25.2 us (15%)
  waiting for transfers between devices  16.3 us (10%)
  starting transfers between devices  7.74 us (5%)
  local copies, waits for them, and re-layouts  2.08 us (1%)
    all_gather x1, blocking collectives, on_device(): gathered = lax.all_gather(piece, 'ka', axis=0, tiled=False)  38.7 us
    all_to_all x2, blocking collectives, to_all(): lax.all_to_all(jnp.broadcast_to(x[None], (size, *x.shape)), axis, 0, 0, t...  31.9 us
    all_to_all x1, blocking collectives, on_device(): lax.all_to_all(corr, 'ka', 0, 0, tiled=True)  17.9 us
    all_to_all x1, waiting for transfers between devices, on_device(): lax.all_to_all(pick(vmem(gathered), table), 'kp', 0, 0, tiled=True)  16.3 us
    pallas_call x1, Pallas kernels, pair_blocks(): pl.pallas_call(pair_kernel, in_specs=[SM, VM, VM, pl.BlockSpec(memory_spa...  14.2 us
    all_to_all x1, blocking collectives, on_device(): sent = lax.all_to_all(sent, 'kp', 0, 0, tiled=True)  13.5 us
    all_to_all x1, blocking collectives, on_device(): lax.all_to_all(second_product(vmem(sent), vmem(to_all(image, 'ka'))), 'kp...  12.2 us
    all_to_all x1, starting transfers between devices, on_device(): lax.all_to_all(pick(vmem(gathered), table), 'kp', 0, 0, tiled=True)  7.74 us
  transfers between devices with their start and end apart: 1, of which 1 were waited for; matrix products, arithmetic and copies ran while one was open for 0% of the time, Pallas kernels for 0%

profile of v9, /device:TPU:6, one launch (start us, length us, event | category | flops | bytes accessed | tf_op | source)
XLA Modules:
  0.0 166.4 jit_solution(4300760405572599555)
XLA Ops:
  0.6 1.2 share.1
  1.8 38.7 %all-gather = bf16[2176,128]{1,0:T(8,128)(2,1)S(1)} all-gather(bf16[136,128]{1,0:T(8,128)(2,1)S(1)} %get-tuple-element.11), channel_id=2, replica_groups=mesh['kp'=32,'ka'=16] {'ka'}, dimensions={0}, use_global_device_ids=true | all-gather | bytes 591872 | tf_op jit(solution)/shard_map/all_gather | solution.py:466
  40.5 3.0 %pick.1 = bf16[32,168,128]{2,1,0:T(8,128)(2,1)} custom-call(s32[4,64]{1,0:T(4,128)S(1)} %get-tuple-element.10.t_ref, bf16[16,136,128]{2,1,0:T(8,128)(2,1)S(1)} %bitcast.11), custom_call_target="tpu_custom_call" | custom-call | tf_op jit(solution)/shard_map/pick/pallas_call | solution.py:128
  43.5 0.0 copy-start.1
  43.5 7.7 %all-to-all-start = ((bf16[32,168,128]{2,1,0:T(8,128)(2,1)}), bf16[32,168,128]{2,1,0:T(8,128)(2,1)S(1)}, u32[]{:S(2)}, u32[]{:S(2)}) async-start(bf16[32,168,128]{2,1,0:T(8,128)(2,1)} %pick.1), calls=%async_computation | async-start | bytes 2752512 | tf_op jit(solution)/shard_map/all_to_all | solution.py:467
  51.3 0.0 copy-done.1
  51.3 0.0 copy-start.4
  51.3 0.0 copy-start.2
  51.3 0.0 copy-start.3
  51.3 0.4 prepare.1.wide_hbm
  51.7 0.0 copy-start
  51.7 1.9 %copy-done = bf16[4,16,16,2048]{3,2,1,0:T(8,128)(2,1)} copy-done((bf16[4,16,16,2048]{3,2,1,0:T(8,128)(2,1)}, bf16[4,16,16,2048]{3,2,1,0:T(8,128)(2,1)S(1)}, u32[]{:S(2)}) %copy-start) | copy-done | bytes 4194328
  53.6 0.0 copy-done.4
  53.6 0.1 copy.10
  53.7 16.3 %all-to-all-done.r_ref = bf16[32,168,128]{2,1,0:T(8,128)(2,1)S(1)} async-done(((bf16[32,168,128]{2,1,0:T(8,128)(2,1)}), bf16[32,168,128]{2,1,0:T(8,128)(2,1)S(1)}, u32[]{:S(2)}, u32[]{:S(2)}) %all-to-all-start) | async-done | bytes 1376288 | tf_op jit(solution)/shard_map/all_to_all | solution.py:467
  70.1 0.0 copy-done.2
  70.1 0.0 copy-done.3
  70.1 14.2 %pairs.1 = (bf16[512,256]{1,0:T(8,128)(2,1)}, bf16[32,48,128]{2,1,0:T(8,128)(2,1)S(1)}) custom-call(s32[4,64]{1,0:T(4,128)S(1)} %get-tuple-element.10.t_ref, bf16[32,168,128]{2,1,0:T(8,128)(2,1)S(1)} %all-to-all-done.r_ref, bf16[4,24,2048]{2,1,0:T(8,128)(2,1)S(1)} %copy-done.1, bf16[4,16,16,2048]{3,2,1,0:T(8,128)(2,1)} %copy-done, ...), custom_call_target="tpu_custom_call" | custom-call | tf_op jit(solution)/shard_map/pairs/pallas_call | solution.py:281
  84.3 13.5 %all_to_all.30.r_ref = bf16[32,48,128]{2,1,0:T(8,128)(2,1)S(1)} all-to-all(bf16[32,48,128]{2,1,0:T(8,128)(2,1)S(1)} %get-tuple-element.13), channel_id=1, replica_groups=mesh['kp'=32,'ka'=16] {'kp'}, dimensions={0} | all-to-all | bytes 786432 | tf_op jit(solution)/shard_map/all_to_all | solution.py:472
  97.8 0.1 convert_reduce_fusion
  97.9 19.5 %all_to_all.31.x_ref = f32[16,8,128]{2,1,0:T(8,128)S(1)} all-to-all(f32[16,8,128]{2,1,0:T(8,128)S(1)} %broadcast_in_dim.4), channel_id=1, replica_groups=mesh['kp'=32,'ka'=16] {'ka'}, dimensions={0} | all-to-all | bytes 131072 | tf_op jit(solution)/shard_map/all_to_all | solution.py:461
  117.4 0.5 second.1
  117.9 12.2 %all_to_all.32 = f32[32,9,128]{2,1,0:T(8,128)S(1)} all-to-all(f32[32,9,128]{2,1,0:T(8,128)S(1)} %second.1), channel_id=1, replica_groups=mesh['kp'=32,'ka'=16] {'kp'}, dimensions={0} | all-to-all | bytes 294912 | tf_op jit(solution)/shard_map/all_to_all | solution.py:475
  130.2 12.4 %all_to_all.33.refs_0_ = f32[32,9,128]{2,1,0:T(8,128)S(1)} all-to-all(f32[32,9,128]{2,1,0:T(8,128)S(1)} %broadcast_in_dim.5), channel_id=1, replica_groups=mesh['kp'=32,'ka'=16] {'kp'}, dimensions={0} | all-to-all | bytes 294912 | tf_op jit(solution)/shard_map/all_to_all | solution.py:461
  142.6 2.9 %middle.1 = (f32[256,128]{1,0:T(8,128)S(1)}, bf16[16,40,128]{2,1,0:T(8,128)(2,1)S(1)}) custom-call(f32[32,9,128]{2,1,0:T(8,128)S(1)} %all_to_all.33.refs_0_), custom_call_target="tpu_custom_call" | custom-call | tf_op jit(solution)/shard_map/middle/pallas_call | solution.py:427
  145.5 17.9 %all_to_all.34.refs_1_ = bf16[16,40,128]{2,1,0:T(8,128)(2,1)S(1)} all-to-all(bf16[16,40,128]{2,1,0:T(8,128)(2,1)S(1)} %get-tuple-element.17), channel_id=1, replica_groups=mesh['kp'=32,'ka'=16] {'ka'}, dimensions={0} | all-to-all | bytes 327680 | tf_op jit(solution)/shard_map/all_to_all | solution.py:480
  163.4 3.0 %last.1 = f32[64,512]{1,0:T(8,128)} custom-call(f32[256,128]{1,0:T(8,128)S(1)} %get-tuple-element.16.refs_0_, bf16[16,40,128]{2,1,0:T(8,128)(2,1)S(1)} %all_to_all.34.refs_1_), custom_call_target="tpu_custom_call" | custom-call | tf_op jit(solution)/shard_map/last/pallas_call | solution.py:449
  (6 shorter events, 0.1 us)
Async XLA Ops:
  43.5 7.8 %copy-start.1 = (bf16[4,24,2048]{2,1,0:T(8,128)(2,1)S(1)}, bf16[4,24,2048]{2,1,0:T(8,128)(2,1)}, u32[]{:S(2)}) copy-start(bf16[4,24,2048]{2,1,0:T(8,128)(2,1)} %near_ref.1) | copy-start | bytes 1179652
  43.5 26.6 %all-to-all-start = ((bf16[32,168,128]{2,1,0:T(8,128)(2,1)}), bf16[32,168,128]{2,1,0:T(8,128)(2,1)S(1)}, u32[]{:S(2)}, u32[]{:S(2)}) async-start(bf16[32,168,128]{2,1,0:T(8,128)(2,1)} %pick.1), calls=%async_computation | async-start | bytes 2752512 | tf_op jit(solution)/shard_map/all_to_all | solution.py:467
  51.3 2.4 %copy-start.4 = (s32[64,2048]{1,0:T(8,128)S(1)}, s32[64,2048]{1,0:T(8,128)}, u32[]{:S(2)}) copy-start(s32[64,2048]{1,0:T(8,128)} %param.12) | copy-start | bytes 1572868
  51.3 18.8 %copy-start.2 = (bf16[4,128,128]{2,1,0:T(8,128)(2,1)S(1)}, bf16[4,128,128]{2,1,0:T(8,128)(2,1)}, u32[]{:S(2)}) copy-start(bf16[4,128,128]{2,1,0:T(8,128)(2,1)} %coef_ref.1) | copy-start | bytes 393220
  51.3 18.8 %copy-start.3 = (f32[2048]{0:T(1024)S(1)}, f32[2048]{0:T(1024)}, u32[]{:S(2)}) copy-start(f32[2048]{0:T(1024)} %param.11) | copy-start | bytes 24580
  51.7 1.9 %copy-start = (bf16[4,16,16,2048]{3,2,1,0:T(8,128)(2,1)}, bf16[4,16,16,2048]{3,2,1,0:T(8,128)(2,1)S(1)}, u32[]{:S(2)}) copy-start(bf16[4,16,16,2048]{3,2,1,0:T(8,128)(2,1)S(1)} %prepare.1.wide_hbm) | copy-start | bytes 12582916
